TPU v7x, 768 devices: a whole 4x8x12 slice. The times are simulated.
768 devices in a mesh: blk: 96 (over z_lo, y, x), grp: 8 (over z_hi, core).
Axes of the slice: x: 4, y: 8, z: 12 (z_hi: 4, z_lo: 3; z = z_hi * 3 + z_lo), core: 2. Of those that a mesh axis runs over, the one named last changes fastest.
Arguments:
- latent: bfloat16 [393216, 128], P(('blk', 'grp')), may hold values from -6 to 6
- positions: float32 [3, 393216], P(None, ('blk', 'grp')), may hold values from -6 to 6
- tile_send: int32 [96, 8, 16], P('blk', 'grp'), may hold values from 0 to 31, as said below
- tile_recv: int32 [96, 8, 16], P('blk', 'grp'), may hold values from 0 to 11
- tile_mask: int32 [96, 8, 16, 128, 128], P('blk', 'grp'), may hold values 0 or 1
- tile_count: int32 [96, 8], P('blk', 'grp'), may hold values from 1 to 16
- w_send: bfloat16 [128, 128], replicated, may hold values from -0.5 to 0.5
- w_recv: bfloat16 [128, 128], replicated, may hold values from -0.5 to 0.5
- pos_weight: float32 [3, 128], replicated, may hold values from -3.5 to 3.5
- edge_bias: float32 [128], replicated, may hold values from -3 to 3
- w_edge_out: bfloat16 [128, 128], replicated, may hold values from -0.125 to 0.125
- w_node_self: bfloat16 [128, 128], replicated, may hold values from -0.375 to 0.375
- w_node_msg: bfloat16 [128, 128], replicated, may hold values from -0.375 to 0.375
- node_bias: float32 [128], replicated, may hold values from -3 to 3
- w_node_out: bfloat16 [128, 128], replicated, may hold values from -0.5 to 0.5
- gain: float32 [128], replicated, may hold values from 0.5 to 1.5
- cotangent: bfloat16 [393216, 128], P(('blk', 'grp')), may hold values from -6 to 6
Outputs:
- new_latent: bfloat16 [393216, 128], P(('blk', 'grp'))
- latent_grad: float32 [393216, 128], P(('blk', 'grp'))
- weight_grads: float32 [6, 128, 128], replicated
Inputs may be any that keep to these rules, and one draw needn't show every extreme that they name: `tile_send`: the sender block of every tile lies in the same slab; tile 0 of member g names a block of member (g + 4) mod 8.
All inputs are finite; a program needn't handle non-finite values. No bound on the sum of `tile_mask` on one device may be relied on, other than what follows from the above.
Results may differ from a plain program's by a relative error of at most 0.012.
Values may be sent and summed in bfloat16 or wider, within the bound.
A program may use at most 32 MiB of HBM per device.

v0:
```python
import jax
import jax.numpy as jnp
from jax import lax
from jax.sharding import PartitionSpec as P


def shifted(value, axis, steps):
    count = lax.axis_size(axis)
    pairs = [(source, (source + steps) % count) for source in range(count)]
    return lax.ppermute(value, axis, pairs)


def contract_rows(left_rows, right_rows):
    return lax.dot_general(
        left_rows, right_rows, (((0,), (0,)), ((), ())), preferred_element_type=jnp.float32
    )


def edge_forward(send_block, recv_block, edge_mask):
    size_rows = recv_block.shape[0]
    width = recv_block.shape[1]
    group_rows = min(32, size_rows)
    group_count = size_rows // group_rows
    sender_values = send_block.astype(jnp.float32)

    def one_group(pieces):
        recv_part, mask_part = pieces
        preact = recv_part.astype(jnp.float32)[:, None, :] + sender_values[None, :, :]
        summed = jnp.sum(mask_part[:, :, None] * jnp.maximum(preact, 0.0), axis=1)
        return (summed,)

    results = lax.map(
        one_group,
        (
            recv_block.reshape(group_count, group_rows, width),
            edge_mask.reshape(group_count, group_rows, size_rows),
        ),
    )
    return tuple((item.reshape(size_rows, width) for item in results))


def edge_backward(send_block, recv_block, edge_mask, grad_block):
    size_rows = recv_block.shape[0]
    width = recv_block.shape[1]
    group_rows = min(32, size_rows)
    group_count = size_rows // group_rows
    sender_values = send_block.astype(jnp.float32)

    def one_group(running, pieces):
        recv_part, mask_part, grad_part = pieces
        preact = recv_part.astype(jnp.float32)[:, None, :] + sender_values[None, :, :]
        terms = mask_part[:, :, None] * (preact > 0.0).astype(jnp.float32) * grad_part[:, None, :]
        running = running + jnp.sum(terms, axis=0)
        return (running, jnp.sum(terms, axis=1))

    pieces = (
        recv_block.reshape(group_count, group_rows, width),
        edge_mask.reshape(group_count, group_rows, size_rows),
        grad_block.reshape(group_count, group_rows, width),
    )
    send_grad, recv_grad = lax.scan(one_group, jnp.zeros((size_rows, width), jnp.float32), pieces)
    recv_grad = recv_grad.reshape(size_rows, width)
    return (send_grad, recv_grad)


def node_update(
    latent, aggregate, cotangent, w_edge_out, w_node_self, w_node_msg, node_bias, w_node_out, gain
):
    aggregate_b = aggregate.astype(jnp.bfloat16)
    message = jnp.dot(aggregate_b, w_edge_out, preferred_element_type=jnp.float32).astype(
        jnp.bfloat16
    )
    hidden_pre = (
        jnp.dot(latent, w_node_self, preferred_element_type=jnp.float32)
        + jnp.dot(message, w_node_msg, preferred_element_type=jnp.float32)
        + node_bias
    )
    logistic = jax.nn.sigmoid(hidden_pre)
    hidden = (hidden_pre * logistic).astype(jnp.bfloat16)
    update = jnp.dot(hidden, w_node_out, preferred_element_type=jnp.float32)
    average = jnp.mean(update, axis=-1, keepdims=True)
    centred = update - average
    variance = jnp.mean(centred * centred, axis=-1, keepdims=True)
    inv_std = lax.rsqrt(variance + 1e-05)
    normed = centred * inv_std
    new_latent = (latent.astype(jnp.float32) + normed * gain).astype(jnp.bfloat16)
    cot_float = cotangent.astype(jnp.float32)
    d_normed = cot_float * gain
    d_update = (
        inv_std
        * (
            d_normed
            - jnp.mean(d_normed, axis=-1, keepdims=True)
            - normed * jnp.mean(d_normed * normed, axis=-1, keepdims=True)
        )
    ).astype(jnp.bfloat16)
    d_hidden = jnp.dot(d_update, w_node_out.T, preferred_element_type=jnp.float32)
    d_hidden_pre = (d_hidden * logistic * (1.0 + hidden_pre * (1.0 - logistic))).astype(
        jnp.bfloat16
    )
    d_message = jnp.dot(d_hidden_pre, w_node_msg.T, preferred_element_type=jnp.float32).astype(
        jnp.bfloat16
    )
    d_aggregate = jnp.dot(d_message, w_edge_out.T, preferred_element_type=jnp.float32)
    direct = cot_float + jnp.dot(d_hidden_pre, w_node_self.T, preferred_element_type=jnp.float32)
    grad_list = [
        contract_rows(aggregate_b, d_message),
        contract_rows(latent, d_hidden_pre),
        contract_rows(message, d_hidden_pre),
        contract_rows(hidden, d_update),
    ]
    return (new_latent, d_aggregate, d_message, direct, grad_list)


def from_slab(values, offset):
    return shifted(values, "blk", offset)


def to_slab(values, offset):
    return shifted(values, "blk", offset)


def add_rows(buffer, start, size_rows, added_rows):
    current = lax.dynamic_slice_in_dim(buffer, start, size_rows, 0)
    return lax.dynamic_update_slice_in_dim(buffer, current + added_rows, start, 0)


def body(
    latent,
    positions,
    tile_send,
    tile_recv,
    tile_mask,
    tile_count,
    w_send,
    w_recv,
    pos_weight,
    edge_bias,
    w_edge_out,
    w_node_self,
    w_node_msg,
    node_bias,
    w_node_out,
    gain,
    cotangent,
):
    own_rows = latent.shape[0]
    width = latent.shape[1]
    block_size = tile_mask.shape[-1]
    tiles_here = tile_mask.shape[2]
    placed = lax.dot_general(
        positions,
        pos_weight,
        (((0,), (0,)), ((), ())),
        precision=lax.Precision.HIGHEST,
        preferred_element_type=jnp.float32,
    )
    send_rows = (jnp.dot(latent, w_send, preferred_element_type=jnp.float32) + placed).astype(
        jnp.bfloat16
    )
    recv_rows = (
        jnp.dot(latent, w_recv, preferred_element_type=jnp.float32) - placed + edge_bias
    ).astype(jnp.bfloat16)
    senders = lax.all_gather(send_rows, "grp", axis=0, tiled=True)
    receivers = jnp.concatenate([from_slab(recv_rows, 1), recv_rows, from_slab(recv_rows, -1)], 0)
    send_table = tile_send[0, 0]
    recv_table = tile_recv[0, 0]
    mask_table = tile_mask[0, 0]
    live_count = tile_count[0, 0]

    def locate(tile_step):
        send_start = send_table[tile_step] * block_size
        recv_start = recv_table[tile_step] * block_size
        tile_alive = (tile_step < live_count).astype(jnp.float32)
        edge_mask = mask_table[tile_step].astype(jnp.float32) * tile_alive
        send_block = lax.dynamic_slice_in_dim(senders, send_start, block_size, 0)
        recv_block = lax.dynamic_slice_in_dim(receivers, recv_start, block_size, 0)
        return (send_start, recv_start, send_block, recv_block, edge_mask)

    window = jnp.zeros((3 * own_rows, width), jnp.float32)

    def forward_tile(tile_step, running):
        send_start, recv_start, send_block, recv_block, edge_mask = locate(tile_step)
        results = edge_forward(send_block, recv_block, edge_mask)
        return tuple(
            (
                add_rows(buffer, recv_start, block_size, added)
                for buffer, added in zip(running, results)
            )
        )

    start_state = (window,)
    sums = lax.fori_loop(0, tiles_here, forward_tile, start_state)
    partial_value = sums[0]
    aggregate = (
        partial_value[own_rows : 2 * own_rows]
        + to_slab(partial_value[:own_rows], -1)
        + to_slab(partial_value[2 * own_rows :], 1)
    )
    new_latent, d_aggregate, d_message, direct, grad_list = node_update(
        latent,
        aggregate,
        cotangent,
        w_edge_out,
        w_node_self,
        w_node_msg,
        node_bias,
        w_node_out,
        gain,
    )
    grad_window = jnp.concatenate(
        [to_slab(d_aggregate, 1), d_aggregate, to_slab(d_aggregate, -1)], 0
    )

    def backward_tile(tile_step, running):
        send_start, recv_start, send_block, recv_block, edge_mask = locate(tile_step)
        grad_block = lax.dynamic_slice_in_dim(grad_window, recv_start, block_size, 0)
        send_part, recv_part = edge_backward(send_block, recv_block, edge_mask, grad_block)
        send_buffer = add_rows(running[0], send_start, block_size, send_part)
        return (send_buffer, add_rows(running[1], recv_start, block_size, recv_part))

    send_zero = jnp.zeros(senders.shape, jnp.float32)
    back_state = (send_zero, window)
    grads_out = lax.fori_loop(0, tiles_here, backward_tile, back_state)
    send_grad = lax.psum_scatter(
        grads_out[0].astype(jnp.bfloat16), "grp", scatter_dimension=0, tiled=True
    )
    recv_window = grads_out[1]
    recv_grad = (
        recv_window[own_rows : 2 * own_rows]
        + to_slab(recv_window[:own_rows], -1)
        + to_slab(recv_window[2 * own_rows :], 1)
    )
    recv_bf = recv_grad.astype(jnp.bfloat16)
    latent_grad = (
        direct
        + jnp.dot(send_grad, w_send.T, preferred_element_type=jnp.float32)
        + jnp.dot(recv_bf, w_recv.T, preferred_element_type=jnp.float32)
    )
    local_grads = jnp.stack(
        [contract_rows(latent, send_grad), contract_rows(latent, recv_bf)] + grad_list
    )
    weight_grads = lax.psum(local_grads, ("blk", "grp"))
    return (new_latent, latent_grad, weight_grads)


def solution(mesh):
    in_specs = (
        P(("blk", "grp"), None),
        P(None, ("blk", "grp")),
        P("blk", "grp", None),
        P("blk", "grp", None),
        P("blk", "grp", None, None, None),
        P("blk", "grp"),
        P(),
        P(),
        P(),
        P(),
        P(),
        P(),
        P(),
        P(),
        P(),
        P(),
        P(("blk", "grp"), None),
    )
    out_specs = (P(("blk", "grp"), None), P(("blk", "grp"), None), P())
    return jax.shard_map(body, mesh=mesh, in_specs=in_specs, out_specs=out_specs, check_vma=False)
```

profile of v0, /device:TPU:1, one launch (start us, length us, event | category | flops | bytes accessed | tf_op | source)
XLA Modules:
  0.0 970.4 jit_solution(6638560213508016409)
XLA Ops:
  7.2 1.3 fusion.26
  8.5 1.7 fusion.6
  10.4 1.1 fusion.5
  11.5 3.9 collective-permute-start
  15.4 9.7 %collective-permute-start.1 = (bf16[512,128]{1,0:T(8,128)(2,1)S(1)}, bf16[512,128]{1,0:T(8,128)(2,1)S(1)}, u32[]{:S(2)}, u32[]{:S(2)}) collective-permute-start(bf16[512,128]{1,0:T(8,128)(2,1)S(1)} %fusion.5), channel_id=1, source_target_pairs={{0,760},{8,0},{16,8},{24,16},{32,24},{40,32},{48,40},{56,48},{64,5... | collective-permute-start | bytes 393224 | tf_op jit(solution)/shard_map/ppermute | solution.py:10
  25.6 1.5 collective-permute-done.1
  27.1 33.2 %all-gather.2.cloned.1.call-done = bf16[4096,128]{1,0:T(8,128)(2,1)} async-done(((bf16[512,128]{1,0:T(8,128)(2,1)}), bf16[4096,128]{1,0:T(8,128)(2,1)}) %all-gather.2.cloned.1.call-update) | async-done | bytes 1048592 | tf_op jit(solution)/shard_map/all_gather | solution.py:164
  60.4 127.0 %while.80 = (s32[]{:T(128)}, f32[1536,128]{1,0:T(8,128)S(1)}, s32[16]{0:T(128)S(1)}, bf16[1536,128]{1,0:T(8,128)(2,1)S(1)}, s32[16,128,128]{2,1,0:T(8,128)}, /*i...) while((s32[]{:T(128)}, f32[1536,128]{1,0:T(8,128)S(1)}, ...), condition=%wide.region_4.5_spmd, body=%wide.region_0.4_spmd.sunk | while | flops 2162702 | bytes 696740 | solution.py:193
  65.2 3.1 while.83
  73.1 3.1 while.83
  81.1 3.1 while.83
  89.0 3.1 while.83
  96.9 3.1 while.83
  104.9 3.1 while.83
  112.8 3.1 while.83
  120.7 3.1 while.83
  128.7 3.1 while.83
  136.6 3.1 while.83
  144.6 3.1 while.83
  152.5 3.1 while.83
  160.4 3.1 while.83
  168.4 3.1 while.83
  176.3 3.1 while.83
  184.2 3.1 while.83
  187.5 7.7 collective-permute-start.2
  195.2 1.9 collective-permute-start.3
  197.6 3.0 collective-permute-done.2
  200.6 8.9 collective-permute-done.3
  213.2 1.9 collective-permute-start.4
  215.1 8.5 collective-permute-start.5
  223.6 3.0 collective-permute-done.4
  226.6 0.9 collective-permute-done.5
  227.5 1.0 pad_maximum_fusion
  228.6 210.6 %while.82 = (s32[]{:T(128)}, f32[4096,128]{1,0:T(8,128)S(1)}, f32[1536,128]{1,0:T(8,128)S(1)}, s32[16]{0:T(128)S(1)}, s32[16]{0:T(128)S(1)}, /*index=5*/bf16[153...) while((s32[]{:T(128)}, f32[4096,128]{1,0:T(8,128)S(1)}, ...), condition=%wide.region_14.15_spmd, body=%wide.region_9.14_spmd.sunk | while | flops 3244047 | bytes 1336314 | solution.py:224
  235.2 5.7 while.84
  248.4 5.7 while.84
  261.6 5.7 while.84
  267.2 0.9 add_dynamic-update-slice_fusion.2
  274.7 5.7 while.84
  287.9 5.7 while.84
  301.0 5.7 while.84
  306.7 0.9 add_dynamic-update-slice_fusion.2
  314.2 5.7 while.84
  319.9 0.9 add_dynamic-update-slice_fusion.2
  327.4 5.7 while.84
  340.5 5.7 while.84
  353.7 5.7 while.84
  359.4 0.9 add_dynamic-update-slice_fusion.2
  366.9 5.7 while.84
  372.5 0.9 add_dynamic-update-slice_fusion.2
  380.0 5.7 while.84
  393.2 5.7 while.84
  406.3 5.7 while.84
  419.5 5.7 while.84
  432.7 5.7 while.84
  439.2 1.1 convert_element_type.117
  440.5 9.4 collective-permute-start.6
  449.8 1.9 collective-permute-start.7
  453.1 8.9 collective-permute-done.7
  462.1 26.0 %reduce-scatter.2.cloned.1.call-done = bf16[512,128]{1,0:T(8,128)(2,1)} async-done(((bf16[4096,128]{1,0:T(8,128)(2,1)}), bf16[512,128]{1,0:T(8,128)(2,1)}) %reduce-scatter.2.cloned.1.call-update) | async-done | bytes 131088 | tf_op jit(solution)/shard_map/reduce_scatter | solution.py:225
  488.2 1.2 fusion.13
  490.3 1.1 fusion.8
  493.5 468.4 %all-reduce.2.cloned.1.call-done = f32[6,128,128]{1,2,0:T(8,128)} async-done(((f32[6,128,128]{1,2,0:T(8,128)}), f32[6,128,128]{1,2,0:T(8,128)}) %all-reduce.2.cloned.1.call-update) | async-done | bytes 393232 | tf_op jit(solution)/shard_map/psum | solution.py:243
  961.9 1.9 copy.41
  (907 shorter events, 271.8 us)
Async XLA Ops:
  7.2 203.2 %copy-start = (bf16[128,128]{1,0:T(8,128)(2,1)S(1)}, bf16[128,128]{1,0:T(8,128)(2,1)}, u32[]{:S(2)}) copy-start(bf16[128,128]{1,0:T(8,128)(2,1)} %param.39) | copy-start | bytes 98308
  7.2 53.2 %copy-start.26 = (s32[1,1,16]{2,1,0:T(1,128)S(1)}, s32[1,1,16]{2,1,0:T(1,128)}, u32[]{:S(2)}) copy-start(s32[1,1,16]{2,1,0:T(1,128)} %param.28) | copy-start | bytes 196
  7.2 53.2 %copy-start.27 = (s32[1,1,16]{2,1,0:T(1,128)S(1)}, s32[1,1,16]{2,1,0:T(1,128)}, u32[]{:S(2)}) copy-start(s32[1,1,16]{2,1,0:T(1,128)} %param.27) | copy-start | bytes 196
  7.2 53.1 %all-gather.2.cloned.1.call-start = ((), (), s32[]{:S(2)}) async-start(), calls=%async_computation.1 | async-start | bytes 1179648 | tf_op jit(solution)/shard_map/all_gather | solution.py:164
  10.3 477.9 %reduce-scatter.2.cloned.1.call-start = ((), (), s32[]{:S(2)}) async-start(), calls=%async_computation.2 | async-start | bytes 1179648 | tf_op jit(solution)/shard_map/reduce_scatter | solution.py:225
  11.5 14.1 %collective-permute-start = (bf16[512,128]{1,0:T(8,128)(2,1)S(1)}, bf16[512,128]{1,0:T(8,128)(2,1)S(1)}, u32[]{:S(2)}, u32[]{:S(2)}) collective-permute-start(bf16[512,128]{1,0:T(8,128)(2,1)S(1)} %fusion.5), channel_id=1, source_target_pairs={{0,8},{8,16},{16,24},{24,32},{32,40},{40,48},{48,56},{56,64},{64,7... | collective-permute-start | bytes 393224 | tf_op jit(solution)/shard_map/ppermute | solution.py:10
  15.4 11.6 %collective-permute-start.1 = (bf16[512,128]{1,0:T(8,128)(2,1)S(1)}, bf16[512,128]{1,0:T(8,128)(2,1)S(1)}, u32[]{:S(2)}, u32[]{:S(2)}) collective-permute-start(bf16[512,128]{1,0:T(8,128)(2,1)S(1)} %fusion.5), channel_id=1, source_target_pairs={{0,760},{8,0},{16,8},{24,16},{32,24},{40,32},{48,40},{56,48},{64,5... | collective-permute-start | bytes 393224 | tf_op jit(solution)/shard_map/ppermute | solution.py:10
  60.4 136.8 %copy-start.1 = (bf16[512,128]{1,0:T(8,128)(2,1)S(1)}, bf16[512,128]{1,0:T(8,128)(2,1)}, u32[]{:S(2)}) copy-start(bf16[512,128]{1,0:T(8,128)(2,1)} %param.25) | copy-start | bytes 393220
  60.4 136.9 %copy-start.17 = (bf16[512,128]{1,0:T(8,128)(2,1)S(1)}, bf16[512,128]{1,0:T(8,128)(2,1)}, u32[]{:S(2)}) copy-start(bf16[512,128]{1,0:T(8,128)(2,1)} %param.41) | copy-start | bytes 393220
  60.4 137.0 %copy-start.20 = (bf16[128,128]{1,0:T(8,128)(2,1)S(1)}, bf16[128,128]{1,0:T(8,128)(2,1)}, u32[]{:S(2)}) copy-start(bf16[128,128]{1,0:T(8,128)(2,1)} %param.36) | copy-start | bytes 98308
  187.4 23.3 %copy-start.4 = (bf16[1536,128]{1,0:T(8,128)(2,1)}, bf16[1536,128]{1,0:T(8,128)(2,1)S(1)}, u32[]{:S(2)}) copy-start(bf16[1536,128]{1,0:T(8,128)(2,1)S(1)} %get-tuple-element.865) | copy-start | bytes 1179652
  187.4 22.1 %copy-start.19 = (bf16[128,128]{1,0:T(8,128)(2,1)S(1)}, bf16[128,128]{1,0:T(8,128)(2,1)}, u32[]{:S(2)}) copy-start(bf16[128,128]{1,0:T(8,128)(2,1)} %param.35) | copy-start | bytes 98308
  187.4 22.8 %copy-start.16 = (bf16[128,128]{1,0:T(8,128)(2,1)S(1)}, bf16[128,128]{1,0:T(8,128)(2,1)}, u32[]{:S(2)}) copy-start(bf16[128,128]{1,0:T(8,128)(2,1)} %param.37) | copy-start | bytes 98308
  187.4 22.8 %copy-start.25 = (f32[128]{0:T(128)S(1)}, f32[128]{0:T(128)}, u32[]{:S(2)}) copy-start(f32[128]{0:T(128)} %param.38) | copy-start | bytes 1540
  187.5 13.1 %collective-permute-start.2 = (f32[512,128]{1,0:T(8,128)S(1)}, f32[512,128]{1,0:T(8,128)S(1)}, u32[]{:S(2)}, u32[]{:S(2)}) collective-permute-start(f32[512,128]{1,0:T(8,128)S(1)} %get-tuple-element.482), channel_id=1, source_target_pairs={{0,760},{8,0},{16,8},{24,16},{32,24},{40,32},{48,40},{56,48},{64,5... | collective-permute-start | bytes 786440 | tf_op jit(solution)/shard_map/ppermute | solution.py:10
  195.2 15.8 %copy-start.24 = (f32[128]{0:T(128)S(1)}, f32[128]{0:T(128)}, u32[]{:S(2)}) copy-start(f32[128]{0:T(128)} %param.40) | copy-start | bytes 1540
  195.2 14.3 %collective-permute-start.3 = (f32[512,128]{1,0:T(8,128)S(1)}, f32[512,128]{1,0:T(8,128)S(1)}, u32[]{:S(2)}, u32[]{:S(2)}) collective-permute-start(f32[512,128]{1,0:T(8,128)S(1)} %get-tuple-element.483), channel_id=1, source_target_pairs={{0,8},{8,16},{16,24},{24,32},{32,40},{40,48},{48,56},{56,64},{64,7... | collective-permute-start | bytes 786440 | tf_op jit(solution)/shard_map/ppermute | solution.py:10
  197.4 13.7 %copy-start.2 = (bf16[512,128]{0,1:T(8,128)(2,1)}, bf16[512,128]{0,1:T(8,128)(2,1)S(1)}, u32[]{:S(2)}) copy-start(bf16[512,128]{0,1:T(8,128)(2,1)S(1)} %copy.32) | copy-start | bytes 393220
  209.6 0.6 copy-start.5
  210.2 0.7 copy-start.9
  210.4 1.9 copy-start.14
  211.9 1.3 copy-start.18
  212.3 0.6 copy-start.7
  213.2 13.4 %collective-permute-start.4 = (f32[512,128]{1,0:T(8,128)S(1)}, f32[512,128]{1,0:T(8,128)S(1)}, u32[]{:S(2)}, u32[]{:S(2)}) collective-permute-start(f32[512,128]{1,0:T(8,128)S(1)} %fusion.27), channel_id=1, source_target_pairs={{0,8},{8,16},{16,24},{24,32},{32,40},{40,48},{48,56},{56,64},{64,7... | collective-permute-start | bytes 786440 | tf_op jit(solution)/shard_map/ppermute | solution.py:10
  215.1 12.4 %collective-permute-start.5 = (f32[512,128]{1,0:T(8,128)S(1)}, f32[512,128]{1,0:T(8,128)S(1)}, u32[]{:S(2)}, u32[]{:S(2)}) collective-permute-start(f32[512,128]{1,0:T(8,128)S(1)} %fusion.27), channel_id=1, source_target_pairs={{0,760},{8,0},{16,8},{24,16},{32,24},{40,32},{48,40},{56,48},{64,5... | collective-permute-start | bytes 786440 | tf_op jit(solution)/shard_map/ppermute | solution.py:10
  439.2 12.6 %copy-start.12 = (bf16[512,128]{0,1:T(8,128)(2,1)S(1)}, bf16[512,128]{0,1:T(8,128)(2,1)}, u32[]{:S(2)}) copy-start(bf16[512,128]{0,1:T(8,128)(2,1)} %get-tuple-element.485) | copy-start | bytes 393220
  439.2 13.3 %copy-start.3 = (bf16[512,128]{0,1:T(8,128)(2,1)S(1)}, bf16[512,128]{0,1:T(8,128)(2,1)}, u32[]{:S(2)}) copy-start(bf16[512,128]{0,1:T(8,128)(2,1)} %copy-done.2) | copy-start | bytes 393220
  439.2 13.3 %copy-start.21 = (bf16[128,128]{1,0:T(8,128)(2,1)S(1)}, bf16[128,128]{1,0:T(8,128)(2,1)}, u32[]{:S(2)}) copy-start(bf16[128,128]{1,0:T(8,128)(2,1)} %param.36) | copy-start | bytes 98308
  440.3 49.3 %copy-start.6 = (bf16[512,128]{1,0:T(8,128)(2,1)S(1)}, bf16[512,128]{1,0:T(8,128)(2,1)}, u32[]{:S(2)}) copy-start(bf16[512,128]{1,0:T(8,128)(2,1)} %copy-done.5) | copy-start | bytes 393220
  440.3 49.3 %copy-start.8 = (bf16[512,128]{1,0:T(8,128)(2,1)S(1)}, bf16[512,128]{1,0:T(8,128)(2,1)}, u32[]{:S(2)}) copy-start(bf16[512,128]{1,0:T(8,128)(2,1)} %copy-done.7) | copy-start | bytes 393220
  440.4 49.7 %copy-start.10 = (bf16[512,128]{1,0:T(8,128)(2,1)S(1)}, bf16[512,128]{1,0:T(8,128)(2,1)}, u32[]{:S(2)}) copy-start(bf16[512,128]{1,0:T(8,128)(2,1)} %copy-done.9) | copy-start | bytes 393220
  440.4 521.5 %all-reduce.2.cloned.1.call-start = ((), (), s32[]{:S(2)}) async-start(), calls=%async_computation.3 | async-start | bytes 786432 | tf_op jit(solution)/shard_map/psum | solution.py:243
  440.4 49.9 %copy-start.15 = (f32[512,128]{1,0:T(8,128)S(1)}, f32[512,128]{1,0:T(8,128)}, u32[]{:S(2)}) copy-start(f32[512,128]{1,0:T(8,128)} %copy-done.14) | copy-start | bytes 786436
  440.5 12.7 %collective-permute-start.6 = (f32[512,128]{1,0:T(8,128)S(1)}, f32[512,128]{1,0:T(8,128)S(1)}, u32[]{:S(2)}, u32[]{:S(2)}) collective-permute-start(f32[512,128]{1,0:T(8,128)S(1)} %get-tuple-element.480), channel_id=1, source_target_pairs={{0,760},{8,0},{16,8},{24,16},{32,24},{40,32},{48,40},{56,48},{64,5... | collective-permute-start | bytes 786440 | tf_op jit(solution)/shard_map/ppermute | solution.py:10
  449.8 12.2 %collective-permute-start.7 = (f32[512,128]{1,0:T(8,128)S(1)}, f32[512,128]{1,0:T(8,128)S(1)}, u32[]{:S(2)}, u32[]{:S(2)}) collective-permute-start(f32[512,128]{1,0:T(8,128)S(1)} %get-tuple-element.481), channel_id=1, source_target_pairs={{0,8},{8,16},{16,24},{24,32},{32,40},{40,48},{48,56},{56,64},{64,7... | collective-permute-start | bytes 786440 | tf_op jit(solution)/shard_map/ppermute | solution.py:10
  452.7 39.5 %copy-start.22 = (bf16[128,128]{1,0:T(8,128)(2,1)S(1)}, bf16[128,128]{1,0:T(8,128)(2,1)}, u32[]{:S(2)}) copy-start(bf16[128,128]{1,0:T(8,128)(2,1)} %param.31) | copy-start | bytes 98308
  462.1 30.4 %copy-start.23 = (bf16[128,128]{1,0:T(8,128)(2,1)S(1)}, bf16[128,128]{1,0:T(8,128)(2,1)}, u32[]{:S(2)}) copy-start(bf16[128,128]{1,0:T(8,128)(2,1)} %param.32) | copy-start | bytes 98308
  488.2 4.1 copy-start.13
  491.5 0.7 copy-start.11
Sparse Core Ops, SparseCore 0:
  11.1 49.1 all-gather.1
  440.5 47.6 reduce-scatter.1
  494.1 467.7 all-reduce.1
where the time goes:
time: 978 us; the launch traced here: 970 us
  waiting for transfers between devices  555 us (57%)
  other arithmetic  164 us (17%)
  local copies, waits for them, and re-layouts  113 us (12%)
  loops' own time  70.7 us (7%)
  starting transfers between devices  45 us (5%)
  between operations  14.4 us (1%)
    psum x1, waiting for transfers between devices, body(): weight_grads = lax.psum(local_grads, ('blk', 'grp'))  468 us
    reduce_sum x64, other arithmetic, one_group(): return (running, jnp.sum(terms, axis=1))  46.5 us
    reduce_sum x64, other arithmetic, one_group(): summed = jnp.sum(mask_part[:, :, None] * jnp.maximum(preact, 0.0), axis=1)  45.5 us
    ppermute x8, starting transfers between devices, shifted(): return lax.ppermute(value, axis, pairs)  44.9 us
    dynamic_update_slice x128, local copies, waits for them, and re-layouts, edge_forward(): lax.map(one_group, (recv_block.reshape(group_count, group_rows, width), e...  39.5 us
    another operation x1, loops' own time, body(): grads_out = lax.fori_loop(0, tiles_here, backward_tile, back_state)  33.3 us
    all_gather x1, waiting for transfers between devices, body(): senders = lax.all_gather(send_rows, 'grp', axis=0, tiled=True)  33.2 us
    another operation x1, loops' own time, body(): sums = lax.fori_loop(0, tiles_here, forward_tile, start_state)  32 us
  transfers between devices with their start and end apart: 11, of which 11 were waited for; matrix products, arithmetic and copies ran while one was open for 0% of the time, Pallas kernels for 0%

commit v1 on v0

v1 whole, which is shorter than its diff:
```python
import functools

import jax
import jax.numpy as jnp
from jax import lax
from jax.experimental import pallas as pl
from jax.experimental.pallas import tpu as pltpu
from jax.sharding import PartitionSpec as P

F32, BF16 = jnp.float32, jnp.bfloat16
DN0 = (((0,), (0,)), ((), ()))
DN1 = (((1,), (1,)), ((), ()))
MESH = pl.DeviceIdType.MESH
SMEM = pl.BlockSpec(memory_space=pltpu.SMEM)
VM = pl.BlockSpec(memory_space=pltpu.VMEM)
NX, NY, NZ, ZLO, ZHI = 4, 8, 12, 3, 4
SLABS = NX * NY * ZLO
LIMIT = 56 << 20


class Place:
    def __init__(self):
        self.blk = lax.axis_index("blk")
        self.grp = lax.axis_index("grp")
        self.x = self.blk % NX
        self.y = (self.blk // NX) % NY
        self.zl = self.blk // (NX * NY)
        self.core = self.grp % 2
        self.zh = self.grp // 2
        self.z = self.zh * ZLO + self.zl

    def at(self, x=None, y=None, z=None, core=None):
        x = self.x if x is None else x
        y = self.y if y is None else y
        z = self.z if z is None else z
        core = self.core if core is None else core
        return ((z % ZLO) * (NX * NY) + y * NX + x, (z // ZLO) * 2 + core)

    def slab(self, step):
        return ((self.blk + step + SLABS) % SLABS, self.grp)

    def member(self, step):
        return (self.blk, ((self.zh + step + ZHI) % ZHI) * 2 + self.core)

    def partner(self):
        return (self.blk, self.zh * 2 + 1 - self.core)


def meet(peers):
    barrier = pltpu.get_barrier_semaphore()
    for peer in peers:
        pl.semaphore_signal(barrier, inc=1, device_id=peer, device_id_type=MESH)
    pl.semaphore_wait(barrier, len(peers))


class Copies:
    def __init__(self, send_sem, recv_sem):
        self.send_sem, self.recv_sem, self.started = send_sem, recv_sem, []

    def start(self, src, dst, device):
        number = len(self.started)
        copy = pltpu.make_async_remote_copy(
            src_ref=src, dst_ref=dst, send_sem=self.send_sem.at[number],
            recv_sem=self.recv_sem.at[number], device_id=device, device_id_type=MESH)
        copy.start()
        self.started.append(copy)
        return copy

    def sent(self):
        for copy in self.started:
            copy.wait_send()


def sd(shape, dtype):
    return jax.ShapeDtypeStruct(shape, dtype)


def dot(a, b):
    return jnp.dot(a, b, preferred_element_type=F32)


def dot_t(a, b):
    return lax.dot_general(a, b, DN1, preferred_element_type=F32)


def contract(a, b):
    return lax.dot_general(a, b, DN0, preferred_element_type=F32)


GATHER_COPIES = 24


def gather_kernel(lat, pos, lat_all, pos_all, lat_nb, pos_nb, send_sem, recv_sem):
    me = Place()
    own = lat.shape[0]
    g = me.grp
    up, dn, sib = me.member(1), me.member(-1), me.partner()
    nxt, prv = me.slab(1), me.slab(-1)
    meet([up, dn, sib, nxt, prv])
    cs = Copies(send_sem, recv_sem)
    halves = (pl.ds(0, own // 2), pl.ds(own // 2, own // 2))

    def half(index, h):
        return lat_all.at[index, halves[h]]

    up_pos = cs.start(pos, pos_all.at[g], up)
    dn_pos = cs.start(pos, pos_all.at[g], dn)
    up_a = cs.start(lat.at[halves[0]], half(g, 0), up)
    dn_b = cs.start(lat.at[halves[1]], half(g, 1), dn)
    up_b = cs.start(lat.at[halves[1]], half(g, 1), up)
    dn_a = cs.start(lat.at[halves[0]], half(g, 0), dn)
    waits = [
        cs.start(lat, lat_nb.at[0], nxt),
        cs.start(lat, lat_nb.at[1], prv),
        cs.start(pos, pos_nb.at[0], nxt),
        cs.start(pos, pos_nb.at[1], prv),
        cs.start(lat, lat_all.at[g], sib),
        cs.start(pos, pos_all.at[g], sib),
    ]
    lat_all[g] = lat[...]
    pos_all[g] = pos[...]
    iu, idn, far = up[1], dn[1], me.member(2)[1]

    def pass_on(ref):
        waits.append(cs.start(ref, ref, sib))

    up_pos.wait_recv()
    far_pos = cs.start(pos_all.at[idn], pos_all.at[idn], up)
    pass_on(pos_all.at[idn])
    dn_pos.wait_recv()
    pass_on(pos_all.at[iu])
    up_a.wait_recv()
    far_a = cs.start(half(idn, 0), half(idn, 0), up)
    pass_on(half(idn, 0))
    dn_b.wait_recv()
    far_b = cs.start(half(iu, 1), half(iu, 1), dn)
    pass_on(half(iu, 1))
    up_b.wait_recv()
    pass_on(half(idn, 1))
    dn_a.wait_recv()
    pass_on(half(iu, 0))
    far_pos.wait_recv()
    pass_on(pos_all.at[far])
    far_a.wait_recv()
    pass_on(half(far, 0))
    far_b.wait_recv()
    pass_on(half(far, 1))
    for copy in waits:
        copy.wait_recv()
    cs.sent()


def gather(lat, pos):
    own = lat.shape[0]
    n = GATHER_COPIES
    return pl.pallas_call(
        gather_kernel,
        out_shape=[sd((8, own, 128), BF16), sd((8, 3, own), F32), sd((2, own, 128), BF16),
                   sd((2, 3, own), F32)],
        in_specs=[VM] * 2,
        out_specs=[VM] * 4,
        scratch_shapes=[pltpu.SemaphoreType.DMA((n,)), pltpu.SemaphoreType.DMA((n,))],
        compiler_params=pltpu.CompilerParams(collective_id=0, has_side_effects=True),
        name="gather",
    )(lat, pos)


NODE_COPIES = 6


def node_kernel(agg_own, agg_nb, cnt_own, cnt_nb, lat, cot, w_edge_out, w_node_self, w_node_msg,
                node_bias, w_node_out, gain, w_recv, new_lat, dagg, part, grads, agg_in, cnt_in,
                send_sem, recv_sem):
    me = Place()
    nxt, prv = me.slab(1), me.slab(-1)
    meet([nxt, prv])
    cs = Copies(send_sem, recv_sem)
    a_prv = cs.start(agg_nb.at[0], agg_in.at[0], prv)
    a_nxt = cs.start(agg_nb.at[1], agg_in.at[1], nxt)
    c_prv = cs.start(cnt_nb.at[0], cnt_in.at[0], prv)
    c_nxt = cs.start(cnt_nb.at[1], cnt_in.at[1], nxt)
    latent = lat[...]
    self_pre = dot(latent, w_node_self[...]) + node_bias[...]
    a_prv.wait_recv()
    a_nxt.wait_recv()
    aggregate = agg_own[...] + agg_in[0].astype(F32) + agg_in[1].astype(F32)
    aggregate_b = aggregate.astype(BF16)
    message = dot(aggregate_b, w_edge_out[...]).astype(BF16)
    hidden_pre = self_pre + dot(message, w_node_msg[...])
    logistic = jax.nn.sigmoid(hidden_pre)
    hidden = (hidden_pre * logistic).astype(BF16)
    update = dot(hidden, w_node_out[...])
    average = jnp.mean(update, axis=-1, keepdims=True)
    centred = update - average
    variance = jnp.mean(centred * centred, axis=-1, keepdims=True)
    inv_std = lax.rsqrt(variance + 1e-05)
    normed = centred * inv_std
    new_lat[...] = (latent.astype(F32) + normed * gain[...]).astype(BF16)
    c = cot[...].astype(F32)
    d_normed = c * gain[...]
    d_update = (inv_std * (d_normed - jnp.mean(d_normed, axis=-1, keepdims=True)
                           - normed * jnp.mean(d_normed * normed, axis=-1, keepdims=True))
                ).astype(BF16)
    d_hidden = dot_t(d_update, w_node_out[...])
    d_hidden_pre = (d_hidden * logistic * (1.0 + hidden_pre * (1.0 - logistic))).astype(BF16)
    d_message = dot_t(d_hidden_pre, w_node_msg[...]).astype(BF16)
    d_aggregate = dot_t(d_message, w_edge_out[...])
    dagg[1] = d_aggregate.astype(BF16)
    d_nxt = cs.start(dagg.at[1], dagg.at[0], nxt)
    d_prv = cs.start(dagg.at[1], dagg.at[2], prv)
    grads[1] = contract(aggregate_b, d_message)
    grads[2] = contract(latent, d_hidden_pre)
    grads[3] = contract(message, d_hidden_pre)
    grads[4] = contract(hidden, d_update)
    direct = c + dot_t(d_hidden_pre, w_node_self[...])
    c_prv.wait_recv()
    c_nxt.wait_recv()
    count = cnt_own[...] + cnt_in[0].astype(F32) + cnt_in[1].astype(F32)
    d_recv = (count * d_aggregate).astype(BF16)
    grads[0] = contract(latent, d_recv)
    part[...] = direct + dot_t(d_recv, w_recv[...])
    d_nxt.wait_recv()
    d_prv.wait_recv()
    cs.sent()


def node(agg_own, agg_nb, cnt_own, cnt_nb, lat, cot, *weights):
    own = lat.shape[0]
    n = NODE_COPIES
    return pl.pallas_call(
        node_kernel,
        out_shape=[sd((own, 128), BF16), sd((3, own, 128), BF16), sd((own, 128), F32),
                   sd((5, 128, 128), F32)],
        in_specs=[VM] * 13,
        out_specs=[VM] * 4,
        scratch_shapes=[pltpu.VMEM((2, own, 128), BF16), pltpu.VMEM((2, own, 128), BF16),
                        pltpu.SemaphoreType.DMA((n,)), pltpu.SemaphoreType.DMA((n,))],
        compiler_params=pltpu.CompilerParams(collective_id=1, has_side_effects=True),
        name="node",
    )(agg_own, agg_nb, cnt_own, cnt_nb, lat, cot, *weights)


FINAL_COPIES = 43


def final_kernel(dsend, gsend, grads, part, w_send, latent_grad, weight_grads, v, in_core, vx, in_x,
                 vy, in_y, in_z, out_y, out_x, out_core, rs_core, cs_sum, in_ra, in_rb, in_da, in_db,
                 in_fa, in_fb, fwd_a, fwd_b, vz, send_sem, recv_sem):
    me = Place()
    own = part.shape[0]
    up, dn, sib = me.member(1), me.member(-1), me.partner()
    core, zh = me.core, me.zh
    mats = [gsend[...]] + [grads[i] for i in range(5)]
    zero = jnp.zeros((128, 128), BF16)
    for i in range(8):
        v[i // 4, i % 4] = mats[i].astype(BF16) if i < 6 else zero
    xs = [me.at(x=(me.x + d) % NX) for d in range(1, NX)]
    ys = [me.at(y=(me.y + d) % NY) for d in range(1, NY)]
    zs = [me.at(z=(me.z + d) % NZ) for d in range(1, NZ)]
    meet([sib] + xs + ys + zs)
    cs = Copies(send_sem, recv_sem)
    ha, hb = pl.ds(0, own // 2), pl.ds(own // 2, own // 2)

    ar_core = cs.start(v.at[1 - core], in_core, sib)
    order = [2, 1, 3, 0]
    rs = [cs.start(dsend.at[((zh + o) % ZHI) * 2 + 1 - core], rs_core.at[(zh + o) % ZHI], sib)
          for o in order]
    ar_core.wait_recv()
    vx[...] = (v[core].astype(F32) + in_core[...].astype(F32)).astype(BF16)
    ar_x = [cs.start(vx.at[(me.x + d) % NX], in_x.at[d - 1], xs[d - 1]) for d in range(1, NX)]

    def chip_sum(i):
        rs[i].wait_recv()
        k = (zh + order[i]) % ZHI
        cs_sum[k] = (dsend[k * 2 + core].astype(F32) + rs_core[k].astype(F32)).astype(BF16)
        return k

    far = chip_sum(0)
    ra = cs.start(cs_sum.at[far, ha], in_ra, up)
    rb = cs.start(cs_sum.at[far, hb], in_rb, dn)
    ku = chip_sum(1)
    db = cs.start(cs_sum.at[ku, hb], in_db, up)
    kd = chip_sum(2)
    da = cs.start(cs_sum.at[kd, ha], in_da, dn)
    chip_sum(3)

    for copy in ar_x:
        copy.wait_recv()
    total = vx[me.x].astype(F32)
    for d in range(NX - 1):
        total = total + in_x[d].astype(F32)
    vy[...] = total.astype(BF16).reshape(NY, 16, 128)
    ar_y = [cs.start(vy.at[(me.y + d) % NY], in_y.at[d - 1], ys[d - 1]) for d in range(1, NY)]

    for copy in ar_y:
        copy.wait_recv()
    total = vy[me.y].astype(F32)
    for d in range(NY - 1):
        total = total + in_y[d].astype(F32)
    vz[...] = total.astype(BF16)
    in_z[me.z] = total.astype(BF16)
    ar_z = [cs.start(vz, in_z.at[me.z], zs[d - 1]) for d in range(1, NZ)]

    ra.wait_recv()
    fwd_a[...] = (in_ra[...].astype(F32) + cs_sum[ku, ha].astype(F32)).astype(BF16)
    fa = cs.start(fwd_a, in_fa, up)
    rb.wait_recv()
    fwd_b[...] = (in_rb[...].astype(F32) + cs_sum[kd, hb].astype(F32)).astype(BF16)
    fb = cs.start(fwd_b, in_fb, dn)

    for copy in ar_z:
        copy.wait_recv()
    total = in_z[0].astype(F32)
    for d in range(1, NZ):
        total = total + in_z[d].astype(F32)
    mine = pl.ds(pl.multiple_of(me.y * 16, 16), 16)
    out_y[mine] = total.astype(BF16)
    ag_y = [cs.start(out_y.at[mine], out_y.at[mine], ys[d - 1]) for d in range(1, NY)]

    da.wait_recv()
    db.wait_recv()
    fa.wait_recv()
    d_a = cs_sum[zh, ha].astype(F32) + in_da[...].astype(F32) + in_fa[...].astype(F32)
    latent_grad[ha] = part[ha] + dot_t(d_a.astype(BF16), w_send[...])
    fb.wait_recv()
    d_b = cs_sum[zh, hb].astype(F32) + in_db[...].astype(F32) + in_fb[...].astype(F32)
    latent_grad[hb] = part[hb] + dot_t(d_b.astype(BF16), w_send[...])

    for copy in ag_y:
        copy.wait_recv()
    out_x[me.x] = out_y[...]
    ag_x = [cs.start(out_y, out_x.at[me.x], xs[d - 1]) for d in range(1, NX)]
    for copy in ag_x:
        copy.wait_recv()
    out_core[core] = out_x[...]
    ag_core = cs.start(out_x, out_core.at[core], sib)
    ag_core.wait_recv()
    for i in range(6):
        weight_grads[i] = out_core[i // 4, i % 4].astype(F32)
    cs.sent()


def final(dsend, gsend, grads, part, w_send):
    own = part.shape[0]
    n = FINAL_COPIES
    b = lambda *shape: pltpu.VMEM(shape, BF16)
    h = own // 2
    return pl.pallas_call(
        final_kernel,
        out_shape=[sd((own, 128), F32), sd((6, 128, 128), F32)],
        in_specs=[VM] * 5,
        out_specs=[VM] * 2,
        scratch_shapes=[
            b(2, NX, 128, 128), b(NX, 128, 128), b(NX, 128, 128), b(NX - 1, 128, 128),
            b(NY, 16, 128), b(NY - 1, 16, 128), b(NZ, 16, 128), b(128, 128),
            b(NX, 128, 128), b(2, NX, 128, 128), b(ZHI, own, 128), b(ZHI, own, 128),
            b(h, 128), b(h, 128), b(h, 128), b(h, 128), b(h, 128), b(h, 128), b(h, 128), b(h, 128),
            b(16, 128),
            pltpu.SemaphoreType.DMA((n,)), pltpu.SemaphoreType.DMA((n,))],
        compiler_params=pltpu.CompilerParams(collective_id=2, has_side_effects=True),
        name="final",
    )(dsend, gsend, grads, part, w_send)


def placed_of(pos, pw):
    return lax.dot_general(pos, pw, DN0, precision=lax.Precision.HIGHEST,
                           preferred_element_type=F32)


def rank_rows(mb, upper):
    before = dot(mb, upper)
    return jnp.where(mb > 0, before, -1.0).astype(BF16)


def forward_kernel(NS, ts, tr, tc, lat_all, pos_all, lat_nb, pos_nb, lat, pos, mask, w_send,
                   w_recv, pw, bias, agg_own, agg_nb, cnt_own, cnt_nb, s_out, r_out, rank_t, kout,
                   rank_r, deg_s, rf, agg, cnt, kvec, ksm, sem):
    tiles = mask.shape[0]
    row = lax.broadcasted_iota(jnp.int32, (128, 128), 0)
    col = lax.broadcasted_iota(jnp.int32, (128, 128), 1)
    upper = jnp.where(row < col, 1.0, 0.0).astype(BF16)
    ones = jnp.ones((128, 128), BF16)

    def prep(t, _):
        mf = mask[t].astype(F32)
        mb = mf.astype(BF16)
        rank_r[t] = rank_rows(mb, upper)
        deg = dot(mb, ones)
        deg_s[t] = deg
        kvec[pl.ds(t, 1), :] = jnp.max(deg, axis=0, keepdims=True).astype(jnp.int32)
        mtb = mf.T.astype(BF16)
        rank_t[t] = rank_rows(mtb, upper)
        degt = dot(mtb, ones)
        kvec[pl.ds(t + tiles, 1), :] = jnp.max(degt, axis=0, keepdims=True).astype(jnp.int32)
        return 0

    lax.fori_loop(0, tiles, prep, 0)
    cp = pltpu.make_async_copy(kvec, ksm, sem)
    cp.start()
    kout[...] = kvec[...]

    for slab in range(3):
        la = lat[...] if slab == 1 else lat_nb[slab // 2]
        po = pos[...] if slab == 1 else pos_nb[slab // 2]
        rr = (dot(la, w_recv[...]) - placed_of(po, pw[...]) + bias[...]).astype(BF16)
        for b in range(4):
            r_out[slab * 4 + b] = rr[b * 128:(b + 1) * 128]
            rf[slab * 4 + b] = rr[b * 128:(b + 1) * 128].astype(F32)
    agg[...] = jnp.zeros_like(agg)
    cnt[...] = jnp.zeros_like(cnt)
    cp.wait()

    def tile(t, _):
        sb = ts[t]
        rb = tr[t]
        g = sb // 4
        b = sb % 4
        po = pos_all[g, :, pl.ds(pl.multiple_of(b * 128, 128), 128)]
        s = (dot(lat_all[sb], w_send[...]) + placed_of(po, pw[...])).astype(BF16)
        s_out[t] = s
        r = rf[rb]
        kmax = ksm[t, 0]
        n = (kmax + NS - 1) // NS
        rk = rank_r[t]

        def slot(i, carry):
            a, c = carry
            base = i * NS
            for q in range(NS):
                kk = (base + q).astype(F32).astype(BF16)
                p = jnp.where(rk == kk, jnp.ones((), BF16), jnp.zeros((), BF16))
                pre = dot(p, s) + r
                a = a + jnp.maximum(pre, 0.0)
                c = c + jnp.where(pre > 0.0, 1.0, 0.0)
            return a, c

        z = jnp.zeros((128, 128), F32)
        a, c = lax.fori_loop(0, n, slot, (z, z))
        spare = (n * NS).astype(F32) - deg_s[t]
        agg[rb] += a - spare * jnp.maximum(r, 0.0)
        cnt[rb] += c - spare * jnp.where(r > 0.0, 1.0, 0.0)
        return 0

    lax.fori_loop(0, tc[0], tile, 0)
    for b in range(4):
        sl = pl.ds(b * 128, 128)
        agg_own[sl] = agg[4 + b]
        cnt_own[sl] = cnt[4 + b]
        agg_nb[0, sl] = agg[b].astype(BF16)
        agg_nb[1, sl] = agg[8 + b].astype(BF16)
        cnt_nb[0, sl] = cnt[b].astype(BF16)
        cnt_nb[1, sl] = cnt[8 + b].astype(BF16)


def forward(ts, tr, tc, lat_all, pos_all, lat_nb, pos_nb, lat, pos, mask, w_send, w_recv, pw, bias,
            NS=4):
    own = lat.shape[0]
    T = mask.shape[0]
    return pl.pallas_call(
        functools.partial(forward_kernel, NS),
        out_shape=[sd((own, 128), F32), sd((2, own, 128), BF16), sd((own, 128), F32),
                   sd((2, own, 128), BF16), sd((T, 128, 128), BF16), sd((12, 128, 128), BF16),
                   sd((T, 128, 128), BF16), sd((2 * T, 128), jnp.int32)],
        in_specs=[SMEM] * 3 + [VM] * 11,
        out_specs=[VM] * 8,
        scratch_shapes=[pltpu.VMEM((T, 128, 128), BF16), pltpu.VMEM((T, 128, 128), F32),
                        pltpu.VMEM((12, 128, 128), F32), pltpu.VMEM((12, 128, 128), F32),
                        pltpu.VMEM((12, 128, 128), F32), pltpu.VMEM((2 * T, 128), jnp.int32),
                        pltpu.SMEM((2 * T, 128), jnp.int32), pltpu.SemaphoreType.DMA(())],
        compiler_params=pltpu.CompilerParams(vmem_limit_bytes=LIMIT),
        name="forward",
    )(ts, tr, tc, lat_all, pos_all, lat_nb, pos_nb, lat, pos, mask, w_send, w_recv, pw, bias)


def backward_kernel(NS, ts, tr, tc, ksm, rank_t, s_in, r_in, dagg, lat_all, dsend, gsend, acc):
    acc[...] = jnp.zeros_like(acc)
    tiles = rank_t.shape[0]

    def tile(t, _):
        sb = ts[t]
        rb = tr[t]
        s = s_in[t].astype(F32)
        rhs = jnp.concatenate([r_in[rb], dagg[rb]], axis=1)
        kmax = ksm[t + tiles, 0]
        n = (kmax + NS - 1) // NS
        rk = rank_t[t]

        def slot(i, a):
            base = i * NS
            for q in range(NS):
                kk = (base + q).astype(F32).astype(BF16)
                p = jnp.where(rk == kk, jnp.ones((), BF16), jnp.zeros((), BF16))
                x = dot(p, rhs)
                a = a + jnp.where(x[:, :128] + s > 0.0, x[:, 128:], 0.0)
            return a

        a = lax.fori_loop(0, n, slot, jnp.zeros((128, 128), F32))
        acc[sb] += a
        return 0

    lax.fori_loop(0, tc[0], tile, 0)
    g = jnp.zeros((128, 128), F32)
    for b in range(8):
        d = acc[pl.ds(4 * b, 4)].reshape(512, 128).astype(BF16)
        dsend[b] = d
        g = g + lax.dot_general(lat_all[b], d, DN0, preferred_element_type=F32)
    gsend[...] = g


def backward(ts, tr, tc, kout, rank_t, s_in, r_in, dagg, lat_all, NS=4):
    return pl.pallas_call(
        functools.partial(backward_kernel, NS),
        out_shape=[sd((8, 512, 128), BF16), sd((128, 128), F32)],
        in_specs=[SMEM] * 4 + [VM] * 5,
        out_specs=[VM] * 2,
        scratch_shapes=[pltpu.VMEM((32, 128, 128), F32)],
        compiler_params=pltpu.CompilerParams(vmem_limit_bytes=LIMIT),
        name="backward",
    )(ts, tr, tc, kout, rank_t, s_in, r_in, dagg, lat_all)


def body(latent, positions, tile_send, tile_recv, tile_mask, tile_count, w_send, w_recv, pos_weight,
         edge_bias, w_edge_out, w_node_self, w_node_msg, node_bias, w_node_out, gain, cotangent):
    own = latent.shape[0]
    ts, tr, tc = tile_send[0, 0], tile_recv[0, 0], tile_count[0]
    lat_all, pos_all, lat_nb, pos_nb = gather(latent, positions)
    agg_own, agg_nb, cnt_own, cnt_nb, s_rows, r_rows, rank_t, slots = forward(
        ts, tr, tc, lat_all.reshape(32, 128, 128), pos_all, lat_nb, pos_nb, latent, positions,
        tile_mask[0, 0], w_send, w_recv, pos_weight, edge_bias[None])
    new_latent, dagg, part, grads = node(
        agg_own, agg_nb, cnt_own, cnt_nb, latent, cotangent, w_edge_out, w_node_self, w_node_msg,
        node_bias[None], w_node_out, gain[None], w_recv)
    dsend, gsend = backward(ts, tr, tc, slots, rank_t, s_rows, r_rows, dagg.reshape(12, 128, 128),
                            lat_all)
    latent_grad, weight_grads = final(dsend, gsend, grads, part, w_send)
    return new_latent, latent_grad, weight_grads


def solution(mesh):
    in_specs = (
        P(("blk", "grp"), None),
        P(None, ("blk", "grp")),
        P("blk", "grp", None),
        P("blk", "grp", None),
        P("blk", "grp", None, None, None),
        P("blk", "grp"),
        P(),
        P(),
        P(),
        P(),
        P(),
        P(),
        P(),
        P(),
        P(),
        P(),
        P(("blk", "grp"), None),
    )
    out_specs = (P(("blk", "grp"), None), P(("blk", "grp"), None), P())
    return jax.shard_map(body, mesh=mesh, in_specs=in_specs, out_specs=out_specs, check_vma=False)
```

time: 978 us -> 147 us (0.15)
  waiting for transfers between devices: 555 us -> 0 us
  other arithmetic: 164 us -> 0 us
  Pallas kernels: 0 us -> 143 us
  local copies, waits for them, and re-layouts: 113 us -> 2.43 us
  loops' own time: 70.7 us -> 0 us
  starting transfers between devices: 45 us -> 0 us
  between operations: 14.4 us -> 1.34 us
    psum x1 -> x0, waiting for transfers between devices: 468 us -> none  [body(): weight_grads = lax.psum(local_grads, ('blk', 'grp'))]
    pallas_call x0 -> x5, Pallas kernels: none -> 143 us  [the longest x1 58.3 us: final(): pl.pallas_call(final_kernel, out_shape=[sd((own, 128), F32), sd((6, 128,...]
    reduce_sum x130 -> x0, other arithmetic: 92.2 us -> none  [the longest x64 46.5 us: one_group(): return (running, jnp.sum(terms, axis=1))]
    another operation x34 -> x0, loops' own time: 70.7 us -> none  [the longest x1 33.3 us: body(): grads_out = lax.fori_loop(0, tiles_here, backward_tile, back_state)]
    dynamic_slice x96 -> x0, local copies, waits for them, and re-layouts: 65.8 us -> none  [the longest x32 20 us: locate(): recv_start = recv_table[tile_step] * block_size]
    ppermute x8 -> x0, starting transfers between devices: 44.9 us -> none  [shifted(): return lax.ppermute(value, axis, pairs)]
    dynamic_update_slice x128 -> x0, local copies, waits for them, and re-layouts: 39.5 us -> none  [edge_forward(): lax.map(one_group, (recv_block.reshape(group_count, group_rows, width), e...]
    all_gather x1 -> x0, waiting for transfers between devices: 33.2 us -> none  [body(): senders = lax.all_gather(send_rows, 'grp', axis=0, tiled=True)]
  transfers between devices with their start and end apart: 11 -> 0, of which waited for: 11 -> 0; matrix products, arithmetic and copies ran while one was open for 0% -> 0% of each run, Pallas kernels for 0% -> 0%
where the time goes in v1:
time: 147 us; the launch traced here: 146 us
  Pallas kernels  143 us (97%)
  local copies, waits for them, and re-layouts  2.43 us (2%)
    pallas_call x1, Pallas kernels, final(): pl.pallas_call(final_kernel, out_shape=[sd((own, 128), F32), sd((6, 128,...  58.3 us
    pallas_call x1, Pallas kernels, gather(): pl.pallas_call(gather_kernel, out_shape=[sd((8, own, 128), BF16), sd((8,...  41.5 us
    pallas_call x1, Pallas kernels, node(): pl.pallas_call(node_kernel, out_shape=[sd((own, 128), BF16), sd((3, own,...  29.4 us
    pallas_call x1, Pallas kernels, forward(): pl.pallas_call(functools.partial(forward_kernel, NS), out_shape=[sd((own,...  9.34 us
    pallas_call x1, Pallas kernels, backward(): pl.pallas_call(functools.partial(backward_kernel, NS), out_shape=[sd((8,...  4.13 us

profile of v1, /device:TPU:1, one launch (start us, length us, event | category | flops | bytes accessed | tf_op | source)
XLA Modules:
  0.0 146.4 jit_solution(3753639024815167196)
XLA Ops:
  1.3 41.5 %gather.1 = (bf16[8,512,128]{2,1,0:T(8,128)(2,1)}, f32[8,3,512]{2,1,0:T(4,128)}, bf16[2,512,128]{2,1,0:T(8,128)(2,1)}, f32[2,3,512]{2,1,0:T(4,128)}) custom-call(bf16[512,128]{1,0:T(8,128)(2,1)} %lat.5, f32[3,512]{1,0:T(4,128)} %pos.3), custom_call_target="tpu_custom_call" | custom-call | tf_op jit(solution)/shard_map/gather/pallas_call | solution.py:156
  42.8 9.3 %forward.1 = (f32[512,128]{1,0:T(8,128)}, bf16[2,512,128]{2,1,0:T(8,128)(2,1)}, f32[512,128]{1,0:T(8,128)}, bf16[2,512,128]{2,1,0:T(8,128)(2,1)}, bf16[16,128,12...) custom-call(s32[16]{0:T(128)} %bitcast.14, s32[16]{0:T(128)} %bitcast.16, ...), custom_call_target="tpu_custom_call" | custom-call | tf_op jit(solution)/shard_map/forward/pallas_call | solution.py:459
  52.1 29.4 %node.1 = (bf16[512,128]{1,0:T(8,128)(2,1)}, bf16[3,512,128]{2,1,0:T(8,128)(2,1)}, f32[512,128]{1,0:T(8,128)}, f32[5,128,128]{2,1,0:T(8,128)}) custom-call(f32[512,128]{1,0:T(8,128)} %get-tuple-element.27.agg_own, bf16[2,512,128]{2,1,0:T(8,128)(2,1)} %get-tuple-element.28.agg_nb, f32[512,128]{1,0:T(8,128)} %get-tuple-element.29.cnt_own, ...), custom_call_target="tpu_custom_call" | custom-call | tf_op jit(solution)/shard_map/node/pallas_call | solution.py:230
  81.5 4.1 %backward.1 = (bf16[8,512,128]{2,1,0:T(8,128)(2,1)}, f32[128,128]{1,0:T(8,128)}) custom-call(s32[16]{0:T(128)} %bitcast.15, s32[16]{0:T(128)} %bitcast.17, s32[1]{0:T(128)} %bitcast.10.tc, s32[32,128]{1,0:T(8,128)} %get-tuple-element.32.ksm, bf16[16,128,128]{2,1,0:T(8,128)(2,1)} %get-tuple-element.33.rank_t, bf16[16,128,128]{2,1,0:T(8,128)(2,1)} %get-tuple-element.34.s_in, ...), custom_call_target="tpu_custom_call" | custom-call | tf_op jit(solution)/shard_map/backward/pallas_call | solution.py:511
  85.7 0.0 copy-start.2
  85.7 58.3 %final.1 = (f32[512,128]{1,0:T(8,128)}, f32[6,128,128]{2,1,0:T(8,128)}) custom-call(bf16[8,512,128]{2,1,0:T(8,128)(2,1)} %get-tuple-element.37.dsend, f32[128,128]{1,0:T(8,128)} %get-tuple-element.38.gsend, f32[5,128,128]{2,1,0:T(8,128)} %get-tuple-element.39.grads, f32[512,128]{1,0:T(8,128)} %get-tuple-element.40.part, bf16[128,128]{1,0:T(8,128)(2,1)} %w_send.3), custom_call_target="tpu_custom_call" | custom-call | tf_op jit(solution)/shard_map/final/pallas_call | solution.py:348
  144.0 0.0 copy-start.1
  144.0 0.0 copy-done.2
  144.0 0.0 copy-start
  144.0 0.7 copy.24
  144.7 0.3 copy-done.1
  145.0 0.7 copy.25
  145.7 0.0 copy-done
  145.7 0.7 copy.26
Async XLA Ops:
  85.7 58.3 %copy-start.2 = (bf16[512,128]{1,0:T(8,128)(2,1)S(1)}, bf16[512,128]{1,0:T(8,128)(2,1)}, u32[]{:S(2)}) copy-start(bf16[512,128]{1,0:T(8,128)(2,1)} %get-tuple-element.46) | copy-start | bytes 393220
  144.0 1.0 copy-start.1
  144.0 1.7 %copy-start = (f32[6,128,128]{2,1,0:T(8,128)S(1)}, f32[6,128,128]{2,1,0:T(8,128)}, u32[]{:S(2)}) copy-start(f32[6,128,128]{2,1,0:T(8,128)} %get-tuple-element.48) | copy-start | bytes 1179652

commit v2 on v1

--- a/solution.py
+++ b/solution.py
@@ -87,10 +87,164 @@
     return lax.dot_general(a, b, DN0, preferred_element_type=F32)
 
 
+def placed_of(pos, pw):
+    return lax.dot_general(pos, pw, DN0, precision=lax.Precision.HIGHEST,
+                           preferred_element_type=F32)
+
+
+def rank_tiles(mask, rank_r, rank_t, top):
+    tiles = mask.shape[0]
+    row = lax.broadcasted_iota(jnp.int32, (128, 128), 0)
+    col = lax.broadcasted_iota(jnp.int32, (128, 128), 1)
+    upper = jnp.where(row < col, 1.0, 0.0).astype(BF16)
+
+    def ranks(values):
+        return jnp.where(values > 0.0, dot(values.astype(BF16), upper), -1.0)
+
+    def tile(t, _):
+        values = mask[t].astype(F32)
+        by_row = ranks(values)
+        rank_r[t] = by_row.astype(BF16)
+        top[pl.ds(t, 1), :] = jnp.max(by_row, axis=0, keepdims=True)
+        by_col = ranks(values.T)
+        rank_t[t] = by_col.astype(BF16)
+        top[pl.ds(t + tiles, 1), :] = jnp.max(by_col, axis=0, keepdims=True)
+        return 0
+
+    lax.fori_loop(0, tiles, tile, 0)
+
+
+def slot_counts(top):
+    most = jnp.max(top[...], axis=1, keepdims=True) + 1.0
+    return jnp.broadcast_to(most, top.shape).astype(jnp.int32)
+
+
+def picks(ranks, slot):
+    one, none = jnp.ones((), BF16), jnp.zeros((), BF16)
+    if isinstance(slot, int):
+        slot = jnp.full((), slot, BF16)
+    else:
+        slot = slot.astype(F32).astype(BF16)
+    return jnp.where(ranks == slot, one, none)
+
+
+def forward_kernel(first, more, ts, tr, tc, most, s_rows, r_rows, rank_r, agg_own, agg_nb, cnt_own,
+                   cnt_nb, agg, cnt):
+    agg[...] = jnp.zeros_like(agg)
+    cnt[...] = jnp.zeros_like(cnt)
+    ones = jnp.ones((128, 128), BF16)
+
+    def tile(t, _):
+        rb = tr[t]
+        s = s_rows[ts[t]]
+        rk = rank_r[t]
+        floor = -(r_rows[rb].astype(F32))
+
+        def add(slot, a, c):
+            x = dot(picks(rk, slot), s)
+            return a + jnp.maximum(x, floor), c + jnp.where(x > floor, 1.0, 0.0)
+
+        a = jnp.zeros((128, 128), F32)
+        c = jnp.zeros((128, 128), F32)
+        for slot in range(first):
+            a, c = add(slot, a, c)
+        n = (jnp.maximum(most[t, 0] - first, 0) + more - 1) // more
+
+        def rest(i, carry):
+            a, c = carry
+            for q in range(more):
+                a, c = add(first + i * more + q, a, c)
+            return a, c
+
+        a, c = lax.fori_loop(0, n, rest, (a, c))
+        degree = dot(jnp.where(rk >= jnp.zeros((), BF16), jnp.ones((), BF16), jnp.zeros((), BF16)), ones)
+        spare = (first + n * more).astype(F32) - degree
+        agg[rb] += a - degree * floor - spare * jnp.maximum(floor, 0.0)
+        cnt[rb] += c - spare * jnp.where(floor < 0.0, 1.0, 0.0)
+        return 0
+
+    lax.fori_loop(0, tc[0], tile, 0)
+    for b in range(4):
+        sl = pl.ds(b * 128, 128)
+        agg_own[sl] = agg[4 + b]
+        cnt_own[sl] = cnt[4 + b]
+        agg_nb[0, sl] = agg[b].astype(BF16)
+        agg_nb[1, sl] = agg[8 + b].astype(BF16)
+        cnt_nb[0, sl] = cnt[b].astype(BF16)
+        cnt_nb[1, sl] = cnt[8 + b].astype(BF16)
+
+
+def forward(ts, tr, tc, most, s_rows, r_rows, rank_r, first=18, more=4):
+    own = 512
+    return pl.pallas_call(
+        functools.partial(forward_kernel, first, more),
+        out_shape=[sd((own, 128), F32), sd((2, own, 128), BF16), sd((own, 128), F32),
+                   sd((2, own, 128), BF16)],
+        in_specs=[SMEM] * 4 + [VM] * 3,
+        out_specs=[VM] * 4,
+        scratch_shapes=[pltpu.VMEM((12, 128, 128), F32), pltpu.VMEM((12, 128, 128), F32)],
+        compiler_params=pltpu.CompilerParams(vmem_limit_bytes=LIMIT),
+        name="forward",
+    )(ts, tr, tc, most, s_rows, r_rows, rank_r)
+
+
+def backward_kernel(first, more, ts, tr, tc, most, rank_t, s_rows, r_rows, dagg, lat_all, dsend,
+                    gsend, acc):
+    acc[...] = jnp.zeros_like(acc)
+    tiles = rank_t.shape[0]
+
+    def tile(t, _):
+        sb = ts[t]
+        rb = tr[t]
+        floor = -(s_rows[sb].astype(F32))
+        rhs = jnp.concatenate([r_rows[rb], dagg[rb]], axis=1)
+        rk = rank_t[t]
+
+        def add(slot, a):
+            x = dot(picks(rk, slot), rhs)
+            return a + jnp.where(x[:, :128] > floor, x[:, 128:], 0.0)
+
+        a = jnp.zeros((128, 128), F32)
+        for slot in range(first):
+            a = add(slot, a)
+        n = (jnp.maximum(most[t + tiles, 0] - first, 0) + more - 1) // more
+
+        def rest(i, a):
+            for q in range(more):
+                a = add(first + i * more + q, a)
+            return a
+
+        acc[sb] += lax.fori_loop(0, n, rest, a)
+        return 0
+
+    lax.fori_loop(0, tc[0], tile, 0)
+    g = jnp.zeros((128, 128), F32)
+    for b in range(8):
+        d = acc[pl.ds(4 * b, 4)].reshape(512, 128).astype(BF16)
+        dsend[b] = d
+        g = g + contract(lat_all[b], d)
+    gsend[...] = g
+
+
+def backward(ts, tr, tc, most, rank_t, s_rows, r_rows, dagg, lat_all, first=18, more=4):
+    return pl.pallas_call(
+        functools.partial(backward_kernel, first, more),
+        out_shape=[sd((8, 512, 128), BF16), sd((128, 128), F32)],
+        in_specs=[SMEM] * 4 + [VM] * 5,
+        out_specs=[VM] * 2,
+        scratch_shapes=[pltpu.VMEM((32, 128, 128), F32)],
+        compiler_params=pltpu.CompilerParams(vmem_limit_bytes=LIMIT),
+        name="backward",
+    )(ts, tr, tc, most, rank_t, s_rows, r_rows, dagg, lat_all)
+
+
 GATHER_COPIES = 24
 
 
-def gather_kernel(lat, pos, lat_all, pos_all, lat_nb, pos_nb, send_sem, recv_sem):
+def gather_kernel(lat, pos, w_send, w_recv, pw, bias, mask_in, lat_all, s_rows, r_rows, rank_r,
+                  rank_t, most, mask, top, pos_all, lat_nb, pos_nb, mask_sem, send_sem, recv_sem):
+    load = pltpu.make_async_copy(mask_in, mask, mask_sem)
+    load.start()
     me = Place()
     own = lat.shape[0]
     g = me.grp
@@ -109,11 +263,13 @@
     dn_b = cs.start(lat.at[halves[1]], half(g, 1), dn)
     up_b = cs.start(lat.at[halves[1]], half(g, 1), up)
     dn_a = cs.start(lat.at[halves[0]], half(g, 0), dn)
-    waits = [
+    beside = [
         cs.start(lat, lat_nb.at[0], nxt),
         cs.start(lat, lat_nb.at[1], prv),
         cs.start(pos, pos_nb.at[0], nxt),
         cs.start(pos, pos_nb.at[1], prv),
+    ]
+    partner = [
         cs.start(lat, lat_all.at[g], sib),
         cs.start(pos, pos_all.at[g], sib),
     ]
@@ -122,47 +278,83 @@
     iu, idn, far = up[1], dn[1], me.member(2)[1]
 
     def pass_on(ref):
-        waits.append(cs.start(ref, ref, sib))
+        return cs.start(ref, ref, sib)
+
+    def send_rows(index):
+        s_rows[index] = (dot(lat_all[index], w_send[...])
+                         + placed_of(pos_all[index], pw[...])).astype(BF16)
+
+    def recv_rows(slab, rows, places):
+        r_rows[slab] = (dot(rows, w_recv[...]) - placed_of(places, pw[...])
+                        + bias[...]).astype(BF16)
+
+    def other(index):
+        return (index // 2) * 2 + 1 - me.core
+
+    recv_rows(1, lat[...], pos[...])
+    send_rows(g)
+    load.wait()
+    rank_tiles(mask, rank_r, rank_t, top)
+    most[...] = slot_counts(top)
 
     up_pos.wait_recv()
     far_pos = cs.start(pos_all.at[idn], pos_all.at[idn], up)
-    pass_on(pos_all.at[idn])
+    near = [pass_on(pos_all.at[idn])]
     dn_pos.wait_recv()
-    pass_on(pos_all.at[iu])
+    near.append(pass_on(pos_all.at[iu]))
     up_a.wait_recv()
     far_a = cs.start(half(idn, 0), half(idn, 0), up)
-    pass_on(half(idn, 0))
+    near.append(pass_on(half(idn, 0)))
     dn_b.wait_recv()
     far_b = cs.start(half(iu, 1), half(iu, 1), dn)
-    pass_on(half(iu, 1))
+    near.append(pass_on(half(iu, 1)))
+    for copy in beside + partner:
+        copy.wait_recv()
+    recv_rows(0, lat_nb[0], pos_nb[0])
+    recv_rows(2, lat_nb[1], pos_nb[1])
+    send_rows(sib[1])
     up_b.wait_recv()
-    pass_on(half(idn, 1))
+    near.append(pass_on(half(idn, 1)))
+    send_rows(idn)
     dn_a.wait_recv()
-    pass_on(half(iu, 0))
+    near.append(pass_on(half(iu, 0)))
+    send_rows(iu)
     far_pos.wait_recv()
-    pass_on(pos_all.at[far])
+    last = [pass_on(pos_all.at[far])]
+    for copy in near:
+        copy.wait_recv()
+    send_rows(other(idn))
+    send_rows(other(iu))
     far_a.wait_recv()
-    pass_on(half(far, 0))
+    last.append(pass_on(half(far, 0)))
     far_b.wait_recv()
-    pass_on(half(far, 1))
-    for copy in waits:
-        copy.wait_recv()
+    last.append(pass_on(half(far, 1)))
+    send_rows(far)
+    for copy in last:
+        copy.wait_recv()
+    send_rows(other(far))
     cs.sent()
 
 
-def gather(lat, pos):
+def gather(lat, pos, w_send, w_recv, pw, bias, mask):
     own = lat.shape[0]
     n = GATHER_COPIES
+    tiles = mask.shape[0]
+    ranks = sd((tiles, 128, 128), BF16)
     return pl.pallas_call(
         gather_kernel,
-        out_shape=[sd((8, own, 128), BF16), sd((8, 3, own), F32), sd((2, own, 128), BF16),
-                   sd((2, 3, own), F32)],
-        in_specs=[VM] * 2,
-        out_specs=[VM] * 4,
-        scratch_shapes=[pltpu.SemaphoreType.DMA((n,)), pltpu.SemaphoreType.DMA((n,))],
-        compiler_params=pltpu.CompilerParams(collective_id=0, has_side_effects=True),
+        out_shape=[sd((8, own, 128), BF16), sd((8, own, 128), BF16), sd((3, own, 128), BF16),
+                   ranks, ranks, sd((2 * tiles, 128), jnp.int32)],
+        in_specs=[VM] * 6 + [pl.BlockSpec(memory_space=pl.ANY)],
+        out_specs=[VM] * 6,
+        scratch_shapes=[pltpu.VMEM((tiles, 128, 128), jnp.int32), pltpu.VMEM((2 * tiles, 128), F32),
+                        pltpu.VMEM((8, 3, own), F32), pltpu.VMEM((2, own, 128), BF16),
+                        pltpu.VMEM((2, 3, own), F32), pltpu.SemaphoreType.DMA(()),
+                        pltpu.SemaphoreType.DMA((n,)), pltpu.SemaphoreType.DMA((n,))],
+        compiler_params=pltpu.CompilerParams(collective_id=0, has_side_effects=True,
+                                             vmem_limit_bytes=LIMIT),
         name="gather",
-    )(lat, pos)
+    )(lat, pos, w_send, w_recv, pw, bias, mask)
 
 
 NODE_COPIES = 6
@@ -177,12 +369,12 @@
     cs = Copies(send_sem, recv_sem)
     a_prv = cs.start(agg_nb.at[0], agg_in.at[0], prv)
     a_nxt = cs.start(agg_nb.at[1], agg_in.at[1], nxt)
-    c_prv = cs.start(cnt_nb.at[0], cnt_in.at[0], prv)
-    c_nxt = cs.start(cnt_nb.at[1], cnt_in.at[1], nxt)
     latent = lat[...]
     self_pre = dot(latent, w_node_self[...]) + node_bias[...]
     a_prv.wait_recv()
     a_nxt.wait_recv()
+    c_prv = cs.start(cnt_nb.at[0], cnt_in.at[0], prv)
+    c_nxt = cs.start(cnt_nb.at[1], cnt_in.at[1], nxt)
     aggregate = agg_own[...] + agg_in[0].astype(F32) + agg_in[1].astype(F32)
     aggregate_b = aggregate.astype(BF16)
     message = dot(aggregate_b, w_edge_out[...]).astype(BF16)
@@ -362,175 +554,18 @@
     )(dsend, gsend, grads, part, w_send)
 
 
-def placed_of(pos, pw):
-    return lax.dot_general(pos, pw, DN0, precision=lax.Precision.HIGHEST,
-                           preferred_element_type=F32)
-
-
-def rank_rows(mb, upper):
-    before = dot(mb, upper)
-    return jnp.where(mb > 0, before, -1.0).astype(BF16)
-
-
-def forward_kernel(NS, ts, tr, tc, lat_all, pos_all, lat_nb, pos_nb, lat, pos, mask, w_send,
-                   w_recv, pw, bias, agg_own, agg_nb, cnt_own, cnt_nb, s_out, r_out, rank_t, kout,
-                   rank_r, deg_s, rf, agg, cnt, kvec, ksm, sem):
-    tiles = mask.shape[0]
-    row = lax.broadcasted_iota(jnp.int32, (128, 128), 0)
-    col = lax.broadcasted_iota(jnp.int32, (128, 128), 1)
-    upper = jnp.where(row < col, 1.0, 0.0).astype(BF16)
-    ones = jnp.ones((128, 128), BF16)
-
-    def prep(t, _):
-        mf = mask[t].astype(F32)
-        mb = mf.astype(BF16)
-        rank_r[t] = rank_rows(mb, upper)
-        deg = dot(mb, ones)
-        deg_s[t] = deg
-        kvec[pl.ds(t, 1), :] = jnp.max(deg, axis=0, keepdims=True).astype(jnp.int32)
-        mtb = mf.T.astype(BF16)
-        rank_t[t] = rank_rows(mtb, upper)
-        degt = dot(mtb, ones)
-        kvec[pl.ds(t + tiles, 1), :] = jnp.max(degt, axis=0, keepdims=True).astype(jnp.int32)
-        return 0
-
-    lax.fori_loop(0, tiles, prep, 0)
-    cp = pltpu.make_async_copy(kvec, ksm, sem)
-    cp.start()
-    kout[...] = kvec[...]
-
-    for slab in range(3):
-        la = lat[...] if slab == 1 else lat_nb[slab // 2]
-        po = pos[...] if slab == 1 else pos_nb[slab // 2]
-        rr = (dot(la, w_recv[...]) - placed_of(po, pw[...]) + bias[...]).astype(BF16)
-        for b in range(4):
-            r_out[slab * 4 + b] = rr[b * 128:(b + 1) * 128]
-            rf[slab * 4 + b] = rr[b * 128:(b + 1) * 128].astype(F32)
-    agg[...] = jnp.zeros_like(agg)
-    cnt[...] = jnp.zeros_like(cnt)
-    cp.wait()
-
-    def tile(t, _):
-        sb = ts[t]
-        rb = tr[t]
-        g = sb // 4
-        b = sb % 4
-        po = pos_all[g, :, pl.ds(pl.multiple_of(b * 128, 128), 128)]
-        s = (dot(lat_all[sb], w_send[...]) + placed_of(po, pw[...])).astype(BF16)
-        s_out[t] = s
-        r = rf[rb]
-        kmax = ksm[t, 0]
-        n = (kmax + NS - 1) // NS
-        rk = rank_r[t]
-
-        def slot(i, carry):
-            a, c = carry
-            base = i * NS
-            for q in range(NS):
-                kk = (base + q).astype(F32).astype(BF16)
-                p = jnp.where(rk == kk, jnp.ones((), BF16), jnp.zeros((), BF16))
-                pre = dot(p, s) + r
-                a = a + jnp.maximum(pre, 0.0)
-                c = c + jnp.where(pre > 0.0, 1.0, 0.0)
-            return a, c
-
-        z = jnp.zeros((128, 128), F32)
-        a, c = lax.fori_loop(0, n, slot, (z, z))
-        spare = (n * NS).astype(F32) - deg_s[t]
-        agg[rb] += a - spare * jnp.maximum(r, 0.0)
-        cnt[rb] += c - spare * jnp.where(r > 0.0, 1.0, 0.0)
-        return 0
-
-    lax.fori_loop(0, tc[0], tile, 0)
-    for b in range(4):
-        sl = pl.ds(b * 128, 128)
-        agg_own[sl] = agg[4 + b]
-        cnt_own[sl] = cnt[4 + b]
-        agg_nb[0, sl] = agg[b].astype(BF16)
-        agg_nb[1, sl] = agg[8 + b].astype(BF16)
-        cnt_nb[0, sl] = cnt[b].astype(BF16)
-        cnt_nb[1, sl] = cnt[8 + b].astype(BF16)
-
-
-def forward(ts, tr, tc, lat_all, pos_all, lat_nb, pos_nb, lat, pos, mask, w_send, w_recv, pw, bias,
-            NS=4):
-    own = lat.shape[0]
-    T = mask.shape[0]
-    return pl.pallas_call(
-        functools.partial(forward_kernel, NS),
-        out_shape=[sd((own, 128), F32), sd((2, own, 128), BF16), sd((own, 128), F32),
-                   sd((2, own, 128), BF16), sd((T, 128, 128), BF16), sd((12, 128, 128), BF16),
-                   sd((T, 128, 128), BF16), sd((2 * T, 128), jnp.int32)],
-        in_specs=[SMEM] * 3 + [VM] * 11,
-        out_specs=[VM] * 8,
-        scratch_shapes=[pltpu.VMEM((T, 128, 128), BF16), pltpu.VMEM((T, 128, 128), F32),
-                        pltpu.VMEM((12, 128, 128), F32), pltpu.VMEM((12, 128, 128), F32),
-                        pltpu.VMEM((12, 128, 128), F32), pltpu.VMEM((2 * T, 128), jnp.int32),
-                        pltpu.SMEM((2 * T, 128), jnp.int32), pltpu.SemaphoreType.DMA(())],
-        compiler_params=pltpu.CompilerParams(vmem_limit_bytes=LIMIT),
-        name="forward",
-    )(ts, tr, tc, lat_all, pos_all, lat_nb, pos_nb, lat, pos, mask, w_send, w_recv, pw, bias)
-
-
-def backward_kernel(NS, ts, tr, tc, ksm, rank_t, s_in, r_in, dagg, lat_all, dsend, gsend, acc):
-    acc[...] = jnp.zeros_like(acc)
-    tiles = rank_t.shape[0]
-
-    def tile(t, _):
-        sb = ts[t]
-        rb = tr[t]
-        s = s_in[t].astype(F32)
-        rhs = jnp.concatenate([r_in[rb], dagg[rb]], axis=1)
-        kmax = ksm[t + tiles, 0]
-        n = (kmax + NS - 1) // NS
-        rk = rank_t[t]
-
-        def slot(i, a):
-            base = i * NS
-            for q in range(NS):
-                kk = (base + q).astype(F32).astype(BF16)
-                p = jnp.where(rk == kk, jnp.ones((), BF16), jnp.zeros((), BF16))
-                x = dot(p, rhs)
-                a = a + jnp.where(x[:, :128] + s > 0.0, x[:, 128:], 0.0)
-            return a
-
-        a = lax.fori_loop(0, n, slot, jnp.zeros((128, 128), F32))
-        acc[sb] += a
-        return 0
-
-    lax.fori_loop(0, tc[0], tile, 0)
-    g = jnp.zeros((128, 128), F32)
-    for b in range(8):
-        d = acc[pl.ds(4 * b, 4)].reshape(512, 128).astype(BF16)
-        dsend[b] = d
-        g = g + lax.dot_general(lat_all[b], d, DN0, preferred_element_type=F32)
-    gsend[...] = g
-
-
-def backward(ts, tr, tc, kout, rank_t, s_in, r_in, dagg, lat_all, NS=4):
-    return pl.pallas_call(
-        functools.partial(backward_kernel, NS),
-        out_shape=[sd((8, 512, 128), BF16), sd((128, 128), F32)],
-        in_specs=[SMEM] * 4 + [VM] * 5,
-        out_specs=[VM] * 2,
-        scratch_shapes=[pltpu.VMEM((32, 128, 128), F32)],
-        compiler_params=pltpu.CompilerParams(vmem_limit_bytes=LIMIT),
-        name="backward",
-    )(ts, tr, tc, kout, rank_t, s_in, r_in, dagg, lat_all)
-
-
 def body(latent, positions, tile_send, tile_recv, tile_mask, tile_count, w_send, w_recv, pos_weight,
          edge_bias, w_edge_out, w_node_self, w_node_msg, node_bias, w_node_out, gain, cotangent):
-    own = latent.shape[0]
     ts, tr, tc = tile_send[0, 0], tile_recv[0, 0], tile_count[0]
-    lat_all, pos_all, lat_nb, pos_nb = gather(latent, positions)
-    agg_own, agg_nb, cnt_own, cnt_nb, s_rows, r_rows, rank_t, slots = forward(
-        ts, tr, tc, lat_all.reshape(32, 128, 128), pos_all, lat_nb, pos_nb, latent, positions,
-        tile_mask[0, 0], w_send, w_recv, pos_weight, edge_bias[None])
+    lat_all, s_rows, r_rows, rank_r, rank_t, most = gather(
+        latent, positions, w_send, w_recv, pos_weight, edge_bias[None], tile_mask[0, 0])
+    s_rows = s_rows.reshape(32, 128, 128)
+    r_rows = r_rows.reshape(12, 128, 128)
+    agg_own, agg_nb, cnt_own, cnt_nb = forward(ts, tr, tc, most, s_rows, r_rows, rank_r)
     new_latent, dagg, part, grads = node(
         agg_own, agg_nb, cnt_own, cnt_nb, latent, cotangent, w_edge_out, w_node_self, w_node_msg,
         node_bias[None], w_node_out, gain[None], w_recv)
-    dsend, gsend = backward(ts, tr, tc, slots, rank_t, s_rows, r_rows, dagg.reshape(12, 128, 128),
+    dsend, gsend = backward(ts, tr, tc, most, rank_t, s_rows, r_rows, dagg.reshape(12, 128, 128),
                             lat_all)
     latent_grad, weight_grads = final(dsend, gsend, grads, part, w_send)
     return new_latent, latent_grad, weight_grads

time: 147 us -> 127 us (0.86)
  Pallas kernels: 143 us -> 123 us
    pallas_call x1, Pallas kernels: 29.4 us -> 19.3 us  [node(): pl.pallas_call(node_kernel, out_shape=[sd((own, 128), BF16), sd((3, own,...]
    pallas_call x2, Pallas kernels: 13.5 us -> 6.94 us  [the longest x1 3.81 us: backward(): pl.pallas_call(functools.partial(backward_kernel, first, more), out_shape...]
    pallas_call x1, Pallas kernels: 58.3 us -> 53.8 us  [final(): pl.pallas_call(final_kernel, out_shape=[sd((own, 128), F32), sd((6, 128,...]
where the time goes in v2:
time: 127 us
  Pallas kernels  123 us (97%)
  local copies, waits for them, and re-layouts  2.43 us (2%)
  between operations  1.33 us (1%)
    pallas_call x1, Pallas kernels, final(): pl.pallas_call(final_kernel, out_shape=[sd((own, 128), F32), sd((6, 128,...  53.8 us
    pallas_call x1, Pallas kernels, gather(): pl.pallas_call(gather_kernel, out_shape=[sd((8, own, 128), BF16), sd((8,...  42.9 us
    pallas_call x1, Pallas kernels, node(): pl.pallas_call(node_kernel, out_shape=[sd((own, 128), BF16), sd((3, own,...  19.3 us
    pallas_call x1, Pallas kernels, backward(): pl.pallas_call(functools.partial(backward_kernel, first, more), out_shape...  3.81 us
    pallas_call x1, Pallas kernels, forward(): pl.pallas_call(functools.partial(forward_kernel, first, more), out_shape=...  3.13 us

profile of v2, /device:TPU:1, one launch (start us, length us, event | category | flops | bytes accessed | tf_op | source)
XLA Modules:
  0.0 126.7 jit_solution(12233683311518544049)
XLA Ops:
  1.3 42.9 %gather.1 = (bf16[8,512,128]{2,1,0:T(8,128)(2,1)}, bf16[8,512,128]{2,1,0:T(8,128)(2,1)}, bf16[3,512,128]{2,1,0:T(8,128)(2,1)}, bf16[16,128,128]{2,1,0:T(8,128)(2...) custom-call(bf16[512,128]{1,0:T(8,128)(2,1)} %lat.3, f32[3,512]{1,0:T(4,128)} %pos.1, bf16[128,128]{1,0:T(8,128)(2,1)} %w_send.3, ...), custom_call_target="tpu_custom_call" | custom-call | tf_op jit(solution)/shard_map/gather/pallas_call | solution.py:344
  44.2 3.1 %forward.1 = (f32[512,128]{1,0:T(8,128)}, bf16[2,512,128]{2,1,0:T(8,128)(2,1)}, f32[512,128]{1,0:T(8,128)}, bf16[2,512,128]{2,1,0:T(8,128)(2,1)}) custom-call(s32[16]{0:T(128)} %bitcast.18, s32[16]{0:T(128)} %bitcast.20, s32[1]{0:T(128)} %bitcast.10.tc, s32[32,128]{1,0:T(8,128)} %get-tuple-element.21.most, bf16[32,128,128]{2,1,0:T(8,128)(2,1)} %bitcast.12, ...), custom_call_target="tpu_custom_call" | custom-call | tf_op jit(solution)/shard_map/forward/pallas_call | solution.py:179
  47.3 19.3 %node.1 = (bf16[512,128]{1,0:T(8,128)(2,1)}, bf16[3,512,128]{2,1,0:T(8,128)(2,1)}, f32[512,128]{1,0:T(8,128)}, f32[5,128,128]{2,1,0:T(8,128)}) custom-call(f32[512,128]{1,0:T(8,128)} %get-tuple-element.25.agg_own, bf16[2,512,128]{2,1,0:T(8,128)(2,1)} %get-tuple-element.26.agg_nb, f32[512,128]{1,0:T(8,128)} %get-tuple-element.27.cnt_own, ...), custom_call_target="tpu_custom_call" | custom-call | tf_op jit(solution)/shard_map/node/pallas_call | solution.py:422
  66.7 3.8 %backward.1 = (bf16[8,512,128]{2,1,0:T(8,128)(2,1)}, f32[128,128]{1,0:T(8,128)}) custom-call(s32[16]{0:T(128)} %bitcast.19, s32[16]{0:T(128)} %bitcast.21, s32[1]{0:T(128)} %bitcast.11.tc, s32[32,128]{1,0:T(8,128)} %get-tuple-element.21.most, bf16[16,128,128]{2,1,0:T(8,128)(2,1)} %get-tuple-element.30.rank_t, bf16[32,128,128]{2,1,0:T(8,128)(2,1)} %bitcast.13, ...), custom_call_target="tpu_custom_call" | custom-call | tf_op jit(solution)/shard_map/backward/pallas_call | solution.py:230
  70.5 0.0 copy-start.2
  70.5 53.8 %final.1 = (f32[512,128]{1,0:T(8,128)}, f32[6,128,128]{2,1,0:T(8,128)}) custom-call(bf16[8,512,128]{2,1,0:T(8,128)(2,1)} %get-tuple-element.33.dsend, f32[128,128]{1,0:T(8,128)} %get-tuple-element.34.gsend, f32[5,128,128]{2,1,0:T(8,128)} %get-tuple-element.35.grads, f32[512,128]{1,0:T(8,128)} %get-tuple-element.36.part, bf16[128,128]{1,0:T(8,128)(2,1)} %w_send.3), custom_call_target="tpu_custom_call" | custom-call | tf_op jit(solution)/shard_map/final/pallas_call | solution.py:540
  124.2 0.0 copy-start.1
  124.2 0.0 copy-done.2
  124.3 0.0 copy-start
  124.3 0.7 copy.24
  124.9 0.3 copy-done.1
  125.2 0.7 copy.25
  125.9 0.0 copy-done
  125.9 0.7 copy.26
Async XLA Ops:
  70.5 53.8 %copy-start.2 = (bf16[512,128]{1,0:T(8,128)(2,1)S(1)}, bf16[512,128]{1,0:T(8,128)(2,1)}, u32[]{:S(2)}) copy-start(bf16[512,128]{1,0:T(8,128)(2,1)} %get-tuple-element.42) | copy-start | bytes 393220
  124.2 1.0 copy-start.1
  124.3 1.7 %copy-start = (f32[6,128,128]{2,1,0:T(8,128)S(1)}, f32[6,128,128]{2,1,0:T(8,128)}, u32[]{:S(2)}) copy-start(f32[6,128,128]{2,1,0:T(8,128)} %get-tuple-element.44) | copy-start | bytes 1179652

commit v3 on v2

--- a/solution.py
+++ b/solution.py
@@ -15,7 +15,7 @@
 VM = pl.BlockSpec(memory_space=pltpu.VMEM)
 NX, NY, NZ, ZLO, ZHI = 4, 8, 12, 3, 4
 SLABS = NX * NY * ZLO
-LIMIT = 56 << 20
+LIMIT = 16 << 20
 
 
 class Place:
@@ -188,8 +188,9 @@
     )(ts, tr, tc, most, s_rows, r_rows, rank_r)
 
 
-def backward_kernel(first, more, ts, tr, tc, most, rank_t, s_rows, r_rows, dagg, lat_all, dsend,
-                    gsend, acc):
+def backward_kernel(first, more, ts, tr, tc, most, rank_t, s_rows, r_rows, dagg, lat_all, new_in,
+                    dsend, gsend, new_out, acc):
+    new_out[...] = new_in[...]
     acc[...] = jnp.zeros_like(acc)
     tiles = rank_t.shape[0]
 
@@ -226,16 +227,16 @@
     gsend[...] = g
 
 
-def backward(ts, tr, tc, most, rank_t, s_rows, r_rows, dagg, lat_all, first=18, more=4):
+def backward(ts, tr, tc, most, rank_t, s_rows, r_rows, dagg, lat_all, new_lat, first=18, more=4):
     return pl.pallas_call(
         functools.partial(backward_kernel, first, more),
-        out_shape=[sd((8, 512, 128), BF16), sd((128, 128), F32)],
-        in_specs=[SMEM] * 4 + [VM] * 5,
-        out_specs=[VM] * 2,
+        out_shape=[sd((8, 512, 128), BF16), sd((128, 128), F32), sd((512, 128), BF16)],
+        in_specs=[SMEM] * 4 + [VM] * 6,
+        out_specs=[VM] * 3,
         scratch_shapes=[pltpu.VMEM((32, 128, 128), F32)],
         compiler_params=pltpu.CompilerParams(vmem_limit_bytes=LIMIT),
         name="backward",
-    )(ts, tr, tc, most, rank_t, s_rows, r_rows, dagg, lat_all)
+    )(ts, tr, tc, most, rank_t, s_rows, r_rows, dagg, lat_all, new_lat)
 
 
 GATHER_COPIES = 24
@@ -345,7 +346,7 @@
         gather_kernel,
         out_shape=[sd((8, own, 128), BF16), sd((8, own, 128), BF16), sd((3, own, 128), BF16),
                    ranks, ranks, sd((2 * tiles, 128), jnp.int32)],
-        in_specs=[VM] * 6 + [pl.BlockSpec(memory_space=pl.ANY)],
+        in_specs=[VM] * 6 + [pl.BlockSpec(memory_space=pltpu.HBM)],
         out_specs=[VM] * 6,
         scratch_shapes=[pltpu.VMEM((tiles, 128, 128), jnp.int32), pltpu.VMEM((2 * tiles, 128), F32),
                         pltpu.VMEM((8, 3, own), F32), pltpu.VMEM((2, own, 128), BF16),
@@ -357,68 +358,88 @@
     )(lat, pos, w_send, w_recv, pw, bias, mask)
 
 
-NODE_COPIES = 6
+PIECES = 1
+NODE_COPIES = 4 * PIECES + 2
 
 
 def node_kernel(agg_own, agg_nb, cnt_own, cnt_nb, lat, cot, w_edge_out, w_node_self, w_node_msg,
                 node_bias, w_node_out, gain, w_recv, new_lat, dagg, part, grads, agg_in, cnt_in,
-                send_sem, recv_sem):
+                d_agg, direct, agg_b, message_b, hidden_b, d_update_b, d_pre_b, d_message_b, send_sem,
+                recv_sem):
     me = Place()
     nxt, prv = me.slab(1), me.slab(-1)
     meet([nxt, prv])
     cs = Copies(send_sem, recv_sem)
-    a_prv = cs.start(agg_nb.at[0], agg_in.at[0], prv)
-    a_nxt = cs.start(agg_nb.at[1], agg_in.at[1], nxt)
+    size = lat.shape[0] // PIECES
+    pieces = [pl.ds(p * size, size) for p in range(PIECES)]
+    arrive = []
+    for p in pieces:
+        arrive.append((cs.start(agg_nb.at[0, p], agg_in.at[0, p], prv),
+                       cs.start(agg_nb.at[1, p], agg_in.at[1, p], nxt)))
+    counts, leave = [], []
+    for i, p in enumerate(pieces):
+        latent = lat[p]
+        self_pre = dot(latent, w_node_self[...]) + node_bias[...]
+        c = cot[p].astype(F32)
+        d_normed = c * gain[...]
+        d_centre = d_normed - jnp.mean(d_normed, axis=-1, keepdims=True)
+        for copy in arrive[i]:
+            copy.wait_recv()
+        if i == PIECES - 1:
+            counts = [cs.start(cnt_nb.at[0], cnt_in.at[0], prv),
+                      cs.start(cnt_nb.at[1], cnt_in.at[1], nxt)]
+        aggregate = agg_own[p] + agg_in[0, p].astype(F32) + agg_in[1, p].astype(F32)
+        aggregate_b = aggregate.astype(BF16)
+        message = dot(aggregate_b, w_edge_out[...]).astype(BF16)
+        hidden_pre = self_pre + dot(message, w_node_msg[...])
+        logistic = jax.nn.sigmoid(hidden_pre)
+        hidden = (hidden_pre * logistic).astype(BF16)
+        update = dot(hidden, w_node_out[...])
+        average = jnp.mean(update, axis=-1, keepdims=True)
+        centred = update - average
+        variance = jnp.mean(centred * centred, axis=-1, keepdims=True)
+        inv_std = lax.rsqrt(variance + 1e-05)
+        normed = centred * inv_std
+        d_update = (inv_std * (d_centre - normed * jnp.mean(d_normed * normed, axis=-1, keepdims=True))
+                    ).astype(BF16)
+        d_hidden = dot_t(d_update, w_node_out[...])
+        d_hidden_pre = (d_hidden * logistic * (1.0 + hidden_pre * (1.0 - logistic))).astype(BF16)
+        d_message = dot_t(d_hidden_pre, w_node_msg[...]).astype(BF16)
+        d_aggregate = dot_t(d_message, w_edge_out[...])
+        dagg[1, p] = d_aggregate.astype(BF16)
+        leave.append(cs.start(dagg.at[1, p], dagg.at[0, p], nxt))
+        leave.append(cs.start(dagg.at[1, p], dagg.at[2, p], prv))
+        new_lat[p] = (latent.astype(F32) + normed * gain[...]).astype(BF16)
+        d_agg[p] = d_aggregate
+        agg_b[p] = aggregate_b
+        message_b[p] = message
+        hidden_b[p] = hidden
+        d_update_b[p] = d_update
+        d_pre_b[p] = d_hidden_pre
+        d_message_b[p] = d_message
+        direct[p] = c
     latent = lat[...]
-    self_pre = dot(latent, w_node_self[...]) + node_bias[...]
-    a_prv.wait_recv()
-    a_nxt.wait_recv()
-    c_prv = cs.start(cnt_nb.at[0], cnt_in.at[0], prv)
-    c_nxt = cs.start(cnt_nb.at[1], cnt_in.at[1], nxt)
-    aggregate = agg_own[...] + agg_in[0].astype(F32) + agg_in[1].astype(F32)
-    aggregate_b = aggregate.astype(BF16)
-    message = dot(aggregate_b, w_edge_out[...]).astype(BF16)
-    hidden_pre = self_pre + dot(message, w_node_msg[...])
-    logistic = jax.nn.sigmoid(hidden_pre)
-    hidden = (hidden_pre * logistic).astype(BF16)
-    update = dot(hidden, w_node_out[...])
-    average = jnp.mean(update, axis=-1, keepdims=True)
-    centred = update - average
-    variance = jnp.mean(centred * centred, axis=-1, keepdims=True)
-    inv_std = lax.rsqrt(variance + 1e-05)
-    normed = centred * inv_std
-    new_lat[...] = (latent.astype(F32) + normed * gain[...]).astype(BF16)
-    c = cot[...].astype(F32)
-    d_normed = c * gain[...]
-    d_update = (inv_std * (d_normed - jnp.mean(d_normed, axis=-1, keepdims=True)
-                           - normed * jnp.mean(d_normed * normed, axis=-1, keepdims=True))
-                ).astype(BF16)
-    d_hidden = dot_t(d_update, w_node_out[...])
-    d_hidden_pre = (d_hidden * logistic * (1.0 + hidden_pre * (1.0 - logistic))).astype(BF16)
-    d_message = dot_t(d_hidden_pre, w_node_msg[...]).astype(BF16)
-    d_aggregate = dot_t(d_message, w_edge_out[...])
-    dagg[1] = d_aggregate.astype(BF16)
-    d_nxt = cs.start(dagg.at[1], dagg.at[0], nxt)
-    d_prv = cs.start(dagg.at[1], dagg.at[2], prv)
-    grads[1] = contract(aggregate_b, d_message)
+    d_hidden_pre = d_pre_b[...]
+    grads[1] = contract(agg_b[...], d_message_b[...])
     grads[2] = contract(latent, d_hidden_pre)
-    grads[3] = contract(message, d_hidden_pre)
-    grads[4] = contract(hidden, d_update)
-    direct = c + dot_t(d_hidden_pre, w_node_self[...])
-    c_prv.wait_recv()
-    c_nxt.wait_recv()
+    grads[3] = contract(message_b[...], d_hidden_pre)
+    grads[4] = contract(hidden_b[...], d_update_b[...])
+    base = direct[...] + dot_t(d_hidden_pre, w_node_self[...])
+    for copy in counts:
+        copy.wait_recv()
     count = cnt_own[...] + cnt_in[0].astype(F32) + cnt_in[1].astype(F32)
-    d_recv = (count * d_aggregate).astype(BF16)
+    d_recv = (count * d_agg[...]).astype(BF16)
     grads[0] = contract(latent, d_recv)
-    part[...] = direct + dot_t(d_recv, w_recv[...])
-    d_nxt.wait_recv()
-    d_prv.wait_recv()
+    part[...] = base + dot_t(d_recv, w_recv[...])
+    for copy in leave:
+        copy.wait_recv()
     cs.sent()
 
 
 def node(agg_own, agg_nb, cnt_own, cnt_nb, lat, cot, *weights):
     own = lat.shape[0]
     n = NODE_COPIES
+    rows = pltpu.VMEM((own, 128), BF16)
     return pl.pallas_call(
         node_kernel,
         out_shape=[sd((own, 128), BF16), sd((3, own, 128), BF16), sd((own, 128), F32),
@@ -426,40 +447,54 @@
         in_specs=[VM] * 13,
         out_specs=[VM] * 4,
         scratch_shapes=[pltpu.VMEM((2, own, 128), BF16), pltpu.VMEM((2, own, 128), BF16),
+                        pltpu.VMEM((own, 128), F32), pltpu.VMEM((own, 128), F32),
+                        rows, rows, rows, rows, rows, rows,
                         pltpu.SemaphoreType.DMA((n,)), pltpu.SemaphoreType.DMA((n,))],
-        compiler_params=pltpu.CompilerParams(collective_id=1, has_side_effects=True),
+        compiler_params=pltpu.CompilerParams(collective_id=1, has_side_effects=True,
+                                             vmem_limit_bytes=LIMIT),
         name="node",
     )(agg_own, agg_nb, cnt_own, cnt_nb, lat, cot, *weights)
 
 
-FINAL_COPIES = 43
-
-
-def final_kernel(dsend, gsend, grads, part, w_send, latent_grad, weight_grads, v, in_core, vx, in_x,
-                 vy, in_y, in_z, out_y, out_x, out_core, rs_core, cs_sum, in_ra, in_rb, in_da, in_db,
-                 in_fa, in_fb, fwd_a, fwd_b, vz, send_sem, recv_sem):
+FINAL_COPIES = 49
+
+
+def final_kernel(dsend, gsend, grads, part, w_send, latent_grad, weight_grads, v, in_xc, vy, in_y,
+                 vz, in_z, out_y, out, rs_core, cs_sum, in_ra, in_rb, in_da, in_db, in_fa, in_fb,
+                 fwd_a, fwd_b, ready_y, ready_z, send_sem, recv_sem):
     me = Place()
     own = part.shape[0]
     up, dn, sib = me.member(1), me.member(-1), me.partner()
     core, zh = me.core, me.zh
-    mats = [gsend[...]] + [grads[i] for i in range(5)]
-    zero = jnp.zeros((128, 128), BF16)
-    for i in range(8):
-        v[i // 4, i % 4] = mats[i].astype(BF16) if i < 6 else zero
-    xs = [me.at(x=(me.x + d) % NX) for d in range(1, NX)]
-    ys = [me.at(y=(me.y + d) % NY) for d in range(1, NY)]
-    zs = [me.at(z=(me.z + d) % NZ) for d in range(1, NZ)]
-    meet([sib] + xs + ys + zs)
+    v[pl.ds(0, 128)] = gsend[...].astype(BF16)
+    for i in range(5):
+        v[pl.ds(128 * (i + 1), 128)] = grads[i].astype(BF16)
+    vy[...] = jnp.zeros_like(vy)
+
+    def chunk(c, x):
+        return pl.ds(pl.multiple_of((c * NX + x) * 96, 16), 96)
+
+    def y_peer(d):
+        return me.at(y=(me.y + d + NY) % NY)
+
+    def z_peer(d):
+        return me.at(z=(me.z + d + NZ) % NZ)
+
+    plane = [(dx, dc) for dx in range(NX) for dc in range(2) if dx or dc]
+    spots = [((core + dc) % 2, (me.x + dx) % NX) for dx, dc in plane]
+    peers = [me.at(x=x, core=c) for c, x in spots]
+    meet(peers + [y_peer(d) for d in (1, 2, -1, -2)] + [z_peer(d) for d in (1, 2, 3, -1, -2, -3)])
+    for d in (2, -2):
+        pl.semaphore_signal(ready_y, inc=1, device_id=y_peer(d), device_id_type=MESH)
+    for d in (3, -3):
+        pl.semaphore_signal(ready_z, inc=1, device_id=z_peer(d), device_id_type=MESH)
     cs = Copies(send_sem, recv_sem)
     ha, hb = pl.ds(0, own // 2), pl.ds(own // 2, own // 2)
 
-    ar_core = cs.start(v.at[1 - core], in_core, sib)
+    ar_xc = [cs.start(v.at[chunk(*spots[j])], in_xc.at[j], peers[j]) for j in range(len(peers))]
     order = [2, 1, 3, 0]
     rs = [cs.start(dsend.at[((zh + o) % ZHI) * 2 + 1 - core], rs_core.at[(zh + o) % ZHI], sib)
           for o in order]
-    ar_core.wait_recv()
-    vx[...] = (v[core].astype(F32) + in_core[...].astype(F32)).astype(BF16)
-    ar_x = [cs.start(vx.at[(me.x + d) % NX], in_x.at[d - 1], xs[d - 1]) for d in range(1, NX)]
 
     def chip_sum(i):
         rs[i].wait_recv()
@@ -474,15 +509,17 @@
     db = cs.start(cs_sum.at[ku, hb], in_db, up)
     kd = chip_sum(2)
     da = cs.start(cs_sum.at[kd, ha], in_da, dn)
+
+    for copy in ar_xc:
+        copy.wait_recv()
+    total = v[chunk(core, me.x)].astype(F32)
+    for j in range(len(peers)):
+        total = total + in_xc[j].astype(F32)
+    for q in range(NY):
+        vy[q, pl.ds(0, 12)] = total[12 * q:12 * q + 12].astype(BF16)
+    pl.semaphore_wait(ready_y, 2)
+    ar_y = [cs.start(vy.at[(me.y + d) % NY], in_y.at[d - 1], y_peer(d)) for d in range(1, NY)]
     chip_sum(3)
-
-    for copy in ar_x:
-        copy.wait_recv()
-    total = vx[me.x].astype(F32)
-    for d in range(NX - 1):
-        total = total + in_x[d].astype(F32)
-    vy[...] = total.astype(BF16).reshape(NY, 16, 128)
-    ar_y = [cs.start(vy.at[(me.y + d) % NY], in_y.at[d - 1], ys[d - 1]) for d in range(1, NY)]
 
     for copy in ar_y:
         copy.wait_recv()
@@ -491,7 +528,8 @@
         total = total + in_y[d].astype(F32)
     vz[...] = total.astype(BF16)
     in_z[me.z] = total.astype(BF16)
-    ar_z = [cs.start(vz, in_z.at[me.z], zs[d - 1]) for d in range(1, NZ)]
+    pl.semaphore_wait(ready_z, 2)
+    ar_z = [cs.start(vz, in_z.at[me.z], z_peer(d)) for d in range(1, NZ)]
 
     ra.wait_recv()
     fwd_a[...] = (in_ra[...].astype(F32) + cs_sum[ku, ha].astype(F32)).astype(BF16)
@@ -505,9 +543,8 @@
     total = in_z[0].astype(F32)
     for d in range(1, NZ):
         total = total + in_z[d].astype(F32)
-    mine = pl.ds(pl.multiple_of(me.y * 16, 16), 16)
-    out_y[mine] = total.astype(BF16)
-    ag_y = [cs.start(out_y.at[mine], out_y.at[mine], ys[d - 1]) for d in range(1, NY)]
+    out_y[me.y] = total.astype(BF16)
+    ag_y = [cs.start(out_y.at[me.y], out_y.at[me.y], y_peer(d)) for d in range(1, NY)]
 
     da.wait_recv()
     db.wait_recv()
@@ -520,15 +557,13 @@
 
     for copy in ag_y:
         copy.wait_recv()
-    out_x[me.x] = out_y[...]
-    ag_x = [cs.start(out_y, out_x.at[me.x], xs[d - 1]) for d in range(1, NX)]
-    for copy in ag_x:
-        copy.wait_recv()
-    out_core[core] = out_x[...]
-    ag_core = cs.start(out_x, out_core.at[core], sib)
-    ag_core.wait_recv()
+    mine = chunk(core, me.x)
+    out[mine] = jnp.concatenate([out_y[q].astype(F32)[:12] for q in range(NY)], 0).astype(BF16)
+    ag_xc = [cs.start(out.at[mine], out.at[mine], peer) for peer in peers]
+    for copy in ag_xc:
+        copy.wait_recv()
     for i in range(6):
-        weight_grads[i] = out_core[i // 4, i % 4].astype(F32)
+        weight_grads[i] = out[pl.ds(128 * i, 128)].astype(F32)
     cs.sent()
 
 
@@ -543,13 +578,13 @@
         in_specs=[VM] * 5,
         out_specs=[VM] * 2,
         scratch_shapes=[
-            b(2, NX, 128, 128), b(NX, 128, 128), b(NX, 128, 128), b(NX - 1, 128, 128),
-            b(NY, 16, 128), b(NY - 1, 16, 128), b(NZ, 16, 128), b(128, 128),
-            b(NX, 128, 128), b(2, NX, 128, 128), b(ZHI, own, 128), b(ZHI, own, 128),
+            b(768, 128), b(2 * NX - 1, 96, 128), b(NY, 16, 128), b(NY - 1, 16, 128), b(16, 128),
+            b(NZ, 16, 128), b(NY, 16, 128), b(768, 128), b(ZHI, own, 128), b(ZHI, own, 128),
             b(h, 128), b(h, 128), b(h, 128), b(h, 128), b(h, 128), b(h, 128), b(h, 128), b(h, 128),
-            b(16, 128),
+            pltpu.SemaphoreType.REGULAR, pltpu.SemaphoreType.REGULAR,
             pltpu.SemaphoreType.DMA((n,)), pltpu.SemaphoreType.DMA((n,))],
-        compiler_params=pltpu.CompilerParams(collective_id=2, has_side_effects=True),
+        compiler_params=pltpu.CompilerParams(collective_id=2, has_side_effects=True,
+                                             vmem_limit_bytes=LIMIT),
         name="final",
     )(dsend, gsend, grads, part, w_send)
 
@@ -565,8 +600,8 @@
     new_latent, dagg, part, grads = node(
         agg_own, agg_nb, cnt_own, cnt_nb, latent, cotangent, w_edge_out, w_node_self, w_node_msg,
         node_bias[None], w_node_out, gain[None], w_recv)
-    dsend, gsend = backward(ts, tr, tc, most, rank_t, s_rows, r_rows, dagg.reshape(12, 128, 128),
-                            lat_all)
+    dsend, gsend, new_latent = backward(ts, tr, tc, most, rank_t, s_rows, r_rows, dagg.reshape(12, 128, 128),
+                            lat_all, new_latent)
     latent_grad, weight_grads = final(dsend, gsend, grads, part, w_send)
     return new_latent, latent_grad, weight_grads
 

time: 127 us -> 116 us (0.913)
  Pallas kernels: 123 us -> 107 us
  local copies, waits for them, and re-layouts: 2.43 us -> 7.07 us
    pallas_call x1, Pallas kernels: 53.8 us -> 44.9 us  [final(): pl.pallas_call(final_kernel, out_shape=[sd((own, 128), F32), sd((6, 128,...]
    unnamed x9 -> x38, local copies, waits for them, and re-layouts: 2.43 us -> 7.07 us
    pallas_call x1, Pallas kernels: 42.9 us -> 40.3 us  [gather(): pl.pallas_call(gather_kernel, out_shape=[sd((8, own, 128), BF16), sd((8,...]
    pallas_call x1, Pallas kernels: 3.13 us -> 1.53 us  [forward(): pl.pallas_call(functools.partial(forward_kernel, first, more), out_shape=...]
    pallas_call x1, Pallas kernels: 3.81 us -> 2.4 us  [backward(): pl.pallas_call(functools.partial(backward_kernel, first, more), out_shape...]
    pallas_call x1, Pallas kernels: 19.3 us -> 18 us  [node(): pl.pallas_call(node_kernel, out_shape=[sd((own, 128), BF16), sd((3, own,...]
where the time goes in v3:
time: 116 us
  Pallas kernels  107 us (92%)
  local copies, waits for them, and re-layouts  7.07 us (6%)
  between operations  1.45 us (1%)
    pallas_call x1, Pallas kernels, final(): pl.pallas_call(final_kernel, out_shape=[sd((own, 128), F32), sd((6, 128,...  44.9 us
    pallas_call x1, Pallas kernels, gather(): pl.pallas_call(gather_kernel, out_shape=[sd((8, own, 128), BF16), sd((8,...  40.3 us
    pallas_call x1, Pallas kernels, node(): pl.pallas_call(node_kernel, out_shape=[sd((own, 128), BF16), sd((3, own,...  18 us
    unnamed x38, local copies, waits for them, and re-layouts  7.07 us
    pallas_call x1, Pallas kernels, backward(): pl.pallas_call(functools.partial(backward_kernel, first, more), out_shape...  2.4 us

profile of v3, /device:TPU:1, one launch (start us, length us, event | category | flops | bytes accessed | tf_op | source)
XLA Modules:
  0.0 115.6 jit_solution(8086834542140793124)
XLA Ops:
  1.3 0.0 copy-start.11
  1.3 0.0 copy-start.12
  1.3 0.0 copy-start.17
  1.3 0.7 copy-done.11
  2.0 0.0 copy-done.12
  2.0 0.0 copy-done.17
  2.0 0.0 copy-start
  2.0 1.2 %copy-done = s32[1,1,16,128,128]{4,3,2,1,0:T(8,128)S(1)} copy-done((s32[1,1,16,128,128]{4,3,2,1,0:T(8,128)S(1)}, s32[1,1,16,128,128]{4,3,2,1,0:T(8,128)}, u32[]{:S(2)}) %copy-start) | copy-done | bytes 1048600
  3.2 0.0 copy-start.1
  3.2 0.9 copy-done.1
  4.1 0.0 copy-start.3
  4.1 0.8 copy-done.3
  4.9 0.0 copy-start.5
  4.9 0.8 copy-done.5
  5.6 40.3 %gather.1 = (bf16[8,512,128]{2,1,0:T(8,128)(2,1)S(1)}, bf16[8,512,128]{2,1,0:T(8,128)(2,1)S(1)}, bf16[3,512,128]{2,1,0:T(8,128)(2,1)S(1)}, bf16[16,128,128]{2,1,...) custom-call(bf16[512,128]{1,0:T(8,128)(2,1)S(1)} %copy-done.1, f32[3,512]{1,0:T(4,128)S(1)} %copy-done.11, ...), custom_call_target="tpu_custom_call" | custom-call | tf_op jit(solution)/shard_map/gather/pallas_call | solution.py:345
  45.9 0.0 copy-start.13
  45.9 0.0 copy-start.14
  46.0 0.6 copy-done.13
  46.6 0.0 copy-done.14
  46.6 0.0 copy-start.2
  46.6 0.0 copy-start.4
  46.6 0.0 copy-start.7
  46.6 0.0 copy-start.8
  46.6 0.0 copy-start.9
  46.6 0.0 copy-start.10
  46.6 1.5 %forward.1 = (f32[512,128]{1,0:T(8,128)S(1)}, bf16[2,512,128]{2,1,0:T(8,128)(2,1)S(1)}, f32[512,128]{1,0:T(8,128)S(1)}, bf16[2,512,128]{2,1,0:T(8,128)(2,1)S(1)}) custom-call(s32[16]{0:T(128)S(1)} %bitcast.18, s32[16]{0:T(128)S(1)} %bitcast.20, s32[1]{0:T(128)} %bitcast.10.tc, s32[32,128]{1,0:T(8,128)S(1)} %get-tuple-element.22.most, ...), custom_call_target="tpu_custom_call" | custom-call | tf_op jit(solution)/shard_map/forward/pallas_call | solution.py:179
  48.2 0.0 copy-start.15
  48.2 0.0 copy-start.16
  48.2 0.0 copy-done.2
  48.2 0.0 copy-done.4
  48.2 0.0 copy-done.7
  48.2 0.0 copy-done.8
  48.2 0.0 copy-done.9
  48.3 0.0 copy-done.10
  48.3 0.6 copy-done.15
  48.8 0.0 copy-done.16
  48.9 18.0 %node.1 = (bf16[512,128]{1,0:T(8,128)(2,1)S(1)}, bf16[3,512,128]{2,1,0:T(8,128)(2,1)S(1)}, f32[512,128]{1,0:T(8,128)S(1)}, f32[5,128,128]{2,1,0:T(8,128)S(1)}) custom-call(f32[512,128]{1,0:T(8,128)S(1)} %get-tuple-element.27.agg_own, bf16[2,512,128]{2,1,0:T(8,128)(2,1)S(1)} %get-tuple-element.28.agg_nb, f32[512,128]{1,0:T(8,128)S(1)} %get-tuple-element.29.cnt_own, ...), custom_call_target="tpu_custom_call" | custom-call | tf_op jit(solution)/shard_map/node/pallas_call | solution.py:443
  66.9 0.0 copy-start.6
  66.9 2.4 %backward.1 = (bf16[8,512,128]{2,1,0:T(8,128)(2,1)S(1)}, f32[128,128]{1,0:T(8,128)S(1)}, bf16[512,128]{1,0:T(8,128)(2,1)}) custom-call(s32[16]{0:T(128)S(1)} %bitcast.19, s32[16]{0:T(128)S(1)} %bitcast.21, s32[1]{0:T(128)} %bitcast.11.tc, s32[32,128]{1,0:T(8,128)S(1)} %get-tuple-element.22.most, bf16[16,128,128]{2,1,0:T(8,128)(2,1)S(1)} %get-tuple-element.23.rank_t, ...), custom_call_target="tpu_custom_call" | custom-call | tf_op jit(solution)/shard_map/backward/pallas_call | solution.py:231
  69.3 0.0 copy-done.6
  69.3 44.9 %final.1 = (f32[512,128]{1,0:T(8,128)S(1)}, f32[6,128,128]{2,1,0:T(8,128)S(1)}) custom-call(bf16[8,512,128]{2,1,0:T(8,128)(2,1)S(1)} %get-tuple-element.35.dsend, f32[128,128]{1,0:T(8,128)S(1)} %get-tuple-element.36.gsend, f32[5,128,128]{2,1,0:T(8,128)S(1)} %get-tuple-element.37.grads, f32[512,128]{1,0:T(8,128)S(1)} %get-tuple-element.38.part, ...), custom_call_target="tpu_custom_call" | custom-call | tf_op jit(solution)/shard_map/final/pallas_call | solution.py:575
  114.2 0.7 copy.23
  114.9 0.7 copy.24
Async XLA Ops:
  1.3 0.7 copy-start.11
  1.3 0.7 copy-start.12
  1.3 0.7 copy-start.17
  2.0 1.2 %copy-start = (s32[1,1,16,128,128]{4,3,2,1,0:T(8,128)S(1)}, s32[1,1,16,128,128]{4,3,2,1,0:T(8,128)}, u32[]{:S(2)}) copy-start(s32[1,1,16,128,128]{4,3,2,1,0:T(8,128)} %param.21) | copy-start | bytes 3145732
  3.2 0.9 copy-start.1
  4.1 0.8 copy-start.3
  4.9 0.8 copy-start.5
  45.9 0.7 copy-start.13
  45.9 0.7 copy-start.14
  46.6 1.6 %copy-start.2 = (bf16[512,128]{1,0:T(8,128)(2,1)S(1)}, bf16[512,128]{1,0:T(8,128)(2,1)}, u32[]{:S(2)}) copy-start(bf16[512,128]{1,0:T(8,128)(2,1)} %cot.1) | copy-start | bytes 393220
  46.6 1.6 %copy-start.4 = (bf16[128,128]{1,0:T(8,128)(2,1)S(1)}, bf16[128,128]{1,0:T(8,128)(2,1)}, u32[]{:S(2)}) copy-start(bf16[128,128]{1,0:T(8,128)(2,1)} %w_recv.3) | copy-start | bytes 98308
  46.6 1.6 %copy-start.7 = (bf16[128,128]{1,0:T(8,128)(2,1)S(1)}, bf16[128,128]{1,0:T(8,128)(2,1)}, u32[]{:S(2)}) copy-start(bf16[128,128]{1,0:T(8,128)(2,1)} %w_edge_out.1) | copy-start | bytes 98308
  46.6 1.6 %copy-start.8 = (bf16[128,128]{1,0:T(8,128)(2,1)S(1)}, bf16[128,128]{1,0:T(8,128)(2,1)}, u32[]{:S(2)}) copy-start(bf16[128,128]{1,0:T(8,128)(2,1)} %w_node_self.1) | copy-start | bytes 98308
  46.6 1.6 %copy-start.9 = (bf16[128,128]{1,0:T(8,128)(2,1)S(1)}, bf16[128,128]{1,0:T(8,128)(2,1)}, u32[]{:S(2)}) copy-start(bf16[128,128]{1,0:T(8,128)(2,1)} %w_node_msg.1) | copy-start | bytes 98308
  46.6 1.6 %copy-start.10 = (bf16[128,128]{1,0:T(8,128)(2,1)S(1)}, bf16[128,128]{1,0:T(8,128)(2,1)}, u32[]{:S(2)}) copy-start(bf16[128,128]{1,0:T(8,128)(2,1)} %w_node_out.1) | copy-start | bytes 98308
  48.2 0.7 copy-start.15
  48.2 0.7 copy-start.16
  66.9 2.4 %copy-start.6 = (bf16[128,128]{1,0:T(8,128)(2,1)S(1)}, bf16[128,128]{1,0:T(8,128)(2,1)}, u32[]{:S(2)}) copy-start(bf16[128,128]{1,0:T(8,128)(2,1)} %w_send.3) | copy-start | bytes 98308

commit v4 on v3

--- a/solution.py
+++ b/solution.py
@@ -13,6 +13,7 @@
 MESH = pl.DeviceIdType.MESH
 SMEM = pl.BlockSpec(memory_space=pltpu.SMEM)
 VM = pl.BlockSpec(memory_space=pltpu.VMEM)
+HBM = pl.BlockSpec(memory_space=pltpu.HBM)
 NX, NY, NZ, ZLO, ZHI = 4, 8, 12, 3, 4
 SLABS = NX * NY * ZLO
 LIMIT = 16 << 20
@@ -69,6 +70,17 @@
     def sent(self):
         for copy in self.started:
             copy.wait_send()
+
+
+def fetch(pairs, sem):
+    copies = [pltpu.make_async_copy(src, dst, sem.at[i]) for i, (src, dst) in enumerate(pairs)]
+    for copy in copies:
+        copy.start()
+    return copies
+
+
+def in_hbm(*arrays):
+    return [pltpu.with_memory_space_constraint(a, pltpu.HBM) for a in arrays]
 
 
 def sd(shape, dtype):
@@ -242,13 +254,15 @@
 GATHER_COPIES = 24
 
 
-def gather_kernel(lat, pos, w_send, w_recv, pw, bias, mask_in, lat_all, s_rows, r_rows, rank_r,
-                  rank_t, most, mask, top, pos_all, lat_nb, pos_nb, mask_sem, send_sem, recv_sem):
-    load = pltpu.make_async_copy(mask_in, mask, mask_sem)
-    load.start()
+def gather_kernel(lat, pos, w_send_in, w_recv_in, pw_in, bias_in, mask_in, ts_in, tr_in, tc_in,
+                  lat_all, s_rows, r_rows, rank_r, rank_t, most, ts, tr, tc, mask, top, pos_all,
+                  lat_nb, pos_nb, w_send, w_recv, pw, bias, load_sem, send_sem, recv_sem):
     me = Place()
     own = lat.shape[0]
     g = me.grp
+    loads = fetch([(lat, lat_all.at[g]), (pos, pos_all.at[g]), (w_send_in, w_send),
+                   (w_recv_in, w_recv), (pw_in, pw), (bias_in, bias), (mask_in, mask), (ts_in, ts),
+                   (tr_in, tr), (tc_in, tc)], load_sem)
     up, dn, sib = me.member(1), me.member(-1), me.partner()
     nxt, prv = me.slab(1), me.slab(-1)
     meet([up, dn, sib, nxt, prv])
@@ -274,8 +288,6 @@
         cs.start(lat, lat_all.at[g], sib),
         cs.start(pos, pos_all.at[g], sib),
     ]
-    lat_all[g] = lat[...]
-    pos_all[g] = pos[...]
     iu, idn, far = up[1], dn[1], me.member(2)[1]
 
     def pass_on(ref):
@@ -292,9 +304,10 @@
     def other(index):
         return (index // 2) * 2 + 1 - me.core
 
-    recv_rows(1, lat[...], pos[...])
+    for load in loads:
+        load.wait()
+    recv_rows(1, lat_all[g], pos_all[g])
     send_rows(g)
-    load.wait()
     rank_tiles(mask, rank_r, rank_t, top)
     most[...] = slot_counts(top)
 
@@ -337,7 +350,7 @@
     cs.sent()
 
 
-def gather(lat, pos, w_send, w_recv, pw, bias, mask):
+def gather(lat, pos, w_send, w_recv, pw, bias, mask, ts, tr, tc):
     own = lat.shape[0]
     n = GATHER_COPIES
     tiles = mask.shape[0]
@@ -345,17 +358,20 @@
     return pl.pallas_call(
         gather_kernel,
         out_shape=[sd((8, own, 128), BF16), sd((8, own, 128), BF16), sd((3, own, 128), BF16),
-                   ranks, ranks, sd((2 * tiles, 128), jnp.int32)],
-        in_specs=[VM] * 6 + [pl.BlockSpec(memory_space=pltpu.HBM)],
-        out_specs=[VM] * 6,
+                   ranks, ranks, sd((2 * tiles, 128), jnp.int32), sd((tiles,), jnp.int32),
+                   sd((tiles,), jnp.int32), sd((1,), jnp.int32)],
+        in_specs=[HBM] * 10,
+        out_specs=[VM] * 9,
         scratch_shapes=[pltpu.VMEM((tiles, 128, 128), jnp.int32), pltpu.VMEM((2 * tiles, 128), F32),
                         pltpu.VMEM((8, 3, own), F32), pltpu.VMEM((2, own, 128), BF16),
-                        pltpu.VMEM((2, 3, own), F32), pltpu.SemaphoreType.DMA(()),
+                        pltpu.VMEM((2, 3, own), F32), pltpu.VMEM((128, 128), BF16),
+                        pltpu.VMEM((128, 128), BF16), pltpu.VMEM((3, 128), F32),
+                        pltpu.VMEM((1, 128), F32), pltpu.SemaphoreType.DMA((10,)),
                         pltpu.SemaphoreType.DMA((n,)), pltpu.SemaphoreType.DMA((n,))],
         compiler_params=pltpu.CompilerParams(collective_id=0, has_side_effects=True,
                                              vmem_limit_bytes=LIMIT),
         name="gather",
-    )(lat, pos, w_send, w_recv, pw, bias, mask)
+    )(*in_hbm(lat, pos, w_send, w_recv, pw, bias, mask, ts, tr), tc)
 
 
 PIECES = 1
@@ -363,9 +379,10 @@
 
 
 def node_kernel(agg_own, agg_nb, cnt_own, cnt_nb, lat, cot, w_edge_out, w_node_self, w_node_msg,
-                node_bias, w_node_out, gain, w_recv, new_lat, dagg, part, grads, agg_in, cnt_in,
-                d_agg, direct, agg_b, message_b, hidden_b, d_update_b, d_pre_b, d_message_b, send_sem,
-                recv_sem):
+                node_bias_in, w_node_out, gain_in, w_recv, new_lat, dagg, part, grads, agg_in, cnt_in,
+                d_agg, direct, agg_b, message_b, hidden_b, d_update_b, d_pre_b, d_message_b,
+                node_bias, gain, load_sem, send_sem, recv_sem):
+    loads = fetch([(node_bias_in, node_bias), (gain_in, gain)], load_sem)
     me = Place()
     nxt, prv = me.slab(1), me.slab(-1)
     meet([nxt, prv])
@@ -377,6 +394,8 @@
         arrive.append((cs.start(agg_nb.at[0, p], agg_in.at[0, p], prv),
                        cs.start(agg_nb.at[1, p], agg_in.at[1, p], nxt)))
     counts, leave = [], []
+    for load in loads:
+        load.wait()
     for i, p in enumerate(pieces):
         latent = lat[p]
         self_pre = dot(latent, w_node_self[...]) + node_bias[...]
@@ -444,11 +463,12 @@
         node_kernel,
         out_shape=[sd((own, 128), BF16), sd((3, own, 128), BF16), sd((own, 128), F32),
                    sd((5, 128, 128), F32)],
-        in_specs=[VM] * 13,
+        in_specs=[VM] * 9 + [HBM, VM, HBM, VM],
         out_specs=[VM] * 4,
         scratch_shapes=[pltpu.VMEM((2, own, 128), BF16), pltpu.VMEM((2, own, 128), BF16),
                         pltpu.VMEM((own, 128), F32), pltpu.VMEM((own, 128), F32),
-                        rows, rows, rows, rows, rows, rows,
+                        rows, rows, rows, rows, rows, rows, pltpu.VMEM((1, 128), F32),
+                        pltpu.VMEM((1, 128), F32), pltpu.SemaphoreType.DMA((2,)),
                         pltpu.SemaphoreType.DMA((n,)), pltpu.SemaphoreType.DMA((n,))],
         compiler_params=pltpu.CompilerParams(collective_id=1, has_side_effects=True,
                                              vmem_limit_bytes=LIMIT),
@@ -531,6 +551,14 @@
     pl.semaphore_wait(ready_z, 2)
     ar_z = [cs.start(vz, in_z.at[me.z], z_peer(d)) for d in range(1, NZ)]
 
+    for copy in ar_z:
+        copy.wait_recv()
+    total = in_z[0].astype(F32)
+    for d in range(1, NZ):
+        total = total + in_z[d].astype(F32)
+    out_y[me.y] = total.astype(BF16)
+    ag_y = [cs.start(out_y.at[me.y], out_y.at[me.y], y_peer(d)) for d in range(1, NY)]
+
     ra.wait_recv()
     fwd_a[...] = (in_ra[...].astype(F32) + cs_sum[ku, ha].astype(F32)).astype(BF16)
     fa = cs.start(fwd_a, in_fa, up)
@@ -538,14 +566,11 @@
     fwd_b[...] = (in_rb[...].astype(F32) + cs_sum[kd, hb].astype(F32)).astype(BF16)
     fb = cs.start(fwd_b, in_fb, dn)
 
-    for copy in ar_z:
-        copy.wait_recv()
-    total = in_z[0].astype(F32)
-    for d in range(1, NZ):
-        total = total + in_z[d].astype(F32)
-    out_y[me.y] = total.astype(BF16)
-    ag_y = [cs.start(out_y.at[me.y], out_y.at[me.y], y_peer(d)) for d in range(1, NY)]
-
+    for copy in ag_y:
+        copy.wait_recv()
+    mine = chunk(core, me.x)
+    out[mine] = jnp.concatenate([out_y[q].astype(F32)[:12] for q in range(NY)], 0).astype(BF16)
+    ag_xc = [cs.start(out.at[mine], out.at[mine], peer) for peer in peers]
     da.wait_recv()
     db.wait_recv()
     fa.wait_recv()
@@ -555,11 +580,6 @@
     d_b = cs_sum[zh, hb].astype(F32) + in_db[...].astype(F32) + in_fb[...].astype(F32)
     latent_grad[hb] = part[hb] + dot_t(d_b.astype(BF16), w_send[...])
 
-    for copy in ag_y:
-        copy.wait_recv()
-    mine = chunk(core, me.x)
-    out[mine] = jnp.concatenate([out_y[q].astype(F32)[:12] for q in range(NY)], 0).astype(BF16)
-    ag_xc = [cs.start(out.at[mine], out.at[mine], peer) for peer in peers]
     for copy in ag_xc:
         copy.wait_recv()
     for i in range(6):
@@ -589,20 +609,37 @@
     )(dsend, gsend, grads, part, w_send)
 
 
+def finish_kernel(a, b, a_out, b_out, sem):
+    for copy in fetch([(a, a_out), (b, b_out)], sem):
+        copy.wait()
+
+
+def finish(a, b):
+    return pl.pallas_call(
+        finish_kernel,
+        out_shape=[sd(a.shape, a.dtype), sd(b.shape, b.dtype)],
+        in_specs=[VM] * 2,
+        out_specs=[HBM] * 2,
+        scratch_shapes=[pltpu.SemaphoreType.DMA((2,))],
+        compiler_params=pltpu.CompilerParams(vmem_limit_bytes=LIMIT),
+        name="finish",
+    )(a, b)
+
+
 def body(latent, positions, tile_send, tile_recv, tile_mask, tile_count, w_send, w_recv, pos_weight,
          edge_bias, w_edge_out, w_node_self, w_node_msg, node_bias, w_node_out, gain, cotangent):
     ts, tr, tc = tile_send[0, 0], tile_recv[0, 0], tile_count[0]
-    lat_all, s_rows, r_rows, rank_r, rank_t, most = gather(
-        latent, positions, w_send, w_recv, pos_weight, edge_bias[None], tile_mask[0, 0])
+    lat_all, s_rows, r_rows, rank_r, rank_t, most, ts, tr, tc = gather(
+        latent, positions, w_send, w_recv, pos_weight, edge_bias[None], tile_mask[0, 0], ts, tr, tc)
     s_rows = s_rows.reshape(32, 128, 128)
     r_rows = r_rows.reshape(12, 128, 128)
     agg_own, agg_nb, cnt_own, cnt_nb = forward(ts, tr, tc, most, s_rows, r_rows, rank_r)
     new_latent, dagg, part, grads = node(
         agg_own, agg_nb, cnt_own, cnt_nb, latent, cotangent, w_edge_out, w_node_self, w_node_msg,
-        node_bias[None], w_node_out, gain[None], w_recv)
+        *in_hbm(node_bias[None]), w_node_out, *in_hbm(gain[None]), w_recv)
     dsend, gsend, new_latent = backward(ts, tr, tc, most, rank_t, s_rows, r_rows, dagg.reshape(12, 128, 128),
                             lat_all, new_latent)
-    latent_grad, weight_grads = final(dsend, gsend, grads, part, w_send)
+    latent_grad, weight_grads = finish(*final(dsend, gsend, grads, part, w_send))
     return new_latent, latent_grad, weight_grads
 
 

time: 116 us -> 112 us (0.966)
  local copies, waits for them, and re-layouts: 7.07 us -> 0.05 us
  Pallas kernels: 107 us -> 111 us
    unnamed x38 -> x16, local copies, waits for them, and re-layouts: 7.07 us -> 0.05 us
    pallas_call x1, Pallas kernels: 44.9 us -> 47.1 us  [final(): pl.pallas_call(final_kernel, out_shape=[sd((own, 128), F32), sd((6, 128,...]
    pallas_call x1, Pallas kernels: 18 us -> 16.3 us  [node(): pl.pallas_call(node_kernel, out_shape=[sd((own, 128), BF16), sd((3, own,...]
where the time goes in v4:
time: 112 us
  Pallas kernels  111 us (99%)
  between operations  1.43 us (1%)
    pallas_call x1, Pallas kernels, final(): pl.pallas_call(final_kernel, out_shape=[sd((own, 128), F32), sd((6, 128,...  47.1 us
    pallas_call x1, Pallas kernels, gather(): pl.pallas_call(gather_kernel, out_shape=[sd((8, own, 128), BF16), sd((8,...  41 us
    pallas_call x1, Pallas kernels, node(): pl.pallas_call(node_kernel, out_shape=[sd((own, 128), BF16), sd((3, own,...  16.3 us
    pallas_call x1, Pallas kernels, backward(): pl.pallas_call(functools.partial(backward_kernel, first, more), out_shape...  2.98 us

profile of v4, /device:TPU:1, one launch (start us, length us, event | category | flops | bytes accessed | tf_op | source)
XLA Modules:
  0.0 112.0 jit_solution(17971785869888318010)
XLA Ops:
  1.3 41.0 %gather.1 = (bf16[8,512,128]{2,1,0:T(8,128)(2,1)S(1)}, bf16[8,512,128]{2,1,0:T(8,128)(2,1)S(1)}, bf16[3,512,128]{2,1,0:T(8,128)(2,1)S(1)}, bf16[16,128,128]{2,1,...) custom-call(bf16[512,128]{1,0:T(8,128)(2,1)} %lat.3, ...), custom_call_target="tpu_custom_call" | custom-call | tf_op jit(solution)/shard_map/gather/pallas_call | solution.py:358
  42.3 0.0 copy-start
  42.3 0.0 copy-start.1
  42.4 0.0 copy-start.2
  42.4 0.0 copy-start.4
  42.4 0.0 copy-start.5
  42.4 0.0 copy-start.6
  42.4 0.0 copy-start.7
  42.4 2.2 %forward.1 = (f32[512,128]{1,0:T(8,128)S(1)}, bf16[2,512,128]{2,1,0:T(8,128)(2,1)S(1)}, f32[512,128]{1,0:T(8,128)S(1)}, bf16[2,512,128]{2,1,0:T(8,128)(2,1)S(1)}) custom-call(s32[16]{0:T(128)S(1)} %get-tuple-element.27.ts, s32[16]{0:T(128)S(1)} %get-tuple-element.28.tr, s32[1]{0:T(128)} %get-tuple-element.29.tc, s32[32,128]{1,0:T(8,128)S(1)} %get-tuple-element.30.most, ...), custom_call_target="tpu_custom_call" | custom-call | tf_op jit(solution)/shard_map/forward/pallas_call | solution.py:191
  44.6 0.0 copy-done
  44.6 0.0 copy-done.1
  44.6 0.0 copy-done.2
  44.6 0.0 copy-done.4
  44.7 0.0 copy-done.5
  44.7 0.0 copy-done.6
  44.7 0.0 copy-done.7
  44.7 16.3 %node.1 = (bf16[512,128]{1,0:T(8,128)(2,1)S(1)}, bf16[3,512,128]{2,1,0:T(8,128)(2,1)S(1)}, f32[512,128]{1,0:T(8,128)S(1)}, f32[5,128,128]{2,1,0:T(8,128)S(1)}) custom-call(f32[512,128]{1,0:T(8,128)S(1)} %get-tuple-element.35.agg_own, bf16[2,512,128]{2,1,0:T(8,128)(2,1)S(1)} %get-tuple-element.36.agg_nb, f32[512,128]{1,0:T(8,128)S(1)} %get-tuple-element.37.cnt_own, ...), custom_call_target="tpu_custom_call" | custom-call | tf_op jit(solution)/shard_map/node/pallas_call | solution.py:462
  61.0 0.0 copy-start.3
  61.0 3.0 %backward.1 = (bf16[8,512,128]{2,1,0:T(8,128)(2,1)S(1)}, f32[128,128]{1,0:T(8,128)S(1)}, bf16[512,128]{1,0:T(8,128)(2,1)}) custom-call(s32[16]{0:T(128)S(1)} %get-tuple-element.27.ts, s32[16]{0:T(128)S(1)} %get-tuple-element.28.tr, s32[1]{0:T(128)} %get-tuple-element.29.tc, s32[32,128]{1,0:T(8,128)S(1)} %get-tuple-element.30.most, ...), custom_call_target="tpu_custom_call" | custom-call | tf_op jit(solution)/shard_map/backward/pallas_call | solution.py:243
  64.0 0.0 copy-done.3
  64.0 47.1 %final.1 = (f32[512,128]{1,0:T(8,128)S(1)}, f32[6,128,128]{2,1,0:T(8,128)S(1)}) custom-call(bf16[8,512,128]{2,1,0:T(8,128)(2,1)S(1)} %get-tuple-element.43.dsend, f32[128,128]{1,0:T(8,128)S(1)} %get-tuple-element.44.gsend, f32[5,128,128]{2,1,0:T(8,128)S(1)} %get-tuple-element.45.grads, f32[512,128]{1,0:T(8,128)S(1)} %get-tuple-element.46.part, ...), custom_call_target="tpu_custom_call" | custom-call | tf_op jit(solution)/shard_map/final/pallas_call | solution.py:595
  111.2 0.9 finish.1
Async XLA Ops:
  42.3 2.3 %copy-start = (bf16[512,128]{1,0:T(8,128)(2,1)S(1)}, bf16[512,128]{1,0:T(8,128)(2,1)}, u32[]{:S(2)}) copy-start(bf16[512,128]{1,0:T(8,128)(2,1)} %lat.3) | copy-start | bytes 393220
  42.3 2.3 %copy-start.1 = (bf16[512,128]{1,0:T(8,128)(2,1)S(1)}, bf16[512,128]{1,0:T(8,128)(2,1)}, u32[]{:S(2)}) copy-start(bf16[512,128]{1,0:T(8,128)(2,1)} %cot.1) | copy-start | bytes 393220
  42.4 2.3 %copy-start.2 = (bf16[128,128]{1,0:T(8,128)(2,1)S(1)}, bf16[128,128]{1,0:T(8,128)(2,1)}, u32[]{:S(2)}) copy-start(bf16[128,128]{1,0:T(8,128)(2,1)} %w_recv.1) | copy-start | bytes 98308
  42.4 2.3 %copy-start.4 = (bf16[128,128]{1,0:T(8,128)(2,1)S(1)}, bf16[128,128]{1,0:T(8,128)(2,1)}, u32[]{:S(2)}) copy-start(bf16[128,128]{1,0:T(8,128)(2,1)} %w_edge_out.1) | copy-start | bytes 98308
  42.4 2.3 %copy-start.5 = (bf16[128,128]{1,0:T(8,128)(2,1)S(1)}, bf16[128,128]{1,0:T(8,128)(2,1)}, u32[]{:S(2)}) copy-start(bf16[128,128]{1,0:T(8,128)(2,1)} %w_node_self.1) | copy-start | bytes 98308
  42.4 2.3 %copy-start.6 = (bf16[128,128]{1,0:T(8,128)(2,1)S(1)}, bf16[128,128]{1,0:T(8,128)(2,1)}, u32[]{:S(2)}) copy-start(bf16[128,128]{1,0:T(8,128)(2,1)} %w_node_msg.1) | copy-start | bytes 98308
  42.4 2.3 %copy-start.7 = (bf16[128,128]{1,0:T(8,128)(2,1)S(1)}, bf16[128,128]{1,0:T(8,128)(2,1)}, u32[]{:S(2)}) copy-start(bf16[128,128]{1,0:T(8,128)(2,1)} %w_node_out.1) | copy-start | bytes 98308
  61.0 3.0 %copy-start.3 = (bf16[128,128]{1,0:T(8,128)(2,1)S(1)}, bf16[128,128]{1,0:T(8,128)(2,1)}, u32[]{:S(2)}) copy-start(bf16[128,128]{1,0:T(8,128)(2,1)} %w_send.1) | copy-start | bytes 98308

commit v5 on v4

--- a/solution.py
+++ b/solution.py
@@ -116,10 +116,10 @@
     def tile(t, _):
         values = mask[t].astype(F32)
         by_row = ranks(values)
-        rank_r[t] = by_row.astype(BF16)
+        rank_r[t] = by_row
         top[pl.ds(t, 1), :] = jnp.max(by_row, axis=0, keepdims=True)
         by_col = ranks(values.T)
-        rank_t[t] = by_col.astype(BF16)
+        rank_t[t] = by_col
         top[pl.ds(t + tiles, 1), :] = jnp.max(by_col, axis=0, keepdims=True)
         return 0
 
@@ -140,39 +140,46 @@
     return jnp.where(ranks == slot, one, none)
 
 
-def forward_kernel(first, more, ts, tr, tc, most, s_rows, r_rows, rank_r, agg_own, agg_nb, cnt_own,
-                   cnt_nb, agg, cnt):
+def slot_batches(first, group):
+    return [range(k, min(k + group, first)) for k in range(0, first, group)]
+
+
+def forward_kernel(first, more, group, ts, tr, tc, most, s_rows, r_rows, rank_r, agg_own, agg_nb,
+                   cnt_own, cnt_nb, agg, cnt):
     agg[...] = jnp.zeros_like(agg)
     cnt[...] = jnp.zeros_like(cnt)
     ones = jnp.ones((128, 128), BF16)
+    none = jnp.zeros((), BF16)
 
     def tile(t, _):
         rb = tr[t]
         s = s_rows[ts[t]]
-        rk = rank_r[t]
+        rk = rank_r[t].astype(BF16)
         floor = -(r_rows[rb].astype(F32))
-
-        def add(slot, a, c):
-            x = dot(picks(rk, slot), s)
-            return a + jnp.maximum(x, floor), c + jnp.where(x > floor, 1.0, 0.0)
+        floor_b = floor.astype(BF16)
+
+        def add(slots, a, c):
+            x = dot(jnp.concatenate([picks(rk, slot) for slot in slots], 0), s)
+            for q in range(len(slots)):
+                part = x[128 * q:128 * q + 128]
+                a = a + jnp.maximum(part, floor)
+                c = c + jnp.where(part.astype(BF16) > floor_b, jnp.ones((), BF16), none)
+            return a, c
 
         a = jnp.zeros((128, 128), F32)
-        c = jnp.zeros((128, 128), F32)
-        for slot in range(first):
-            a, c = add(slot, a, c)
+        c = jnp.zeros((128, 128), BF16)
+        for slots in slot_batches(first, group):
+            a, c = add(slots, a, c)
         n = (jnp.maximum(most[t, 0] - first, 0) + more - 1) // more
 
         def rest(i, carry):
-            a, c = carry
-            for q in range(more):
-                a, c = add(first + i * more + q, a, c)
-            return a, c
+            return add([first + i * more + q for q in range(more)], *carry)
 
         a, c = lax.fori_loop(0, n, rest, (a, c))
-        degree = dot(jnp.where(rk >= jnp.zeros((), BF16), jnp.ones((), BF16), jnp.zeros((), BF16)), ones)
+        degree = dot(jnp.where(rk >= none, jnp.ones((), BF16), none), ones)
         spare = (first + n * more).astype(F32) - degree
         agg[rb] += a - degree * floor - spare * jnp.maximum(floor, 0.0)
-        cnt[rb] += c - spare * jnp.where(floor < 0.0, 1.0, 0.0)
+        cnt[rb] += c.astype(F32) - spare * jnp.where(floor < 0.0, 1.0, 0.0)
         return 0
 
     lax.fori_loop(0, tc[0], tile, 0)
@@ -186,10 +193,10 @@
         cnt_nb[1, sl] = cnt[8 + b].astype(BF16)
 
 
-def forward(ts, tr, tc, most, s_rows, r_rows, rank_r, first=18, more=4):
+def forward(ts, tr, tc, most, s_rows, r_rows, rank_r, first=18, more=4, group=3):
     own = 512
     return pl.pallas_call(
-        functools.partial(forward_kernel, first, more),
+        functools.partial(forward_kernel, first, more, group),
         out_shape=[sd((own, 128), F32), sd((2, own, 128), BF16), sd((own, 128), F32),
                    sd((2, own, 128), BF16)],
         in_specs=[SMEM] * 4 + [VM] * 3,
@@ -200,8 +207,8 @@
     )(ts, tr, tc, most, s_rows, r_rows, rank_r)
 
 
-def backward_kernel(first, more, ts, tr, tc, most, rank_t, s_rows, r_rows, dagg, lat_all, new_in,
-                    dsend, gsend, new_out, acc):
+def backward_kernel(first, more, group, ts, tr, tc, most, rank_t, s_rows, r_rows, dagg, lat_all,
+                    new_in, dsend, gsend, new_out, acc):
     new_out[...] = new_in[...]
     acc[...] = jnp.zeros_like(acc)
     tiles = rank_t.shape[0]
@@ -209,23 +216,24 @@
     def tile(t, _):
         sb = ts[t]
         rb = tr[t]
+        rk = rank_t[t].astype(BF16)
         floor = -(s_rows[sb].astype(F32))
         rhs = jnp.concatenate([r_rows[rb], dagg[rb]], axis=1)
-        rk = rank_t[t]
-
-        def add(slot, a):
-            x = dot(picks(rk, slot), rhs)
-            return a + jnp.where(x[:, :128] > floor, x[:, 128:], 0.0)
+
+        def add(slots, a):
+            x = dot(jnp.concatenate([picks(rk, slot) for slot in slots], 0), rhs)
+            for q in range(len(slots)):
+                part = x[128 * q:128 * q + 128]
+                a = a + jnp.where(part[:, :128] > floor, part[:, 128:], 0.0)
+            return a
 
         a = jnp.zeros((128, 128), F32)
-        for slot in range(first):
-            a = add(slot, a)
+        for slots in slot_batches(first, group):
+            a = add(slots, a)
         n = (jnp.maximum(most[t + tiles, 0] - first, 0) + more - 1) // more
 
         def rest(i, a):
-            for q in range(more):
-                a = add(first + i * more + q, a)
-            return a
+            return add([first + i * more + q for q in range(more)], a)
 
         acc[sb] += lax.fori_loop(0, n, rest, a)
         return 0
@@ -239,9 +247,9 @@
     gsend[...] = g
 
 
-def backward(ts, tr, tc, most, rank_t, s_rows, r_rows, dagg, lat_all, new_lat, first=18, more=4):
+def backward(ts, tr, tc, most, rank_t, s_rows, r_rows, dagg, lat_all, new_lat, first=18, more=4, group=6):
     return pl.pallas_call(
-        functools.partial(backward_kernel, first, more),
+        functools.partial(backward_kernel, first, more, group),
         out_shape=[sd((8, 512, 128), BF16), sd((128, 128), F32), sd((512, 128), BF16)],
         in_specs=[SMEM] * 4 + [VM] * 6,
         out_specs=[VM] * 3,
@@ -354,7 +362,7 @@
     own = lat.shape[0]
     n = GATHER_COPIES
     tiles = mask.shape[0]
-    ranks = sd((tiles, 128, 128), BF16)
+    ranks = sd((tiles, 128, 128), F32)
     return pl.pallas_call(
         gather_kernel,
         out_shape=[sd((8, own, 128), BF16), sd((8, own, 128), BF16), sd((3, own, 128), BF16),

time: 112 us -> 111 us (level)
  Pallas kernels: 111 us -> 109 us
    pallas_call x1, Pallas kernels: 47.1 us -> 44.7 us  [final(): pl.pallas_call(final_kernel, out_shape=[sd((own, 128), F32), sd((6, 128,...]
    pallas_call x1, Pallas kernels: 16.3 us -> 17.6 us  [node(): pl.pallas_call(node_kernel, out_shape=[sd((own, 128), BF16), sd((3, own,...]
where the time goes in v5:
time: 111 us
  Pallas kernels  109 us (98%)
  between operations  1.43 us (1%)
    pallas_call x1, Pallas kernels, final(): pl.pallas_call(final_kernel, out_shape=[sd((own, 128), F32), sd((6, 128,...  44.7 us
    pallas_call x1, Pallas kernels, gather(): pl.pallas_call(gather_kernel, out_shape=[sd((8, own, 128), BF16), sd((8,...  41 us
    pallas_call x1, Pallas kernels, node(): pl.pallas_call(node_kernel, out_shape=[sd((own, 128), BF16), sd((3, own,...  17.6 us
    pallas_call x1, Pallas kernels, backward(): pl.pallas_call(functools.partial(backward_kernel, first, more, group), ou...  2.98 us

profile of v5, /device:TPU:1, one launch (start us, length us, event | category | flops | bytes accessed | tf_op | source)
XLA Modules:
  0.0 110.8 jit_solution(13500641753325893399)
XLA Ops:
  1.3 41.0 %gather.1 = (bf16[8,512,128]{2,1,0:T(8,128)(2,1)S(1)}, bf16[8,512,128]{2,1,0:T(8,128)(2,1)S(1)}, bf16[3,512,128]{2,1,0:T(8,128)(2,1)S(1)}, f32[16,128,128]{2,1,0...) custom-call(bf16[512,128]{1,0:T(8,128)(2,1)} %lat.3, ...), custom_call_target="tpu_custom_call" | custom-call | tf_op jit(solution)/shard_map/gather/pallas_call | solution.py:366
  42.3 0.0 copy-start
  42.3 0.0 copy-start.1
  42.4 0.0 copy-start.2
  42.4 0.0 copy-start.4
  42.4 0.0 copy-start.5
  42.4 0.0 copy-start.6
  42.4 0.0 copy-start.7
  42.4 2.1 %forward.1 = (f32[512,128]{1,0:T(8,128)S(1)}, bf16[2,512,128]{2,1,0:T(8,128)(2,1)S(1)}, f32[512,128]{1,0:T(8,128)S(1)}, bf16[2,512,128]{2,1,0:T(8,128)(2,1)S(1)}) custom-call(s32[16]{0:T(128)S(1)} %get-tuple-element.27.ts, s32[16]{0:T(128)S(1)} %get-tuple-element.28.tr, s32[1]{0:T(128)} %get-tuple-element.29.tc, s32[32,128]{1,0:T(8,128)S(1)} %get-tuple-element.30.most, ...), custom_call_target="tpu_custom_call" | custom-call | tf_op jit(solution)/shard_map/forward/pallas_call | solution.py:198
  44.6 0.0 copy-done
  44.6 0.0 copy-done.1
  44.6 0.0 copy-done.2
  44.6 0.0 copy-done.4
  44.6 0.0 copy-done.5
  44.6 0.0 copy-done.6
  44.6 0.0 copy-done.7
  44.6 17.6 %node.1 = (bf16[512,128]{1,0:T(8,128)(2,1)S(1)}, bf16[3,512,128]{2,1,0:T(8,128)(2,1)S(1)}, f32[512,128]{1,0:T(8,128)S(1)}, f32[5,128,128]{2,1,0:T(8,128)S(1)}) custom-call(f32[512,128]{1,0:T(8,128)S(1)} %get-tuple-element.35.agg_own, bf16[2,512,128]{2,1,0:T(8,128)(2,1)S(1)} %get-tuple-element.36.agg_nb, f32[512,128]{1,0:T(8,128)S(1)} %get-tuple-element.37.cnt_own, ...), custom_call_target="tpu_custom_call" | custom-call | tf_op jit(solution)/shard_map/node/pallas_call | solution.py:470
  62.2 0.0 copy-start.3
  62.2 3.0 %backward.1 = (bf16[8,512,128]{2,1,0:T(8,128)(2,1)S(1)}, f32[128,128]{1,0:T(8,128)S(1)}, bf16[512,128]{1,0:T(8,128)(2,1)}) custom-call(s32[16]{0:T(128)S(1)} %get-tuple-element.27.ts, s32[16]{0:T(128)S(1)} %get-tuple-element.28.tr, s32[1]{0:T(128)} %get-tuple-element.29.tc, s32[32,128]{1,0:T(8,128)S(1)} %get-tuple-element.30.most, ...), custom_call_target="tpu_custom_call" | custom-call | tf_op jit(solution)/shard_map/backward/pallas_call | solution.py:251
  65.2 0.0 copy-done.3
  65.2 44.7 %final.1 = (f32[512,128]{1,0:T(8,128)S(1)}, f32[6,128,128]{2,1,0:T(8,128)S(1)}) custom-call(bf16[8,512,128]{2,1,0:T(8,128)(2,1)S(1)} %get-tuple-element.43.dsend, f32[128,128]{1,0:T(8,128)S(1)} %get-tuple-element.44.gsend, f32[5,128,128]{2,1,0:T(8,128)S(1)} %get-tuple-element.45.grads, f32[512,128]{1,0:T(8,128)S(1)} %get-tuple-element.46.part, ...), custom_call_target="tpu_custom_call" | custom-call | tf_op jit(solution)/shard_map/final/pallas_call | solution.py:603
  109.9 0.9 finish.1
Async XLA Ops:
  42.3 2.2 %copy-start = (bf16[512,128]{1,0:T(8,128)(2,1)S(1)}, bf16[512,128]{1,0:T(8,128)(2,1)}, u32[]{:S(2)}) copy-start(bf16[512,128]{1,0:T(8,128)(2,1)} %lat.3) | copy-start | bytes 393220
  42.3 2.2 %copy-start.1 = (bf16[512,128]{1,0:T(8,128)(2,1)S(1)}, bf16[512,128]{1,0:T(8,128)(2,1)}, u32[]{:S(2)}) copy-start(bf16[512,128]{1,0:T(8,128)(2,1)} %cot.1) | copy-start | bytes 393220
  42.4 2.2 %copy-start.2 = (bf16[128,128]{1,0:T(8,128)(2,1)S(1)}, bf16[128,128]{1,0:T(8,128)(2,1)}, u32[]{:S(2)}) copy-start(bf16[128,128]{1,0:T(8,128)(2,1)} %w_recv.1) | copy-start | bytes 98308
  42.4 2.2 %copy-start.4 = (bf16[128,128]{1,0:T(8,128)(2,1)S(1)}, bf16[128,128]{1,0:T(8,128)(2,1)}, u32[]{:S(2)}) copy-start(bf16[128,128]{1,0:T(8,128)(2,1)} %w_edge_out.1) | copy-start | bytes 98308
  42.4 2.2 %copy-start.5 = (bf16[128,128]{1,0:T(8,128)(2,1)S(1)}, bf16[128,128]{1,0:T(8,128)(2,1)}, u32[]{:S(2)}) copy-start(bf16[128,128]{1,0:T(8,128)(2,1)} %w_node_self.1) | copy-start | bytes 98308
  42.4 2.2 %copy-start.6 = (bf16[128,128]{1,0:T(8,128)(2,1)S(1)}, bf16[128,128]{1,0:T(8,128)(2,1)}, u32[]{:S(2)}) copy-start(bf16[128,128]{1,0:T(8,128)(2,1)} %w_node_msg.1) | copy-start | bytes 98308
  42.4 2.2 %copy-start.7 = (bf16[128,128]{1,0:T(8,128)(2,1)S(1)}, bf16[128,128]{1,0:T(8,128)(2,1)}, u32[]{:S(2)}) copy-start(bf16[128,128]{1,0:T(8,128)(2,1)} %w_node_out.1) | copy-start | bytes 98308
  62.2 3.0 %copy-start.3 = (bf16[128,128]{1,0:T(8,128)(2,1)S(1)}, bf16[128,128]{1,0:T(8,128)(2,1)}, u32[]{:S(2)}) copy-start(bf16[128,128]{1,0:T(8,128)(2,1)} %w_send.1) | copy-start | bytes 98308

commit v6 on v5

--- a/solution.py
+++ b/solution.py
@@ -145,7 +145,7 @@
 
 
 def forward_kernel(first, more, group, ts, tr, tc, most, s_rows, r_rows, rank_r, agg_own, agg_nb,
-                   cnt_own, cnt_nb, agg, cnt):
+                   cnt, agg):
     agg[...] = jnp.zeros_like(agg)
     cnt[...] = jnp.zeros_like(cnt)
     ones = jnp.ones((128, 128), BF16)
@@ -186,29 +186,25 @@
     for b in range(4):
         sl = pl.ds(b * 128, 128)
         agg_own[sl] = agg[4 + b]
-        cnt_own[sl] = cnt[4 + b]
         agg_nb[0, sl] = agg[b].astype(BF16)
         agg_nb[1, sl] = agg[8 + b].astype(BF16)
-        cnt_nb[0, sl] = cnt[b].astype(BF16)
-        cnt_nb[1, sl] = cnt[8 + b].astype(BF16)
 
 
 def forward(ts, tr, tc, most, s_rows, r_rows, rank_r, first=18, more=4, group=3):
     own = 512
     return pl.pallas_call(
         functools.partial(forward_kernel, first, more, group),
-        out_shape=[sd((own, 128), F32), sd((2, own, 128), BF16), sd((own, 128), F32),
-                   sd((2, own, 128), BF16)],
+        out_shape=[sd((own, 128), F32), sd((2, own, 128), BF16), sd((12, 128, 128), F32)],
         in_specs=[SMEM] * 4 + [VM] * 3,
-        out_specs=[VM] * 4,
-        scratch_shapes=[pltpu.VMEM((12, 128, 128), F32), pltpu.VMEM((12, 128, 128), F32)],
+        out_specs=[VM] * 3,
+        scratch_shapes=[pltpu.VMEM((12, 128, 128), F32)],
         compiler_params=pltpu.CompilerParams(vmem_limit_bytes=LIMIT),
         name="forward",
     )(ts, tr, tc, most, s_rows, r_rows, rank_r)
 
 
 def backward_kernel(first, more, group, ts, tr, tc, most, rank_t, s_rows, r_rows, dagg, lat_all,
-                    new_in, dsend, gsend, new_out, acc):
+                    new_in, cnt, lat, lat_nb, dsend, gsend, new_out, grecv, dr_nb, dr_own, acc):
     new_out[...] = new_in[...]
     acc[...] = jnp.zeros_like(acc)
     tiles = rank_t.shape[0]
@@ -245,26 +241,39 @@
         dsend[b] = d
         g = g + contract(lat_all[b], d)
     gsend[...] = g
-
-
-def backward(ts, tr, tc, most, rank_t, s_rows, r_rows, dagg, lat_all, new_lat, first=18, more=4, group=6):
+    g = jnp.zeros((128, 128), F32)
+    for slab in range(3):
+        block = pl.ds(4 * slab, 4)
+        d = (cnt[block] * dagg[block].astype(F32)).reshape(512, 128)
+        if slab == 1:
+            dr_own[...] = d
+            g = g + contract(lat[...], d.astype(BF16))
+        else:
+            dr_nb[slab // 2] = d.astype(BF16)
+            g = g + contract(lat_nb[slab // 2], d.astype(BF16))
+    grecv[...] = g
+
+
+def backward(ts, tr, tc, most, rank_t, s_rows, r_rows, dagg, lat_all, new_lat, cnt, lat, lat_nb,
+             first=18, more=4, group=6):
     return pl.pallas_call(
         functools.partial(backward_kernel, first, more, group),
-        out_shape=[sd((8, 512, 128), BF16), sd((128, 128), F32), sd((512, 128), BF16)],
-        in_specs=[SMEM] * 4 + [VM] * 6,
-        out_specs=[VM] * 3,
+        out_shape=[sd((8, 512, 128), BF16), sd((128, 128), F32), sd((512, 128), BF16),
+                   sd((128, 128), F32), sd((2, 512, 128), BF16), sd((512, 128), F32)],
+        in_specs=[SMEM] * 4 + [VM] * 9,
+        out_specs=[VM] * 6,
         scratch_shapes=[pltpu.VMEM((32, 128, 128), F32)],
         compiler_params=pltpu.CompilerParams(vmem_limit_bytes=LIMIT),
         name="backward",
-    )(ts, tr, tc, most, rank_t, s_rows, r_rows, dagg, lat_all, new_lat)
+    )(ts, tr, tc, most, rank_t, s_rows, r_rows, dagg, lat_all, new_lat, cnt, lat, lat_nb)
 
 
 GATHER_COPIES = 24
 
 
 def gather_kernel(lat, pos, w_send_in, w_recv_in, pw_in, bias_in, mask_in, ts_in, tr_in, tc_in,
-                  lat_all, s_rows, r_rows, rank_r, rank_t, most, ts, tr, tc, mask, top, pos_all,
-                  lat_nb, pos_nb, w_send, w_recv, pw, bias, load_sem, send_sem, recv_sem):
+                  lat_all, s_rows, r_rows, rank_r, rank_t, most, ts, tr, tc, lat_nb, mask, top,
+                  pos_all, pos_nb, w_send, w_recv, pw, bias, load_sem, send_sem, recv_sem):
     me = Place()
     own = lat.shape[0]
     g = me.grp
@@ -367,11 +376,11 @@
         gather_kernel,
         out_shape=[sd((8, own, 128), BF16), sd((8, own, 128), BF16), sd((3, own, 128), BF16),
                    ranks, ranks, sd((2 * tiles, 128), jnp.int32), sd((tiles,), jnp.int32),
-                   sd((tiles,), jnp.int32), sd((1,), jnp.int32)],
+                   sd((tiles,), jnp.int32), sd((1,), jnp.int32), sd((2, own, 128), BF16)],
         in_specs=[HBM] * 10,
-        out_specs=[VM] * 9,
+        out_specs=[VM] * 10,
         scratch_shapes=[pltpu.VMEM((tiles, 128, 128), jnp.int32), pltpu.VMEM((2 * tiles, 128), F32),
-                        pltpu.VMEM((8, 3, own), F32), pltpu.VMEM((2, own, 128), BF16),
+                        pltpu.VMEM((8, 3, own), F32),
                         pltpu.VMEM((2, 3, own), F32), pltpu.VMEM((128, 128), BF16),
                         pltpu.VMEM((128, 128), BF16), pltpu.VMEM((3, 128), F32),
                         pltpu.VMEM((1, 128), F32), pltpu.SemaphoreType.DMA((10,)),
@@ -383,12 +392,12 @@
 
 
 PIECES = 1
-NODE_COPIES = 4 * PIECES + 2
-
-
-def node_kernel(agg_own, agg_nb, cnt_own, cnt_nb, lat, cot, w_edge_out, w_node_self, w_node_msg,
-                node_bias_in, w_node_out, gain_in, w_recv, new_lat, dagg, part, grads, agg_in, cnt_in,
-                d_agg, direct, agg_b, message_b, hidden_b, d_update_b, d_pre_b, d_message_b,
+NODE_COPIES = 4 * PIECES
+
+
+def node_kernel(agg_own, agg_nb, lat, cot, w_edge_out, w_node_self, w_node_msg,
+                node_bias_in, w_node_out, gain_in, new_lat, dagg, part, grads, agg_in,
+                direct, agg_b, message_b, hidden_b, d_update_b, d_pre_b, d_message_b,
                 node_bias, gain, load_sem, send_sem, recv_sem):
     loads = fetch([(node_bias_in, node_bias), (gain_in, gain)], load_sem)
     me = Place()
@@ -401,7 +410,7 @@
     for p in pieces:
         arrive.append((cs.start(agg_nb.at[0, p], agg_in.at[0, p], prv),
                        cs.start(agg_nb.at[1, p], agg_in.at[1, p], nxt)))
-    counts, leave = [], []
+    leave = []
     for load in loads:
         load.wait()
     for i, p in enumerate(pieces):
@@ -412,9 +421,6 @@
         d_centre = d_normed - jnp.mean(d_normed, axis=-1, keepdims=True)
         for copy in arrive[i]:
             copy.wait_recv()
-        if i == PIECES - 1:
-            counts = [cs.start(cnt_nb.at[0], cnt_in.at[0], prv),
-                      cs.start(cnt_nb.at[1], cnt_in.at[1], nxt)]
         aggregate = agg_own[p] + agg_in[0, p].astype(F32) + agg_in[1, p].astype(F32)
         aggregate_b = aggregate.astype(BF16)
         message = dot(aggregate_b, w_edge_out[...]).astype(BF16)
@@ -437,7 +443,6 @@
         leave.append(cs.start(dagg.at[1, p], dagg.at[0, p], nxt))
         leave.append(cs.start(dagg.at[1, p], dagg.at[2, p], prv))
         new_lat[p] = (latent.astype(F32) + normed * gain[...]).astype(BF16)
-        d_agg[p] = d_aggregate
         agg_b[p] = aggregate_b
         message_b[p] = message
         hidden_b[p] = hidden
@@ -447,56 +452,50 @@
         direct[p] = c
     latent = lat[...]
     d_hidden_pre = d_pre_b[...]
-    grads[1] = contract(agg_b[...], d_message_b[...])
-    grads[2] = contract(latent, d_hidden_pre)
-    grads[3] = contract(message_b[...], d_hidden_pre)
-    grads[4] = contract(hidden_b[...], d_update_b[...])
-    base = direct[...] + dot_t(d_hidden_pre, w_node_self[...])
-    for copy in counts:
-        copy.wait_recv()
-    count = cnt_own[...] + cnt_in[0].astype(F32) + cnt_in[1].astype(F32)
-    d_recv = (count * d_agg[...]).astype(BF16)
-    grads[0] = contract(latent, d_recv)
-    part[...] = base + dot_t(d_recv, w_recv[...])
+    grads[0] = contract(agg_b[...], d_message_b[...])
+    grads[1] = contract(latent, d_hidden_pre)
+    grads[2] = contract(message_b[...], d_hidden_pre)
+    grads[3] = contract(hidden_b[...], d_update_b[...])
+    part[...] = direct[...] + dot_t(d_hidden_pre, w_node_self[...])
     for copy in leave:
         copy.wait_recv()
     cs.sent()
 
 
-def node(agg_own, agg_nb, cnt_own, cnt_nb, lat, cot, *weights):
+def node(agg_own, agg_nb, lat, cot, *weights):
     own = lat.shape[0]
     n = NODE_COPIES
     rows = pltpu.VMEM((own, 128), BF16)
     return pl.pallas_call(
         node_kernel,
         out_shape=[sd((own, 128), BF16), sd((3, own, 128), BF16), sd((own, 128), F32),
-                   sd((5, 128, 128), F32)],
-        in_specs=[VM] * 9 + [HBM, VM, HBM, VM],
+                   sd((4, 128, 128), F32)],
+        in_specs=[VM] * 7 + [HBM, VM, HBM],
         out_specs=[VM] * 4,
-        scratch_shapes=[pltpu.VMEM((2, own, 128), BF16), pltpu.VMEM((2, own, 128), BF16),
-                        pltpu.VMEM((own, 128), F32), pltpu.VMEM((own, 128), F32),
+        scratch_shapes=[pltpu.VMEM((2, own, 128), BF16), pltpu.VMEM((own, 128), F32),
                         rows, rows, rows, rows, rows, rows, pltpu.VMEM((1, 128), F32),
                         pltpu.VMEM((1, 128), F32), pltpu.SemaphoreType.DMA((2,)),
                         pltpu.SemaphoreType.DMA((n,)), pltpu.SemaphoreType.DMA((n,))],
         compiler_params=pltpu.CompilerParams(collective_id=1, has_side_effects=True,
                                              vmem_limit_bytes=LIMIT),
         name="node",
-    )(agg_own, agg_nb, cnt_own, cnt_nb, lat, cot, *weights)
-
-
-FINAL_COPIES = 49
-
-
-def final_kernel(dsend, gsend, grads, part, w_send, latent_grad, weight_grads, v, in_xc, vy, in_y,
-                 vz, in_z, out_y, out, rs_core, cs_sum, in_ra, in_rb, in_da, in_db, in_fa, in_fb,
+    )(agg_own, agg_nb, lat, cot, *weights)
+
+
+FINAL_COPIES = 51
+
+
+def final_kernel(dsend, gsend, grecv, grads, part, w_send, w_recv, dr_nb, dr_own, latent_grad, weight_grads, v, in_xc, vy, in_y,
+                 vz, in_z, out_y, out, in_dr, rs_core, cs_sum, in_ra, in_rb, in_da, in_db, in_fa, in_fb,
                  fwd_a, fwd_b, ready_y, ready_z, send_sem, recv_sem):
     me = Place()
     own = part.shape[0]
     up, dn, sib = me.member(1), me.member(-1), me.partner()
     core, zh = me.core, me.zh
     v[pl.ds(0, 128)] = gsend[...].astype(BF16)
-    for i in range(5):
-        v[pl.ds(128 * (i + 1), 128)] = grads[i].astype(BF16)
+    v[pl.ds(128, 128)] = grecv[...].astype(BF16)
+    for i in range(4):
+        v[pl.ds(128 * (i + 2), 128)] = grads[i].astype(BF16)
     vy[...] = jnp.zeros_like(vy)
 
     def chunk(c, x):
@@ -511,7 +510,8 @@
     plane = [(dx, dc) for dx in range(NX) for dc in range(2) if dx or dc]
     spots = [((core + dc) % 2, (me.x + dx) % NX) for dx, dc in plane]
     peers = [me.at(x=x, core=c) for c, x in spots]
-    meet(peers + [y_peer(d) for d in (1, 2, -1, -2)] + [z_peer(d) for d in (1, 2, 3, -1, -2, -3)])
+    nxt, prv = me.slab(1), me.slab(-1)
+    meet(peers + [nxt, prv] + [y_peer(d) for d in (1, 2, -1, -2)] + [z_peer(d) for d in (1, 2, 3, -1, -2, -3)])
     for d in (2, -2):
         pl.semaphore_signal(ready_y, inc=1, device_id=y_peer(d), device_id_type=MESH)
     for d in (3, -3):
@@ -547,6 +547,7 @@
         vy[q, pl.ds(0, 12)] = total[12 * q:12 * q + 12].astype(BF16)
     pl.semaphore_wait(ready_y, 2)
     ar_y = [cs.start(vy.at[(me.y + d) % NY], in_y.at[d - 1], y_peer(d)) for d in range(1, NY)]
+    beside = [cs.start(dr_nb.at[0], in_dr.at[0], prv), cs.start(dr_nb.at[1], in_dr.at[1], nxt)]
     chip_sum(3)
 
     for copy in ar_y:
@@ -579,14 +580,18 @@
     mine = chunk(core, me.x)
     out[mine] = jnp.concatenate([out_y[q].astype(F32)[:12] for q in range(NY)], 0).astype(BF16)
     ag_xc = [cs.start(out.at[mine], out.at[mine], peer) for peer in peers]
+    for copy in beside:
+        copy.wait_recv()
+    d_recv = (dr_own[...] + in_dr[0].astype(F32) + in_dr[1].astype(F32)).astype(BF16)
+    latent_grad[...] = part[...] + dot_t(d_recv, w_recv[...])
     da.wait_recv()
     db.wait_recv()
     fa.wait_recv()
     d_a = cs_sum[zh, ha].astype(F32) + in_da[...].astype(F32) + in_fa[...].astype(F32)
-    latent_grad[ha] = part[ha] + dot_t(d_a.astype(BF16), w_send[...])
+    latent_grad[ha] = latent_grad[ha] + dot_t(d_a.astype(BF16), w_send[...])
     fb.wait_recv()
     d_b = cs_sum[zh, hb].astype(F32) + in_db[...].astype(F32) + in_fb[...].astype(F32)
-    latent_grad[hb] = part[hb] + dot_t(d_b.astype(BF16), w_send[...])
+    latent_grad[hb] = latent_grad[hb] + dot_t(d_b.astype(BF16), w_send[...])
 
     for copy in ag_xc:
         copy.wait_recv()
@@ -595,7 +600,7 @@
     cs.sent()
 
 
-def final(dsend, gsend, grads, part, w_send):
+def final(dsend, gsend, grecv, grads, part, w_send, w_recv, dr_nb, dr_own):
     own = part.shape[0]
     n = FINAL_COPIES
     b = lambda *shape: pltpu.VMEM(shape, BF16)
@@ -603,18 +608,18 @@
     return pl.pallas_call(
         final_kernel,
         out_shape=[sd((own, 128), F32), sd((6, 128, 128), F32)],
-        in_specs=[VM] * 5,
+        in_specs=[VM] * 9,
         out_specs=[VM] * 2,
         scratch_shapes=[
             b(768, 128), b(2 * NX - 1, 96, 128), b(NY, 16, 128), b(NY - 1, 16, 128), b(16, 128),
-            b(NZ, 16, 128), b(NY, 16, 128), b(768, 128), b(ZHI, own, 128), b(ZHI, own, 128),
+            b(NZ, 16, 128), b(NY, 16, 128), b(768, 128), b(2, own, 128), b(ZHI, own, 128), b(ZHI, own, 128),
             b(h, 128), b(h, 128), b(h, 128), b(h, 128), b(h, 128), b(h, 128), b(h, 128), b(h, 128),
             pltpu.SemaphoreType.REGULAR, pltpu.SemaphoreType.REGULAR,
             pltpu.SemaphoreType.DMA((n,)), pltpu.SemaphoreType.DMA((n,))],
         compiler_params=pltpu.CompilerParams(collective_id=2, has_side_effects=True,
                                              vmem_limit_bytes=LIMIT),
         name="final",
-    )(dsend, gsend, grads, part, w_send)
+    )(dsend, gsend, grecv, grads, part, w_send, w_recv, dr_nb, dr_own)
 
 
 def finish_kernel(a, b, a_out, b_out, sem):
@@ -637,17 +642,19 @@
 def body(latent, positions, tile_send, tile_recv, tile_mask, tile_count, w_send, w_recv, pos_weight,
          edge_bias, w_edge_out, w_node_self, w_node_msg, node_bias, w_node_out, gain, cotangent):
     ts, tr, tc = tile_send[0, 0], tile_recv[0, 0], tile_count[0]
-    lat_all, s_rows, r_rows, rank_r, rank_t, most, ts, tr, tc = gather(
+    lat_all, s_rows, r_rows, rank_r, rank_t, most, ts, tr, tc, lat_nb = gather(
         latent, positions, w_send, w_recv, pos_weight, edge_bias[None], tile_mask[0, 0], ts, tr, tc)
     s_rows = s_rows.reshape(32, 128, 128)
     r_rows = r_rows.reshape(12, 128, 128)
-    agg_own, agg_nb, cnt_own, cnt_nb = forward(ts, tr, tc, most, s_rows, r_rows, rank_r)
+    agg_own, agg_nb, cnt = forward(ts, tr, tc, most, s_rows, r_rows, rank_r)
     new_latent, dagg, part, grads = node(
-        agg_own, agg_nb, cnt_own, cnt_nb, latent, cotangent, w_edge_out, w_node_self, w_node_msg,
-        *in_hbm(node_bias[None]), w_node_out, *in_hbm(gain[None]), w_recv)
-    dsend, gsend, new_latent = backward(ts, tr, tc, most, rank_t, s_rows, r_rows, dagg.reshape(12, 128, 128),
-                            lat_all, new_latent)
-    latent_grad, weight_grads = finish(*final(dsend, gsend, grads, part, w_send))
+        agg_own, agg_nb, latent, cotangent, w_edge_out, w_node_self, w_node_msg,
+        *in_hbm(node_bias[None]), w_node_out, *in_hbm(gain[None]))
+    dsend, gsend, new_latent, grecv, dr_nb, dr_own = backward(
+        ts, tr, tc, most, rank_t, s_rows, r_rows, dagg.reshape(12, 128, 128), lat_all, new_latent,
+        cnt, latent, lat_nb)
+    latent_grad, weight_grads = finish(*final(dsend, gsend, grecv, grads, part, w_send, w_recv,
+                                              dr_nb, dr_own))
     return new_latent, latent_grad, weight_grads
 
 

time: 111 us -> 112 us (level)
  no operation moved by 1% of the time
where the time goes in v6:
time: 112 us; the launch traced here: 111 us
  Pallas kernels  110 us (98%)
  between operations  1.42 us (1%)
    pallas_call x1, Pallas kernels, final(): pl.pallas_call(final_kernel, out_shape=[sd((own, 128), F32), sd((6, 128,...  44.3 us
    pallas_call x1, Pallas kernels, gather(): pl.pallas_call(gather_kernel, out_shape=[sd((8, own, 128), BF16), sd((8,...  41 us
    pallas_call x1, Pallas kernels, node(): pl.pallas_call(node_kernel, out_shape=[sd((own, 128), BF16), sd((3, own,...  18.2 us
    pallas_call x1, Pallas kernels, backward(): pl.pallas_call(functools.partial(backward_kernel, first, more, group), ou...  3.21 us

profile of v6, /device:TPU:1, one launch (start us, length us, event | category | flops | bytes accessed | tf_op | source)
XLA Modules:
  0.0 111.3 jit_solution(5769034367677926307)
XLA Ops:
  1.3 41.0 %gather.1 = (bf16[8,512,128]{2,1,0:T(8,128)(2,1)S(1)}, bf16[8,512,128]{2,1,0:T(8,128)(2,1)S(1)}, bf16[3,512,128]{2,1,0:T(8,128)(2,1)S(1)}, f32[16,128,128]{2,1,0...) custom-call(bf16[512,128]{1,0:T(8,128)(2,1)} %lat.5, ...), custom_call_target="tpu_custom_call" | custom-call | tf_op jit(solution)/shard_map/gather/pallas_call | solution.py:375
  42.3 0.0 copy-start
  42.3 0.0 copy-start.3
  42.4 0.0 copy-start.4
  42.4 0.0 copy-start.5
  42.4 0.0 copy-start.6
  42.4 0.0 copy-start.7
  42.4 2.1 %forward.1 = (f32[512,128]{1,0:T(8,128)S(1)}, bf16[2,512,128]{2,1,0:T(8,128)(2,1)S(1)}, f32[12,128,128]{2,1,0:T(8,128)S(1)}) custom-call(s32[16]{0:T(128)S(1)} %get-tuple-element.30.ts, s32[16]{0:T(128)S(1)} %get-tuple-element.31.tr, s32[1]{0:T(128)} %get-tuple-element.32.tc, s32[32,128]{1,0:T(8,128)S(1)} %get-tuple-element.33.most, ...), custom_call_target="tpu_custom_call" | custom-call | tf_op jit(solution)/shard_map/forward/pallas_call | solution.py:195
  44.5 0.0 copy-done
  44.5 0.0 copy-done.3
  44.5 0.0 copy-done.4
  44.5 0.0 copy-done.5
  44.6 0.0 copy-done.6
  44.6 0.0 copy-done.7
  44.6 18.2 %node.1 = (bf16[512,128]{1,0:T(8,128)(2,1)S(1)}, bf16[3,512,128]{2,1,0:T(8,128)(2,1)S(1)}, f32[512,128]{1,0:T(8,128)S(1)}, f32[4,128,128]{2,1,0:T(8,128)S(1)}) custom-call(f32[512,128]{1,0:T(8,128)S(1)} %get-tuple-element.38.agg_own, bf16[2,512,128]{2,1,0:T(8,128)(2,1)S(1)} %get-tuple-element.39.agg_nb, bf16[512,128]{1,0:T(8,128)(2,1)S(1)} %copy-done, ...), custom_call_target="tpu_custom_call" | custom-call | tf_op jit(solution)/shard_map/node/pallas_call | solution.py:469
  62.8 0.0 copy-start.1
  62.8 0.0 copy-start.2
  62.9 3.2 %backward.1 = (bf16[8,512,128]{2,1,0:T(8,128)(2,1)S(1)}, f32[128,128]{1,0:T(8,128)S(1)}, bf16[512,128]{1,0:T(8,128)(2,1)}, f32[128,128]{1,0:T(8,128)S(1)}, bf16[...) custom-call(s32[16]{0:T(128)S(1)} %get-tuple-element.30.ts, s32[16]{0:T(128)S(1)} %get-tuple-element.31.tr, ...), custom_call_target="tpu_custom_call" | custom-call | tf_op jit(solution)/shard_map/backward/pallas_call | solution.py:259
  66.1 0.0 copy-done.1
  66.1 0.0 copy-done.2
  66.1 44.3 %final.1 = (f32[512,128]{1,0:T(8,128)S(1)}, f32[6,128,128]{2,1,0:T(8,128)S(1)}) custom-call(bf16[8,512,128]{2,1,0:T(8,128)(2,1)S(1)} %get-tuple-element.46.dsend, f32[128,128]{1,0:T(8,128)S(1)} %get-tuple-element.47.gsend, f32[128,128]{1,0:T(8,128)S(1)} %get-tuple-element.48.grecv, f32[4,128,128]{2,1,0:T(8,128)S(1)} %get-tuple-element.49.grads, ...), custom_call_target="tpu_custom_call" | custom-call | tf_op jit(solution)/shard_map/final/pallas_call | solution.py:608
  110.4 0.9 finish.1
Async XLA Ops:
  42.3 2.2 %copy-start = (bf16[512,128]{1,0:T(8,128)(2,1)S(1)}, bf16[512,128]{1,0:T(8,128)(2,1)}, u32[]{:S(2)}) copy-start(bf16[512,128]{1,0:T(8,128)(2,1)} %lat.5) | copy-start | bytes 393220
  42.3 2.2 %copy-start.3 = (bf16[512,128]{1,0:T(8,128)(2,1)S(1)}, bf16[512,128]{1,0:T(8,128)(2,1)}, u32[]{:S(2)}) copy-start(bf16[512,128]{1,0:T(8,128)(2,1)} %cot.1) | copy-start | bytes 393220
  42.4 2.2 %copy-start.4 = (bf16[128,128]{1,0:T(8,128)(2,1)S(1)}, bf16[128,128]{1,0:T(8,128)(2,1)}, u32[]{:S(2)}) copy-start(bf16[128,128]{1,0:T(8,128)(2,1)} %w_edge_out.1) | copy-start | bytes 98308
  42.4 2.2 %copy-start.5 = (bf16[128,128]{1,0:T(8,128)(2,1)S(1)}, bf16[128,128]{1,0:T(8,128)(2,1)}, u32[]{:S(2)}) copy-start(bf16[128,128]{1,0:T(8,128)(2,1)} %w_node_self.1) | copy-start | bytes 98308
  42.4 2.2 %copy-start.6 = (bf16[128,128]{1,0:T(8,128)(2,1)S(1)}, bf16[128,128]{1,0:T(8,128)(2,1)}, u32[]{:S(2)}) copy-start(bf16[128,128]{1,0:T(8,128)(2,1)} %w_node_msg.1) | copy-start | bytes 98308
  42.4 2.2 %copy-start.7 = (bf16[128,128]{1,0:T(8,128)(2,1)S(1)}, bf16[128,128]{1,0:T(8,128)(2,1)}, u32[]{:S(2)}) copy-start(bf16[128,128]{1,0:T(8,128)(2,1)} %w_node_out.1) | copy-start | bytes 98308
  62.8 3.2 %copy-start.1 = (bf16[128,128]{1,0:T(8,128)(2,1)S(1)}, bf16[128,128]{1,0:T(8,128)(2,1)}, u32[]{:S(2)}) copy-start(bf16[128,128]{1,0:T(8,128)(2,1)} %w_send.1) | copy-start | bytes 98308
  62.8 3.2 %copy-start.2 = (bf16[128,128]{1,0:T(8,128)(2,1)S(1)}, bf16[128,128]{1,0:T(8,128)(2,1)}, u32[]{:S(2)}) copy-start(bf16[128,128]{1,0:T(8,128)(2,1)} %w_recv.1) | copy-start | bytes 98308

commit v7 on v6

--- a/solution.py
+++ b/solution.py
@@ -273,7 +273,7 @@
 
 def gather_kernel(lat, pos, w_send_in, w_recv_in, pw_in, bias_in, mask_in, ts_in, tr_in, tc_in,
                   lat_all, s_rows, r_rows, rank_r, rank_t, most, ts, tr, tc, lat_nb, mask, top,
-                  pos_all, pos_nb, w_send, w_recv, pw, bias, load_sem, send_sem, recv_sem):
+                  pos_all, pos_nb, w_send, w_recv, pw, bias, placed, load_sem, send_sem, recv_sem):
     me = Place()
     own = lat.shape[0]
     g = me.grp
@@ -310,9 +310,11 @@
     def pass_on(ref):
         return cs.start(ref, ref, sib)
 
+    def place(index):
+        placed[index] = placed_of(pos_all[index], pw[...])
+
     def send_rows(index):
-        s_rows[index] = (dot(lat_all[index], w_send[...])
-                         + placed_of(pos_all[index], pw[...])).astype(BF16)
+        s_rows[index] = (dot(lat_all[index], w_send[...]) + placed[index]).astype(BF16)
 
     def recv_rows(slab, rows, places):
         r_rows[slab] = (dot(rows, w_recv[...]) - placed_of(places, pw[...])
@@ -324,6 +326,7 @@
     for load in loads:
         load.wait()
     recv_rows(1, lat_all[g], pos_all[g])
+    place(g)
     send_rows(g)
     rank_tiles(mask, rank_r, rank_t, top)
     most[...] = slot_counts(top)
@@ -339,10 +342,13 @@
     dn_b.wait_recv()
     far_b = cs.start(half(iu, 1), half(iu, 1), dn)
     near.append(pass_on(half(iu, 1)))
+    place(idn)
+    place(iu)
     for copy in beside + partner:
         copy.wait_recv()
     recv_rows(0, lat_nb[0], pos_nb[0])
     recv_rows(2, lat_nb[1], pos_nb[1])
+    place(sib[1])
     send_rows(sib[1])
     up_b.wait_recv()
     near.append(pass_on(half(idn, 1)))
@@ -352,16 +358,20 @@
     send_rows(iu)
     far_pos.wait_recv()
     last = [pass_on(pos_all.at[far])]
+    place(far)
     for copy in near:
         copy.wait_recv()
-    send_rows(other(idn))
-    send_rows(other(iu))
+    for index in (other(idn), other(iu)):
+        place(index)
+        send_rows(index)
+    last[0].wait_recv()
+    place(other(far))
     far_a.wait_recv()
     last.append(pass_on(half(far, 0)))
     far_b.wait_recv()
     last.append(pass_on(half(far, 1)))
     send_rows(far)
-    for copy in last:
+    for copy in last[1:]:
         copy.wait_recv()
     send_rows(other(far))
     cs.sent()
@@ -383,7 +393,8 @@
                         pltpu.VMEM((8, 3, own), F32),
                         pltpu.VMEM((2, 3, own), F32), pltpu.VMEM((128, 128), BF16),
                         pltpu.VMEM((128, 128), BF16), pltpu.VMEM((3, 128), F32),
-                        pltpu.VMEM((1, 128), F32), pltpu.SemaphoreType.DMA((10,)),
+                        pltpu.VMEM((1, 128), F32), pltpu.VMEM((8, own, 128), F32),
+                        pltpu.SemaphoreType.DMA((10,)),
                         pltpu.SemaphoreType.DMA((n,)), pltpu.SemaphoreType.DMA((n,))],
         compiler_params=pltpu.CompilerParams(collective_id=0, has_side_effects=True,
                                              vmem_limit_bytes=LIMIT),
@@ -547,7 +558,6 @@
         vy[q, pl.ds(0, 12)] = total[12 * q:12 * q + 12].astype(BF16)
     pl.semaphore_wait(ready_y, 2)
     ar_y = [cs.start(vy.at[(me.y + d) % NY], in_y.at[d - 1], y_peer(d)) for d in range(1, NY)]
-    beside = [cs.start(dr_nb.at[0], in_dr.at[0], prv), cs.start(dr_nb.at[1], in_dr.at[1], nxt)]
     chip_sum(3)
 
     for copy in ar_y:
@@ -559,6 +569,7 @@
     in_z[me.z] = total.astype(BF16)
     pl.semaphore_wait(ready_z, 2)
     ar_z = [cs.start(vz, in_z.at[me.z], z_peer(d)) for d in range(1, NZ)]
+    beside = [cs.start(dr_nb.at[0], in_dr.at[0], prv), cs.start(dr_nb.at[1], in_dr.at[1], nxt)]
 
     for copy in ar_z:
         copy.wait_recv()

time: 112 us -> 110 us (0.982)
  Pallas kernels: 110 us -> 108 us
    pallas_call x1, Pallas kernels: 44.3 us -> 42.3 us  [final(): pl.pallas_call(final_kernel, out_shape=[sd((own, 128), F32), sd((6, 128,...]
where the time goes in v7:
time: 110 us
  Pallas kernels  108 us (98%)
  between operations  1.42 us (1%)
    pallas_call x1, Pallas kernels, final(): pl.pallas_call(final_kernel, out_shape=[sd((own, 128), F32), sd((6, 128,...  42.3 us
    pallas_call x1, Pallas kernels, gather(): pl.pallas_call(gather_kernel, out_shape=[sd((8, own, 128), BF16), sd((8,...  40.6 us
    pallas_call x1, Pallas kernels, node(): pl.pallas_call(node_kernel, out_shape=[sd((own, 128), BF16), sd((3, own,...  19 us
    pallas_call x1, Pallas kernels, backward(): pl.pallas_call(functools.partial(backward_kernel, first, more, group), ou...  3.22 us

profile of v7, /device:TPU:1, one launch (start us, length us, event | category | flops | bytes accessed | tf_op | source)
XLA Modules:
  0.0 109.5 jit_solution(13671023854650587188)
XLA Ops:
  1.3 40.6 %gather.1 = (bf16[8,512,128]{2,1,0:T(8,128)(2,1)S(1)}, bf16[8,512,128]{2,1,0:T(8,128)(2,1)S(1)}, bf16[3,512,128]{2,1,0:T(8,128)(2,1)S(1)}, f32[16,128,128]{2,1,0...) custom-call(bf16[512,128]{1,0:T(8,128)(2,1)} %lat.5, ...), custom_call_target="tpu_custom_call" | custom-call | tf_op jit(solution)/shard_map/gather/pallas_call | solution.py:385
  41.9 0.0 copy-start
  41.9 0.0 copy-start.3
  41.9 0.0 copy-start.4
  41.9 0.0 copy-start.5
  41.9 0.0 copy-start.6
  42.0 0.0 copy-start.7
  42.0 2.1 %forward.1 = (f32[512,128]{1,0:T(8,128)S(1)}, bf16[2,512,128]{2,1,0:T(8,128)(2,1)S(1)}, f32[12,128,128]{2,1,0:T(8,128)S(1)}) custom-call(s32[16]{0:T(128)S(1)} %get-tuple-element.30.ts, s32[16]{0:T(128)S(1)} %get-tuple-element.31.tr, s32[1]{0:T(128)} %get-tuple-element.32.tc, s32[32,128]{1,0:T(8,128)S(1)} %get-tuple-element.33.most, ...), custom_call_target="tpu_custom_call" | custom-call | tf_op jit(solution)/shard_map/forward/pallas_call | solution.py:195
  44.1 0.0 copy-done
  44.1 0.0 copy-done.3
  44.1 0.0 copy-done.4
  44.1 0.0 copy-done.5
  44.1 0.0 copy-done.6
  44.1 0.0 copy-done.7
  44.1 19.0 %node.1 = (bf16[512,128]{1,0:T(8,128)(2,1)S(1)}, bf16[3,512,128]{2,1,0:T(8,128)(2,1)S(1)}, f32[512,128]{1,0:T(8,128)S(1)}, f32[4,128,128]{2,1,0:T(8,128)S(1)}) custom-call(f32[512,128]{1,0:T(8,128)S(1)} %get-tuple-element.38.agg_own, bf16[2,512,128]{2,1,0:T(8,128)(2,1)S(1)} %get-tuple-element.39.agg_nb, bf16[512,128]{1,0:T(8,128)(2,1)S(1)} %copy-done, ...), custom_call_target="tpu_custom_call" | custom-call | tf_op jit(solution)/shard_map/node/pallas_call | solution.py:480
  63.1 0.0 copy-start.1
  63.1 0.0 copy-start.2
  63.1 3.2 %backward.1 = (bf16[8,512,128]{2,1,0:T(8,128)(2,1)S(1)}, f32[128,128]{1,0:T(8,128)S(1)}, bf16[512,128]{1,0:T(8,128)(2,1)}, f32[128,128]{1,0:T(8,128)S(1)}, bf16[...) custom-call(s32[16]{0:T(128)S(1)} %get-tuple-element.30.ts, s32[16]{0:T(128)S(1)} %get-tuple-element.31.tr, ...), custom_call_target="tpu_custom_call" | custom-call | tf_op jit(solution)/shard_map/backward/pallas_call | solution.py:259
  66.4 0.0 copy-done.1
  66.4 0.0 copy-done.2
  66.4 42.3 %final.1 = (f32[512,128]{1,0:T(8,128)S(1)}, f32[6,128,128]{2,1,0:T(8,128)S(1)}) custom-call(bf16[8,512,128]{2,1,0:T(8,128)(2,1)S(1)} %get-tuple-element.46.dsend, f32[128,128]{1,0:T(8,128)S(1)} %get-tuple-element.47.gsend, f32[128,128]{1,0:T(8,128)S(1)} %get-tuple-element.48.grecv, f32[4,128,128]{2,1,0:T(8,128)S(1)} %get-tuple-element.49.grads, ...), custom_call_target="tpu_custom_call" | custom-call | tf_op jit(solution)/shard_map/final/pallas_call | solution.py:619
  108.7 0.9 finish.1
Async XLA Ops:
  41.9 2.2 %copy-start = (bf16[512,128]{1,0:T(8,128)(2,1)S(1)}, bf16[512,128]{1,0:T(8,128)(2,1)}, u32[]{:S(2)}) copy-start(bf16[512,128]{1,0:T(8,128)(2,1)} %lat.5) | copy-start | bytes 393220
  41.9 2.2 %copy-start.3 = (bf16[512,128]{1,0:T(8,128)(2,1)S(1)}, bf16[512,128]{1,0:T(8,128)(2,1)}, u32[]{:S(2)}) copy-start(bf16[512,128]{1,0:T(8,128)(2,1)} %cot.1) | copy-start | bytes 393220
  41.9 2.2 %copy-start.4 = (bf16[128,128]{1,0:T(8,128)(2,1)S(1)}, bf16[128,128]{1,0:T(8,128)(2,1)}, u32[]{:S(2)}) copy-start(bf16[128,128]{1,0:T(8,128)(2,1)} %w_edge_out.1) | copy-start | bytes 98308
  41.9 2.2 %copy-start.5 = (bf16[128,128]{1,0:T(8,128)(2,1)S(1)}, bf16[128,128]{1,0:T(8,128)(2,1)}, u32[]{:S(2)}) copy-start(bf16[128,128]{1,0:T(8,128)(2,1)} %w_node_self.1) | copy-start | bytes 98308
  41.9 2.2 %copy-start.6 = (bf16[128,128]{1,0:T(8,128)(2,1)S(1)}, bf16[128,128]{1,0:T(8,128)(2,1)}, u32[]{:S(2)}) copy-start(bf16[128,128]{1,0:T(8,128)(2,1)} %w_node_msg.1) | copy-start | bytes 98308
  42.0 2.2 %copy-start.7 = (bf16[128,128]{1,0:T(8,128)(2,1)S(1)}, bf16[128,128]{1,0:T(8,128)(2,1)}, u32[]{:S(2)}) copy-start(bf16[128,128]{1,0:T(8,128)(2,1)} %w_node_out.1) | copy-start | bytes 98308
  63.1 3.2 %copy-start.1 = (bf16[128,128]{1,0:T(8,128)(2,1)S(1)}, bf16[128,128]{1,0:T(8,128)(2,1)}, u32[]{:S(2)}) copy-start(bf16[128,128]{1,0:T(8,128)(2,1)} %w_send.1) | copy-start | bytes 98308
  63.1 3.2 %copy-start.2 = (bf16[128,128]{1,0:T(8,128)(2,1)S(1)}, bf16[128,128]{1,0:T(8,128)(2,1)}, u32[]{:S(2)}) copy-start(bf16[128,128]{1,0:T(8,128)(2,1)} %w_recv.1) | copy-start | bytes 98308
